TPU v7x, 32 devices: a whole 2x2x4 slice. The times are simulated.
32 devices in a mesh: probe: 16 (over z, x, core), depth: 2 (over y).
Axes of the slice: x: 2, y: 2, z: 4, core: 2. Of those that a mesh axis runs over, the one named last changes fastest.
Arguments:
- potential: float32 [4, 2048, 1024], P('depth', 'probe'), may hold values from -6 to 6
- probe: float32 [2, 256, 256], replicated, may hold values from -6 to 6
- positions: int32 [16, 2], P('probe'), may hold values from 0 to 2047, as said below
- intensity: float32 [16, 256, 256], P('probe'), may hold values from 0 to 4
Outputs:
- potential_grad: float32 [4, 2048, 1024], P('depth', 'probe')
Inputs may be any that keep to these rules, and one draw needn't show every extreme that they name: `positions`: entry 0 of probe p is the top row of its window and entry 1 its left column, 0 to 768. The window's centre row, (entry 128) mod 2048, lies in rows g * 128 to g * 128 + 127, where g = p // 1 is the probe's group.
All inputs are finite; a program needn't handle non-finite values.
Results may differ from a plain program's by a relative error of at most 0.0003.
Values sent between devices are 32-bit elements; how exact they have to be, the bound alone decides.
No kernel may reach another device: no remote copies, remote signals or barrier semaphores. Data moves between devices by JAX's collectives and lax.ppermute only.
A program may use at most 64 MiB of HBM per device.

v0:
```python
import functools

import jax
import jax.numpy as jnp
import numpy as np
from jax import lax
from jax.experimental import pallas as pl
from jax.experimental.pallas import tpu as pltpu
from jax.sharding import PartitionSpec as P

interaction = 0.5
fresnel_phase = 60.0
f32 = jnp.float32
bf16 = jnp.bfloat16

VMEM = pl.BlockSpec(memory_space=pltpu.VMEM)
SMEM = pl.BlockSpec(memory_space=pltpu.SMEM)


def poly_tables():
    x = np.cos(np.linspace(0.0, np.pi / 2, 4001)) * (np.pi / 2) * 1.0005
    z = x * x
    fit = np.polynomial.chebyshev.Chebyshev.fit
    kind = np.polynomial.Polynomial
    sine = fit(z, np.sinc(x / np.pi), 5).convert(kind=kind).coef
    cosine = fit(z, np.cos(x), 5).convert(kind=kind).coef
    return [float(v) for v in sine], [float(v) for v in cosine]


def split_table(matrix):
    parts = []
    for real in (matrix.real, matrix.imag, -matrix.imag):
        wide = real.astype(np.float32)
        high = wide.astype(bf16)
        parts.append(high)
        parts.append((real - high.astype(np.float64)).astype(np.float32).astype(bf16))
    return np.stack(parts)


def tables(extent):
    index = np.arange(extent)
    dft = np.exp(-2j * np.pi * ((index[:, None] * index[None, :]) % extent) / extent)
    dft = dft / np.sqrt(extent)
    frequency = ((index + extent // 2) % extent - extent // 2) / extent
    chirp = np.exp(-1j * fresnel_phase * frequency**2)
    propagator = np.conj(dft) @ (chirp[:, None] * dft)
    return split_table(propagator), split_table(dft)


def sin_cos(window):
    sine, cosine = poly_tables()
    half = window * (interaction / 2)
    turns = jnp.round(half * (1.0 / np.pi))
    pi_high = float(np.float32(3.140625))
    pi_low = float(np.pi - 3.140625)
    x = (half - turns * pi_high) - turns * pi_low
    z = x * x
    s = sine[5]
    c = cosine[5]
    for k in range(4, -1, -1):
        s = s * z + sine[k]
        c = c * z + cosine[k]
    s = s * x
    return 2.0 * s * c, 1.0 - 2.0 * (s * s)


def columns_of(ref, layer, column):
    extent = 2 * ref.shape[1]
    block = column // extent
    last = ref.shape[2] // extent - 1
    low = ref[layer, :, pl.ds(pl.multiple_of(block * extent, extent), extent)]
    after = jnp.minimum(block + 1, last)
    high = ref[layer, :, pl.ds(pl.multiple_of(after * extent, extent), extent)]
    lane = lax.broadcasted_iota(jnp.int32, low.shape, 1)
    return jnp.where(lane >= column % extent, low, high)


def cut_kernel(*refs):
    count = (len(refs) - 1) // 2
    potential = refs[count]
    for k in range(count):
        for layer in range(potential.shape[0]):
            refs[count + 1 + k][layer] = columns_of(potential, layer, refs[k][0, 1])


def cut(potential, *positions):
    layers, strip, _ = potential.shape
    shape = jax.ShapeDtypeStruct((layers, strip, 2 * strip), f32)
    return pl.pallas_call(
        cut_kernel,
        out_shape=[shape] * len(positions),
        in_specs=[SMEM] * len(positions) + [VMEM],
        out_specs=[VMEM] * len(positions),
        name="cut",
    )(*positions, potential)


def merge_kernel(position, own, above, below, out):
    layers, strip, _ = own.shape
    local_row = position[0, 0] % strip
    for layer in range(layers):
        out[layer, :strip] = own[layer]
        row = lax.broadcasted_iota(jnp.int32, own.shape[1:], 0)
        out[layer, strip:] = jnp.where(row >= local_row, above[layer], below[layer])


def merge(position, own, above, below):
    layers, strip, extent = own.shape
    return pl.pallas_call(
        merge_kernel,
        out_shape=jax.ShapeDtypeStruct((layers, extent, extent), f32),
        in_specs=[SMEM] + [VMEM] * 3,
        out_specs=VMEM,
        name="merge",
    )(position, own, above, below)


def parts_of(x):
    high = x.astype(bf16)
    return high, (x - high.astype(f32)).astype(bf16)


def dot(a, b):
    return jnp.dot(a, b, preferred_element_type=f32)


def sandwich(m, real, imag):
    m = [m[k] for k in range(6)]
    rows = jnp.concatenate
    rh, rl = parts_of(real)
    ih, il = parts_of(imag)
    left = rows([rh, rl, rh, ih, il, ih], axis=1)
    yr = dot(left, rows([m[0], m[0], m[1], m[4], m[4], m[5]], axis=0))
    yi = dot(left, rows([m[2], m[2], m[3], m[0], m[0], m[1]], axis=0))
    rh, rl = parts_of(yr)
    ih, il = parts_of(yi)
    right = rows([rh, rl, rh, ih, il, ih], axis=0)
    zr = dot(rows([m[0], m[0], m[1], m[4], m[4], m[5]], axis=1), right)
    zi = dot(rows([m[2], m[2], m[3], m[0], m[0], m[1]], axis=1), right)
    return zr, zi


def solve_kernel(depth_count, place, position, probe, intensity, prop, dft, *refs):
    blocks = refs[:depth_count]
    out, trans, saved = refs[depth_count:]
    layers, extent, _ = out.shape
    strip = extent // 2
    slices = layers * depth_count
    depth = place[0]
    for k in range(depth_count):
        owner = (depth - k + depth_count) % depth_count
        for layer in range(layers):
            s, c = sin_cos(blocks[k][layer])
            trans[owner * layers + layer, 0] = c
            trans[owner * layers + layer, 1] = s

    row_shift = position[0, 0] % strip + strip
    column_shift = position[0, 1] % extent

    def rolled(x):
        return pltpu.roll(pltpu.roll(x, row_shift, 0), column_shift, 1)

    def transmit(s, real, imag):
        c = trans[s, 0]
        t = trans[s, 1]
        return c * real - t * imag, c * imag + t * real

    def forward(s, wave):
        real, imag = transmit(s, *wave)
        saved[s, 0] = real
        saved[s, 1] = imag
        return sandwich(prop, real, imag)

    wave = (rolled(probe[0]), rolled(probe[1]))
    wave = lax.fori_loop(0, slices - 1, forward, wave)
    real, imag = transmit(slices - 1, *wave)
    saved[slices - 1, 0] = real
    saved[slices - 1, 1] = imag
    far_real, far_imag = sandwich(dft, real, imag)
    misfit = far_real * far_real + far_imag * far_imag - intensity[0]
    wave = sandwich(dft, misfit * far_real, -(misfit * far_imag))

    def term(s, wave):
        @pl.when(s < (depth + 1) * layers)
        def _():
            real = saved[s, 0]
            imag = saved[s, 1]
            out[s - depth * layers] = -interaction * (wave[1] * real + wave[0] * imag)

    term(slices - 1, wave)

    def backward(step, wave):
        s = slices - 1 - step
        real, imag = transmit(s, *wave)
        wave = sandwich(prop, real, imag)
        term(s - 1, wave)
        return wave

    lax.fori_loop(0, slices - 1 - depth * layers, backward, wave)


def solve(place, position, probe, intensity, blocks):
    layers, extent, _ = blocks[0].shape
    count = len(blocks)
    slices = layers * count
    prop, dft = tables(extent)
    return pl.pallas_call(
        functools.partial(solve_kernel, count),
        out_shape=jax.ShapeDtypeStruct((layers, extent, extent), f32),
        in_specs=[SMEM] * 2 + [VMEM] * (4 + count),
        out_specs=VMEM,
        scratch_shapes=[pltpu.VMEM((slices, 2, extent, extent), f32)] * 2,
        compiler_params=pltpu.CompilerParams(vmem_limit_bytes=56 * 2**20),
        name="solve",
    )(place, position, probe, intensity, jnp.asarray(prop), jnp.asarray(dft), *blocks)


def place_kernel(position, before, after, own, from_before, from_after, out):
    layers, strip, columns = out.shape
    extent = 2 * strip
    row = lax.broadcasted_iota(jnp.int32, (strip, extent), 0)
    lane = lax.broadcasted_iota(jnp.int32, (strip, extent), 1)

    def covered(column, block):
        global_column = lane + block * extent
        return (global_column >= column) & (global_column < column + extent)

    below = row < before[0, 0] % strip
    above = row >= after[0, 0] % strip
    for block in range(columns // extent):
        mine = covered(position[0, 1], block)
        low = covered(before[0, 1], block) & below
        high = covered(after[0, 1], block) & above
        for layer in range(layers):
            value = jnp.where(mine, own[layer, :strip], 0.0)
            value = value + jnp.where(low, from_before[layer], 0.0)
            value = value + jnp.where(high, from_after[layer], 0.0)
            out[layer, :, block * extent : (block + 1) * extent] = value


def local(potential, probe, positions, intensity):
    layers, strip, columns = potential.shape
    extent = probe.shape[1]
    assert positions.shape[0] == 1 and extent == 2 * strip and columns % extent == 0
    count = lax.axis_size("probe")
    depth_count = lax.axis_size("depth")
    forward = [(i, (i + 1) % count) for i in range(count)]
    backward = [(i, (i - 1) % count) for i in range(count)]
    before = lax.ppermute(positions, "probe", forward)
    after = lax.ppermute(positions, "probe", backward)
    (own,) = cut(potential, positions)
    for_after, for_before = cut(potential, after, before)
    above = lax.ppermute(for_after, "probe", forward)
    below = lax.ppermute(for_before, "probe", backward)
    window = merge(positions, own, above, below)
    blocks = [window]
    for k in range(1, depth_count):
        pairs = [(i, (i + k) % depth_count) for i in range(depth_count)]
        blocks.append(lax.ppermute(window, "depth", pairs))
    place = lax.axis_index("depth").astype(jnp.int32).reshape(1)
    terms = solve(place, positions, probe, intensity, blocks)
    other = terms[:, strip:]
    from_before = lax.ppermute(other, "probe", forward)
    from_after = lax.ppermute(other, "probe", backward)
    return pl.pallas_call(
        place_kernel,
        out_shape=jax.ShapeDtypeStruct(potential.shape, f32),
        in_specs=[SMEM] * 3 + [VMEM] * 3,
        out_specs=VMEM,
        name="place",
    )(positions, before, after, terms, from_before, from_after)


def solution(mesh):
    in_specs = (P("depth", "probe", None), P(), P("probe", None), P("probe", None, None))
    out_specs = P("depth", "probe", None)
    return jax.shard_map(local, mesh=mesh, in_specs=in_specs, out_specs=out_specs, check_vma=False)
```

profile of v0, /device:TPU:0, one launch (start us, length us, event | category | flops | bytes accessed | tf_op | source)
XLA Modules:
  0.0 66.2 jit_solution(12631736278009873700)
XLA Ops:
  0.0 5.4 %collective-permute-start.1 = (s32[1,2]{1,0:T(1,128)}, s32[1,2]{1,0:T(1,128)S(1)}, u32[]{:S(2)}, u32[]{:S(2)}) collective-permute-start(s32[1,2]{1,0:T(1,128)} %position.5), channel_id=1, source_target_pairs={{0,30},{2,0},{4,2},{6,4},{8,6},{10,8},{12,10},{14,12},{16,14},{18,... | collective-permute-start | bytes 32 | tf_op jit(solution)/shard_map/ppermute | solution.py:250
  5.4 0.0 collective-permute-start
  5.4 1.4 %collective-permute-done.1.refs_0_.after = s32[1,2]{1,0:T(1,128)S(1)} collective-permute-done((s32[1,2]{1,0:T(1,128)}, s32[1,2]{1,0:T(1,128)S(1)}, u32[]{:S(2)}, u32[]{:S(2)}) %collective-permute-start.1) | collective-permute-done | bytes 40 | tf_op jit(solution)/shard_map/ppermute | solution.py:250
  6.9 0.0 copy-start.5
  6.9 4.4 %collective-permute-done.refs_1_.before = s32[1,2]{1,0:T(1,128)S(1)} collective-permute-done((s32[1,2]{1,0:T(1,128)}, s32[1,2]{1,0:T(1,128)S(1)}, u32[]{:S(2)}, u32[]{:S(2)}) %collective-permute-start) | collective-permute-done | bytes 40 | tf_op jit(solution)/shard_map/ppermute | solution.py:249
  11.3 0.0 copy-done.5
  11.3 0.0 copy-start.6
  11.3 0.6 copy-done.6
  11.9 2.1 %cut.3 = (f32[2,128,256]{2,1,0:T(8,128)}, f32[2,128,256]{2,1,0:T(8,128)}) custom-call(s32[1,2]{1,0:T(1,128)} %copy-done.5, s32[1,2]{1,0:T(1,128)} %copy-done.6, f32[2,128,1024]{2,1,0:T(8,128)} %refs_2_.1), custom_call_target="tpu_custom_call" | custom-call | tf_op jit(solution)/shard_map/cut/pallas_call | solution.py:89
  14.0 0.0 collective-permute-start.2
  14.0 4.4 %collective-permute-start.3 = (f32[2,128,256]{2,1,0:T(8,128)}, f32[2,128,256]{2,1,0:T(8,128)S(1)}, u32[]{:S(2)}, u32[]{:S(2)}) collective-permute-start(f32[2,128,256]{2,1,0:T(8,128)} %get-tuple-element.8), channel_id=1, source_target_pairs={{0,30},{2,0},{4,2},{6,4},{8,6},{10,8},{12,10},{14,12},{16,14},{18,... | collective-permute-start | bytes 786440 | tf_op jit(solution)/shard_map/ppermute | solution.py:254
  18.4 2.0 %cut.2.own = f32[2,128,256]{2,1,0:T(8,128)} custom-call(s32[1,2]{1,0:T(1,128)} %position.5, f32[2,128,1024]{2,1,0:T(8,128)} %refs_2_.1), custom_call_target="tpu_custom_call" | custom-call | tf_op jit(solution)/shard_map/cut/pallas_call | solution.py:89
  20.4 2.3 %collective-permute-done.2.above = f32[2,128,256]{2,1,0:T(8,128)S(1)} collective-permute-done((f32[2,128,256]{2,1,0:T(8,128)}, f32[2,128,256]{2,1,0:T(8,128)S(1)}, u32[]{:S(2)}, u32[]{:S(2)}) %collective-permute-start.2) | collective-permute-done | bytes 262176 | tf_op jit(solution)/shard_map/ppermute | solution.py:253
  22.7 0.0 copy-start.1
  22.7 0.0 collective-permute-done.3.below
  22.7 0.7 %copy-done.1 = f32[2,128,256]{2,1,0:T(8,128)} copy-done((f32[2,128,256]{2,1,0:T(8,128)}, f32[2,128,256]{2,1,0:T(8,128)S(1)}, u32[]{:S(2)}) %copy-start.1) | copy-done | bytes 262168
  23.4 0.0 copy-start.4
  23.4 0.7 %copy-done.4 = f32[2,128,256]{2,1,0:T(8,128)} copy-done((f32[2,128,256]{2,1,0:T(8,128)}, f32[2,128,256]{2,1,0:T(8,128)S(1)}, u32[]{:S(2)}) %copy-start.4) | copy-done | bytes 262168
  24.1 2.0 %merge.1.refs_0_ = f32[2,256,256]{2,1,0:T(8,128)} custom-call(s32[1,2]{1,0:T(1,128)} %position.5, f32[2,128,256]{2,1,0:T(8,128)} %cut.2.own, f32[2,128,256]{2,1,0:T(8,128)} %copy-done.1, f32[2,128,256]{2,1,0:T(8,128)} %copy-done.4), custom_call_target="tpu_custom_call" | custom-call | tf_op jit(solution)/shard_map/merge/pallas_call | solution.py:109
  26.1 1.5 %collective-permute-start.4 = (f32[2,256,256]{2,1,0:T(8,128)}, f32[2,256,256]{2,1,0:T(8,128)S(1)}, u32[]{:S(2)}, u32[]{:S(2)}) collective-permute-start(f32[2,256,256]{2,1,0:T(8,128)} %merge.1.refs_0_), channel_id=1, source_target_pairs={{0,1},{1,0},{2,3},{3,2},{4,5},{5,4},{6,7},{7,6},{8,9},{9,8},{10,11... | collective-permute-start | bytes 1572872 | tf_op jit(solution)/shard_map/ppermute | solution.py:259
  27.6 7.9 %collective-permute-done.4.refs_1_ = f32[2,256,256]{2,1,0:T(8,128)S(1)} collective-permute-done((f32[2,256,256]{2,1,0:T(8,128)}, f32[2,256,256]{2,1,0:T(8,128)S(1)}, u32[]{:S(2)}, u32[]{:S(2)}) %collective-permute-start.4) | collective-permute-done | bytes 524320 | tf_op jit(solution)/shard_map/ppermute | solution.py:259
  35.5 0.0 copy-start
  35.5 0.8 %copy-done = f32[2,256,256]{2,1,0:T(8,128)} copy-done((f32[2,256,256]{2,1,0:T(8,128)}, f32[2,256,256]{2,1,0:T(8,128)S(1)}, u32[]{:S(2)}) %copy-start) | copy-done | bytes 524312
  36.3 14.2 %solve.1.own = f32[2,256,256]{2,1,0:T(8,128)} custom-call(s32[1]{0:T(128)} %bitcast.place, s32[1,2]{1,0:T(1,128)} %position.5, f32[2,256,256]{2,1,0:T(8,128)} %probe.1, f32[1,256,256]{2,1,0:T(8,128)} %intensity.1, bf16[6,256,256]{2,1,0:T(8,128)(2,1)} %constant.8.clone.prop, bf16[6,256,256]{2,1,0:T(8,128)(2,1)} %constant.9.clone.dft, ...), custom_call_target="tpu_custom_call" | custom-call | tf_op jit(solution)/shard_map/solve/pallas_call | solution.py:207
  50.4 1.0 %slice.4 = f32[2,128,256]{2,1,0:T(8,128)S(1)} slice(f32[2,256,256]{2,1,0:T(8,128)} %solve.1.own), slice={[0:2], [128:256], [0:256]} | slice | bytes 524288 | tf_op jit(solution)/shard_map/slice | solution.py:262
  51.4 3.1 %collective-permute-start.6 = (f32[2,128,256]{2,1,0:T(8,128)S(1)}, f32[2,128,256]{2,1,0:T(8,128)S(1)}, u32[]{:S(2)}, u32[]{:S(2)}) collective-permute-start(f32[2,128,256]{2,1,0:T(8,128)S(1)} %slice.4), channel_id=1, source_target_pairs={{0,30},{2,0},{4,2},{6,4},{8,6},{10,8},{12,10},{14,12},{16,14},{18,... | collective-permute-start | bytes 786440 | tf_op jit(solution)/shard_map/ppermute | solution.py:264
  54.6 0.0 collective-permute-start.5
  54.6 3.9 %collective-permute-done.6.from_after = f32[2,128,256]{2,1,0:T(8,128)S(1)} collective-permute-done((f32[2,128,256]{2,1,0:T(8,128)S(1)}, f32[2,128,256]{2,1,0:T(8,128)S(1)}, u32[]{:S(2)}, u32[]{:S(2)}) %collective-permute-start.6) | collective-permute-done | bytes 262176 | tf_op jit(solution)/shard_map/ppermute | solution.py:264
  58.4 0.0 copy-start.2
  58.5 4.6 %collective-permute-done.5.from_before = f32[2,128,256]{2,1,0:T(8,128)S(1)} collective-permute-done((f32[2,128,256]{2,1,0:T(8,128)S(1)}, f32[2,128,256]{2,1,0:T(8,128)S(1)}, u32[]{:S(2)}, u32[]{:S(2)}) %collective-permute-start.5) | collective-permute-done | bytes 262176 | tf_op jit(solution)/shard_map/ppermute | solution.py:263
  63.1 0.0 copy-done.2
  63.1 0.0 copy-start.3
  63.1 0.7 %copy-done.3 = f32[2,128,256]{2,1,0:T(8,128)} copy-done((f32[2,128,256]{2,1,0:T(8,128)}, f32[2,128,256]{2,1,0:T(8,128)S(1)}, u32[]{:S(2)}) %copy-start.3) | copy-done | bytes 262168
  63.8 2.5 %place.1 = f32[2,128,1024]{2,1,0:T(8,128)} custom-call(s32[1,2]{1,0:T(1,128)} %position.5, s32[1,2]{1,0:T(1,128)} %copy-done.6, s32[1,2]{1,0:T(1,128)} %copy-done.5, f32[2,256,256]{2,1,0:T(8,128)} %solve.1.own, f32[2,128,256]{2,1,0:T(8,128)} %copy-done.3, f32[2,128,256]{2,1,0:T(8,128)} %copy-done.2), custom_call_target="tpu_custom_call" | custom-call | tf_op jit(solution)/shard_map/place/pallas_call | solution.py:265
Async XLA Ops:
  0.0 6.9 %collective-permute-start.1 = (s32[1,2]{1,0:T(1,128)}, s32[1,2]{1,0:T(1,128)S(1)}, u32[]{:S(2)}, u32[]{:S(2)}) collective-permute-start(s32[1,2]{1,0:T(1,128)} %position.5), channel_id=1, source_target_pairs={{0,30},{2,0},{4,2},{6,4},{8,6},{10,8},{12,10},{14,12},{16,14},{18,... | collective-permute-start | bytes 32 | tf_op jit(solution)/shard_map/ppermute | solution.py:250
  5.4 5.8 %collective-permute-start = (s32[1,2]{1,0:T(1,128)}, s32[1,2]{1,0:T(1,128)S(1)}, u32[]{:S(2)}, u32[]{:S(2)}) collective-permute-start(s32[1,2]{1,0:T(1,128)} %position.5), channel_id=1, source_target_pairs={{0,2},{2,4},{4,6},{6,8},{8,10},{10,12},{12,14},{14,16},{16,18},{18... | collective-permute-start | bytes 32 | tf_op jit(solution)/shard_map/ppermute | solution.py:249
  6.9 4.4 %copy-start.5 = (s32[1,2]{1,0:T(1,128)}, s32[1,2]{1,0:T(1,128)S(1)}, u32[]{:S(2)}) copy-start(s32[1,2]{1,0:T(1,128)S(1)} %collective-permute-done.1.refs_0_.after) | copy-start | bytes 28
  11.3 0.6 copy-start.6
  14.0 8.7 %collective-permute-start.2 = (f32[2,128,256]{2,1,0:T(8,128)}, f32[2,128,256]{2,1,0:T(8,128)S(1)}, u32[]{:S(2)}, u32[]{:S(2)}) collective-permute-start(f32[2,128,256]{2,1,0:T(8,128)} %get-tuple-element.7), channel_id=1, source_target_pairs={{0,2},{2,4},{4,6},{6,8},{8,10},{10,12},{12,14},{14,16},{16,18},{18... | collective-permute-start | bytes 786440 | tf_op jit(solution)/shard_map/ppermute | solution.py:253
  14.0 8.7 %collective-permute-start.3 = (f32[2,128,256]{2,1,0:T(8,128)}, f32[2,128,256]{2,1,0:T(8,128)S(1)}, u32[]{:S(2)}, u32[]{:S(2)}) collective-permute-start(f32[2,128,256]{2,1,0:T(8,128)} %get-tuple-element.8), channel_id=1, source_target_pairs={{0,30},{2,0},{4,2},{6,4},{8,6},{10,8},{12,10},{14,12},{16,14},{18,... | collective-permute-start | bytes 786440 | tf_op jit(solution)/shard_map/ppermute | solution.py:254
  22.7 0.7 %copy-start.1 = (f32[2,128,256]{2,1,0:T(8,128)}, f32[2,128,256]{2,1,0:T(8,128)S(1)}, u32[]{:S(2)}) copy-start(f32[2,128,256]{2,1,0:T(8,128)S(1)} %collective-permute-done.2.above) | copy-start | bytes 786436
  23.4 0.7 %copy-start.4 = (f32[2,128,256]{2,1,0:T(8,128)}, f32[2,128,256]{2,1,0:T(8,128)S(1)}, u32[]{:S(2)}) copy-start(f32[2,128,256]{2,1,0:T(8,128)S(1)} %collective-permute-done.3.below) | copy-start | bytes 786436
  26.1 9.4 %collective-permute-start.4 = (f32[2,256,256]{2,1,0:T(8,128)}, f32[2,256,256]{2,1,0:T(8,128)S(1)}, u32[]{:S(2)}, u32[]{:S(2)}) collective-permute-start(f32[2,256,256]{2,1,0:T(8,128)} %merge.1.refs_0_), channel_id=1, source_target_pairs={{0,1},{1,0},{2,3},{3,2},{4,5},{5,4},{6,7},{7,6},{8,9},{9,8},{10,11... | collective-permute-start | bytes 1572872 | tf_op jit(solution)/shard_map/ppermute | solution.py:259
  35.5 0.8 %copy-start = (f32[2,256,256]{2,1,0:T(8,128)}, f32[2,256,256]{2,1,0:T(8,128)S(1)}, u32[]{:S(2)}) copy-start(f32[2,256,256]{2,1,0:T(8,128)S(1)} %collective-permute-done.4.refs_1_) | copy-start | bytes 1572868
  51.4 7.0 %collective-permute-start.6 = (f32[2,128,256]{2,1,0:T(8,128)S(1)}, f32[2,128,256]{2,1,0:T(8,128)S(1)}, u32[]{:S(2)}, u32[]{:S(2)}) collective-permute-start(f32[2,128,256]{2,1,0:T(8,128)S(1)} %slice.4), channel_id=1, source_target_pairs={{0,30},{2,0},{4,2},{6,4},{8,6},{10,8},{12,10},{14,12},{16,14},{18,... | collective-permute-start | bytes 786440 | tf_op jit(solution)/shard_map/ppermute | solution.py:264
  54.6 8.5 %collective-permute-start.5 = (f32[2,128,256]{2,1,0:T(8,128)S(1)}, f32[2,128,256]{2,1,0:T(8,128)S(1)}, u32[]{:S(2)}, u32[]{:S(2)}) collective-permute-start(f32[2,128,256]{2,1,0:T(8,128)S(1)} %slice.4), channel_id=1, source_target_pairs={{0,2},{2,4},{4,6},{6,8},{8,10},{10,12},{12,14},{14,16},{16,18},{18... | collective-permute-start | bytes 786440 | tf_op jit(solution)/shard_map/ppermute | solution.py:263
  58.4 4.6 %copy-start.2 = (f32[2,128,256]{2,1,0:T(8,128)}, f32[2,128,256]{2,1,0:T(8,128)S(1)}, u32[]{:S(2)}) copy-start(f32[2,128,256]{2,1,0:T(8,128)S(1)} %collective-permute-done.6.from_after) | copy-start | bytes 786436
  63.1 0.7 %copy-start.3 = (f32[2,128,256]{2,1,0:T(8,128)}, f32[2,128,256]{2,1,0:T(8,128)S(1)}, u32[]{:S(2)}) copy-start(f32[2,128,256]{2,1,0:T(8,128)S(1)} %collective-permute-done.5.from_before) | copy-start | bytes 786436
where the time goes:
time: 66.5 us; the launch traced here: 66.2 us
  waiting for transfers between devices  24.5 us (37%)
  Pallas kernels  22.7 us (34%)
  starting transfers between devices  14.6 us (22%)
  local copies, waits for them, and re-layouts  4.5 us (7%)
    pallas_call x1, Pallas kernels, solve(): pl.pallas_call(functools.partial(solve_kernel, count), out_shape=jax.Shap...  14.2 us
    ppermute x1, waiting for transfers between devices, local(): blocks.append(lax.ppermute(window, 'depth', pairs))  7.87 us
    ppermute x1, starting transfers between devices, local(): after = lax.ppermute(positions, 'probe', backward)  5.44 us
    ppermute x1, waiting for transfers between devices, local(): from_before = lax.ppermute(other, 'probe', forward)  4.6 us
    ppermute x1, starting transfers between devices, local(): below = lax.ppermute(for_before, 'probe', backward)  4.44 us
    ppermute x1, waiting for transfers between devices, local(): before = lax.ppermute(positions, 'probe', forward)  4.39 us
    pallas_call x2, Pallas kernels, cut(): pl.pallas_call(cut_kernel, out_shape=[shape] * len(positions), in_specs=[...  4.1 us
    ppermute x1, waiting for transfers between devices, local(): from_after = lax.ppermute(other, 'probe', backward)  3.89 us
  transfers between devices with their start and end apart: 7, of which 6 were waited for; matrix products, arithmetic and copies ran while one was open for 0% of the time, Pallas kernels for 3%

commit v1 on v0

v1 whole, which is shorter than its diff:
```python
import functools

import jax
import jax.numpy as jnp
import numpy as np
from jax import lax
from jax.experimental import pallas as pl
from jax.experimental.pallas import tpu as pltpu
from jax.sharding import PartitionSpec as P

interaction = 0.5
fresnel_phase = 60.0
f32 = jnp.float32
bf16 = jnp.bfloat16

VMEM = pl.BlockSpec(memory_space=pltpu.VMEM)
SMEM = pl.BlockSpec(memory_space=pltpu.SMEM)
ANY = pl.BlockSpec(memory_space=pl.ANY)


def poly_tables():
    x = np.cos(np.linspace(0.0, np.pi / 2, 4001)) * (np.pi / 2) * 1.0005
    z = x * x
    fit = np.polynomial.chebyshev.Chebyshev.fit
    kind = np.polynomial.Polynomial
    sine = fit(z, np.sinc(x / np.pi), 5).convert(kind=kind).coef
    cosine = fit(z, np.cos(x), 5).convert(kind=kind).coef
    return [float(v) for v in sine], [float(v) for v in cosine]


def split_table(matrix):
    parts = []
    for real in (matrix.real, matrix.imag, -matrix.imag):
        wide = real.astype(np.float32)
        high = wide.astype(bf16)
        parts.append(high)
        parts.append((real - high.astype(np.float64)).astype(np.float32).astype(bf16))
    return np.stack(parts)


def tables(extent):
    index = np.arange(extent)
    dft = np.exp(-2j * np.pi * ((index[:, None] * index[None, :]) % extent) / extent)
    dft = dft / np.sqrt(extent)
    frequency = ((index + extent // 2) % extent - extent // 2) / extent
    chirp = np.exp(-1j * fresnel_phase * frequency**2)
    propagator = np.conj(dft) @ (chirp[:, None] * dft)
    return split_table(propagator), split_table(dft)


def sin_cos(window):
    sine, cosine = poly_tables()
    half = window * (interaction / 2)
    turns = jnp.round(half * (1.0 / np.pi))
    pi_high = float(np.float32(3.140625))
    pi_low = float(np.pi - 3.140625)
    x = (half - turns * pi_high) - turns * pi_low
    z = x * x
    s = sine[5]
    c = cosine[5]
    for k in range(4, -1, -1):
        s = s * z + sine[k]
        c = c * z + cosine[k]
    s = s * x
    return 2.0 * s * c, 1.0 - 2.0 * (s * s)


def parts_of(x):
    high = x.astype(bf16)
    return high, (x - high.astype(f32)).astype(bf16)


def dot(a, b):
    return jnp.dot(a, b, preferred_element_type=f32)


def sandwich(m, real, imag):
    m = [m[k] for k in range(6)]
    rows = jnp.concatenate
    rh, rl = parts_of(real)
    ih, il = parts_of(imag)
    left = rows([rh, rl, rh, ih, il, ih], axis=1)
    yr = dot(left, rows([m[0], m[0], m[1], m[4], m[4], m[5]], axis=0))
    yi = dot(left, rows([m[2], m[2], m[3], m[0], m[0], m[1]], axis=0))
    rh, rl = parts_of(yr)
    ih, il = parts_of(yi)
    right = rows([rh, rl, rh, ih, il, ih], axis=0)
    zr = dot(rows([m[0], m[0], m[1], m[4], m[4], m[5]], axis=1), right)
    zi = dot(rows([m[2], m[2], m[3], m[0], m[0], m[1]], axis=1), right)
    return zr, zi


def call(kernel, name, results, scalars, arrays, scratch=(), limit=16):
    arrays = [pltpu.with_memory_space_constraint(x, pltpu.VMEM) for x in arrays]
    out = pl.pallas_call(
        kernel,
        out_shape=[pltpu.VMEM(shape, f32) for shape in results],
        in_specs=[SMEM] * len(scalars) + [VMEM] * len(arrays),
        out_specs=[VMEM] * len(results),
        scratch_shapes=list(scratch),
        compiler_params=pltpu.CompilerParams(vmem_limit_bytes=limit * 2**20),
        name=name,
    )(*scalars, *arrays)
    return out


def entry(position, k):
    return position[0:1, k : k + 1]


def covered(column, block, shape):
    lane = lax.broadcasted_iota(jnp.int32, shape, 1) + block * shape[1]
    return (lane >= column) & (lane < column + shape[1])


def cut_kernel(*refs):
    count = (len(refs) - 1) // 2
    potential = refs[count]
    layers, strip, columns = potential.shape
    extent = 2 * strip
    for k in range(count):
        out = refs[count + 1 + k]
        column = entry(refs[k], 1)
        for layer in range(layers):
            value = potential[layer, :, :extent]
            for block in range(1, columns // extent):
                mask = covered(column, block, value.shape)
                next_value = potential[layer, :, block * extent : (block + 1) * extent]
                value = jnp.where(mask, next_value, value)
            out[layer] = value


def cut(potential, *positions):
    layers, strip, _ = potential.shape
    shapes = [(layers, strip, 2 * strip)] * len(positions)
    return call(cut_kernel, "cut", shapes, [], [*positions, potential])


def prepare_kernel(*refs):
    count = len(refs) // 2
    for k in range(count):
        for layer in range(refs[k].shape[0]):
            s, c = sin_cos(refs[k][layer])
            refs[count + k][layer, 0] = c
            refs[count + k][layer, 1] = s


def prepare(*pieces):
    shapes = [(x.shape[0], 2, *x.shape[1:]) for x in pieces]
    return call(prepare_kernel, "prepare", shapes, [], pieces)


def merge_kernel(position, above, below, out):
    layers, strip, extent = out.shape
    row = lax.broadcasted_iota(jnp.int32, (strip, extent), 0)
    mask = row >= entry(position, 0) % strip
    for layer in range(layers):
        out[layer] = jnp.where(mask, above[layer], below[layer])


def transmit(trans, real, imag):
    c, s = trans
    return c * real - s * imag, c * imag + s * real


def joined(upper, lower, layer):
    return [jnp.concatenate([upper[layer, k], lower[layer, k]], axis=0) for k in range(2)]


def enter_kernel(place, position, probe, prop, upper, other, wave_out, saved, lower):
    layers, strip, extent = other.shape
    for layer in range(layers):
        s, c = sin_cos(other[layer])
        lower[layer, 0] = c
        lower[layer, 1] = s
    row_shift = position[0, 0] % strip + strip
    column_shift = position[0, 1] % extent
    for k in range(2):
        wave_out[k] = pltpu.roll(pltpu.roll(probe[k], row_shift, 0), column_shift, 1)

    def forward(layer, wave):
        wave = transmit(joined(upper, lower, layer), *wave)
        saved[layer, 0] = wave[0]
        saved[layer, 1] = wave[1]
        return sandwich(prop, *wave)

    @pl.when(place[0] == 0)
    def _():
        wave = lax.fori_loop(0, layers, forward, (wave_out[0], wave_out[1]))
        wave_out[0] = wave[0]
        wave_out[1] = wave[1]


def solve_kernel(count, place, wave_in, saved_in, intensity, prop, dft, *refs):
    uppers = refs[:count]
    lower = refs[count]
    others = refs[count + 1 : 2 * count]
    mine, other, trans, saved = refs[2 * count :]
    layers, strip, extent = mine.shape
    slices = layers * count
    depth = place[0]
    for k in range(count):
        owner = (depth - k + count) % count
        for layer in range(layers):
            if k == 0:
                half = lower[layer, 0], lower[layer, 1]
            else:
                half = sin_cos(others[k - 1][layer])[::-1]
            for part in range(2):
                trans[owner * layers + layer, part, :strip] = uppers[k][layer, part]
                trans[owner * layers + layer, part, strip:] = half[part]

    @pl.when(depth == 0)
    def _():
        for layer in range(layers):
            for part in range(2):
                saved[layer, part] = saved_in[layer, part]

    def forward(s, wave):
        wave = transmit((trans[s, 0], trans[s, 1]), *wave)
        saved[s, 0] = wave[0]
        saved[s, 1] = wave[1]
        return sandwich(prop, *wave)

    wave = (wave_in[0], wave_in[1])
    wave = lax.fori_loop(jnp.where(depth == 0, layers, 0), slices - 1, forward, wave)
    last = slices - 1
    real, imag = transmit((trans[last, 0], trans[last, 1]), *wave)
    saved[last, 0] = real
    saved[last, 1] = imag
    far_real, far_imag = sandwich(dft, real, imag)
    misfit = far_real * far_real + far_imag * far_imag - intensity[0]
    wave = sandwich(dft, misfit * far_real, -(misfit * far_imag))

    def term(s, wave):
        @pl.when(s < (depth + 1) * layers)
        def _():
            value = -interaction * (wave[1] * saved[s, 0] + wave[0] * saved[s, 1])
            mine[s - depth * layers] = value[:strip]
            other[s - depth * layers] = value[strip:]

    term(last, wave)

    def backward(step, wave):
        s = last - step
        wave = sandwich(prop, *transmit((trans[s, 0], trans[s, 1]), *wave))
        term(s - 1, wave)
        return wave

    lax.fori_loop(0, last - depth * layers, backward, wave)


def place_kernel(position, before, after, own, from_before, from_after, out, staged, sems):
    layers, strip, columns = out.shape
    extent = 2 * strip
    shape = (strip, extent)
    row = lax.broadcasted_iota(jnp.int32, shape, 0)
    below = row < entry(before, 0) % strip
    above = row >= entry(after, 0) % strip
    copies = []
    for block in range(columns // extent):
        at = slice(block * extent, (block + 1) * extent)
        mine = covered(entry(position, 1), block, shape)
        low = covered(entry(before, 1), block, shape) & below
        high = covered(entry(after, 1), block, shape) & above
        for layer in range(layers):
            value = jnp.where(mine, own[layer], 0.0)
            value = value + jnp.where(low, from_before[layer], 0.0)
            value = value + jnp.where(high, from_after[layer], 0.0)
            staged[layer, :, at] = value
        copy = pltpu.make_async_copy(staged.at[:, :, at], out.at[:, :, at], sems.at[block])
        copy.start()
        copies.append(copy)
    for copy in copies:
        copy.wait()


def local(potential, probe, positions, intensity):
    layers, strip, columns = potential.shape
    extent = probe.shape[1]
    assert positions.shape[0] == 1 and extent == 2 * strip and columns % extent == 0
    count = lax.axis_size("probe")
    depth_count = lax.axis_size("depth")
    slices = layers * depth_count
    onward = [(i, (i + 1) % count) for i in range(count)]
    backward = [(i, (i - 1) % count) for i in range(count)]
    before = lax.ppermute(positions, "probe", onward)
    after = lax.ppermute(positions, "probe", backward)

    def from_depths(x):
        out = [x]
        for k in range(1, depth_count):
            pairs = [(i, (i + k) % depth_count) for i in range(depth_count)]
            out.append(lax.ppermute(x, "depth", pairs))
        return out

    (own,) = cut(potential, positions)
    owns = from_depths(own)
    for_after, for_before = cut(potential, after, before)
    above = lax.ppermute(for_after, "probe", onward)
    below = lax.ppermute(for_before, "probe", backward)
    uppers = [prepare(x)[0] for x in owns]
    half = (layers, strip, extent)
    (other,) = call(merge_kernel, "merge", [half], [], [positions, above, below])
    others = from_depths(other)
    place = lax.axis_index("depth").astype(jnp.int32).reshape(1)
    prop, dft = [jnp.asarray(x) for x in tables(extent)]
    field = (2, extent, extent)
    wave, saved, lower = call(
        enter_kernel,
        "enter",
        [field, (layers, *field), (layers, 2, strip, extent)],
        [place, positions],
        [probe, prop, uppers[0], other],
    )
    mine, outer = call(
        functools.partial(solve_kernel, depth_count),
        "solve",
        [half, half],
        [place],
        [wave, saved, intensity, prop, dft, *uppers, lower, *others[1:]],
        scratch=[pltpu.VMEM((slices, *field), f32)] * 2,
        limit=12 + slices * 4 * extent * extent // 2**20 * 4 + 8,
    )
    from_before = lax.ppermute(outer, "probe", onward)
    from_after = lax.ppermute(outer, "probe", backward)
    arrays = [positions, before, after, mine, from_before, from_after]
    arrays = [pltpu.with_memory_space_constraint(x, pltpu.VMEM) for x in arrays]
    return pl.pallas_call(
        place_kernel,
        out_shape=jax.ShapeDtypeStruct(potential.shape, f32),
        in_specs=[VMEM] * 6,
        out_specs=ANY,
        scratch_shapes=[
            pltpu.VMEM(potential.shape, f32),
            pltpu.SemaphoreType.DMA((columns // extent,)),
        ],
        name="place",
    )(*arrays)


def solution(mesh):
    in_specs = (P("depth", "probe", None), P(), P("probe", None), P("probe", None, None))
    out_specs = P("depth", "probe", None)
    return jax.shard_map(local, mesh=mesh, in_specs=in_specs, out_specs=out_specs, check_vma=False)
```

time: 66.5 us -> 49.7 us (0.75)
  Pallas kernels: 22.7 us -> 13.4 us
  waiting for transfers between devices: 24.5 us -> 17.9 us
  local copies, waits for them, and re-layouts: 4.5 us -> 1.26 us
  starting transfers between devices: 14.6 us -> 16.8 us
    pallas_call x4 -> x7, Pallas kernels: 20.2 us -> 12.2 us  [call(): pl.pallas_call(kernel, out_shape=[pltpu.VMEM(shape, f32) for shape in res...]
    ppermute x5 -> x6, waiting for transfers between devices: 23 us -> 16.5 us  [the longest x1 4.6 us: local(): from_before = lax.ppermute(outer, 'probe', onward)]
    unnamed x14, local copies, waits for them, and re-layouts: 3.54 us -> 1.26 us
    ppermute x5 -> x6, starting transfers between devices: 4.68 us -> 6.88 us  [the longest x1 3.65 us: local(): from_after = lax.ppermute(outer, 'probe', backward)]
    pallas_call x1, Pallas kernels: 2.46 us -> 1.27 us  [local(): pl.pallas_call(place_kernel, out_shape=jax.ShapeDtypeStruct(potential.sha...]
    slice x1 -> x0, local copies, waits for them, and re-layouts: 0.97 us -> none  [local(): other = terms[:, strip:]]
  transfers between devices with their start and end apart: 7 -> 8, of which waited for: 6 -> 6; matrix products, arithmetic and copies ran while one was open for 0% -> 0% of each run, Pallas kernels for 3% -> 9%
where the time goes in v1:
time: 49.7 us; the launch traced here: 49.5 us
  waiting for transfers between devices  17.9 us (36%)
  starting transfers between devices  16.8 us (34%)
  Pallas kernels  13.4 us (27%)
  local copies, waits for them, and re-layouts  1.26 us (3%)
    pallas_call x7, Pallas kernels, call(): pl.pallas_call(kernel, out_shape=[pltpu.VMEM(shape, f32) for shape in res...  12.2 us
    ppermute x1, starting transfers between devices, local(): after = lax.ppermute(positions, 'probe', backward)  5.44 us
    ppermute x1, waiting for transfers between devices, local(): from_before = lax.ppermute(outer, 'probe', onward)  4.6 us
    ppermute x1, starting transfers between devices, local(): below = lax.ppermute(for_before, 'probe', backward)  4.43 us
    ppermute x1, waiting for transfers between devices, local(): before = lax.ppermute(positions, 'probe', onward)  4.4 us
    ppermute x1, waiting for transfers between devices, local(): from_after = lax.ppermute(outer, 'probe', backward)  3.89 us
    ppermute x1, starting transfers between devices, local(): from_after = lax.ppermute(outer, 'probe', backward)  3.65 us
    ppermute x2, starting transfers between devices, from_depths(): out.append(lax.ppermute(x, 'depth', pairs))  3.17 us
  transfers between devices with their start and end apart: 8, of which 6 were waited for; matrix products, arithmetic and copies ran while one was open for 0% of the time, Pallas kernels for 9%

profile of v1, /device:TPU:0, one launch (start us, length us, event | category | flops | bytes accessed | tf_op | source)
XLA Modules:
  0.0 49.5 jit_solution(1635874027120647267)
XLA Ops:
  0.0 5.4 %collective-permute-start.1 = (s32[1,2]{1,0:T(1,128)}, s32[1,2]{1,0:T(1,128)S(1)}, u32[]{:S(2)}, u32[]{:S(2)}) collective-permute-start(s32[1,2]{1,0:T(1,128)} %position.5), channel_id=1, source_target_pairs={{0,30},{2,0},{4,2},{6,4},{8,6},{10,8},{12,10},{14,12},{16,14},{18,... | collective-permute-start | bytes 32 | tf_op jit(solution)/shard_map/ppermute | solution.py:288
  5.4 0.0 collective-permute-start
  5.4 1.4 %collective-permute-done.1.refs_0_.after = s32[1,2]{1,0:T(1,128)S(1)} collective-permute-done((s32[1,2]{1,0:T(1,128)}, s32[1,2]{1,0:T(1,128)S(1)}, u32[]{:S(2)}, u32[]{:S(2)}) %collective-permute-start.1) | collective-permute-done | bytes 40 | tf_op jit(solution)/shard_map/ppermute | solution.py:288
  6.9 4.4 %collective-permute-done.refs_1_.before = s32[1,2]{1,0:T(1,128)S(1)} collective-permute-done((s32[1,2]{1,0:T(1,128)}, s32[1,2]{1,0:T(1,128)S(1)}, u32[]{:S(2)}, u32[]{:S(2)}) %collective-permute-start) | collective-permute-done | bytes 40 | tf_op jit(solution)/shard_map/ppermute | solution.py:287
  11.3 0.0 copy-start
  11.3 1.2 %copy-done = f32[2,128,1024]{2,1,0:T(8,128)S(1)} copy-done((f32[2,128,1024]{2,1,0:T(8,128)S(1)}, f32[2,128,1024]{2,1,0:T(8,128)}, u32[]{:S(2)}) %copy-start) | copy-done | bytes 1048600
  12.5 0.0 copy-start.1
  12.5 0.2 cut.3
  12.7 0.0 copy-start.6
  12.7 0.1 collective-permute-start.2
  12.8 4.4 %collective-permute-start.3 = (f32[2,128,256]{2,1,0:T(8,128)S(1)}, f32[2,128,256]{2,1,0:T(8,128)S(1)}, u32[]{:S(2)}, u32[]{:S(2)}) collective-permute-start(f32[2,128,256]{2,1,0:T(8,128)S(1)} %get-tuple-element.13), channel_id=1, source_target_pairs={{0,30},{2,0},{4,2},{6,4},{8,6},{10,8},{12,10},{14,12},{16,14},{18,... | collective-permute-start | bytes 786440 | tf_op jit(solution)/shard_map/ppermute | solution.py:301
  17.2 0.0 copy-done.1
  17.2 0.0 copy-done.6
  17.2 0.1 cut.2.refs_0_
  17.4 1.6 %collective-permute-start.4 = (f32[2,128,256]{2,1,0:T(8,128)S(1)}, f32[2,128,256]{2,1,0:T(8,128)S(1)}, u32[]{:S(2)}, u32[]{:S(2)}) collective-permute-start(f32[2,128,256]{2,1,0:T(8,128)S(1)} %cut.2.refs_0_), channel_id=1, source_target_pairs={{0,1},{1,0},{2,3},{3,2},{4,5},{5,4},{6,7},{7,6},{8,9},{9,8},{10,11... | collective-permute-start | bytes 786440 | tf_op jit(solution)/shard_map/ppermute | solution.py:294
  19.0 2.3 %collective-permute-done.2.above = f32[2,128,256]{2,1,0:T(8,128)S(1)} collective-permute-done((f32[2,128,256]{2,1,0:T(8,128)S(1)}, f32[2,128,256]{2,1,0:T(8,128)S(1)}, u32[]{:S(2)}, u32[]{:S(2)}) %collective-permute-start.2) | collective-permute-done | bytes 262176 | tf_op jit(solution)/shard_map/ppermute | solution.py:300
  21.3 0.0 collective-permute-done.3.below
  21.3 0.1 merge.1.other
  21.4 1.6 %collective-permute-start.5 = (f32[2,128,256]{2,1,0:T(8,128)S(1)}, f32[2,128,256]{2,1,0:T(8,128)S(1)}, u32[]{:S(2)}, u32[]{:S(2)}) collective-permute-start(f32[2,128,256]{2,1,0:T(8,128)S(1)} %merge.1.other), channel_id=1, source_target_pairs={{0,1},{1,0},{2,3},{3,2},{4,5},{5,4},{6,7},{7,6},{8,9},{9,8},{10,11... | collective-permute-start | bytes 786440 | tf_op jit(solution)/shard_map/ppermute | solution.py:294
  23.0 0.0 copy-start.2
  23.0 0.3 prepare.2.upper.refs_0_
  23.3 0.0 copy-start.4
  23.3 1.3 %collective-permute-done.4.refs_0_ = f32[2,128,256]{2,1,0:T(8,128)S(1)} collective-permute-done((f32[2,128,256]{2,1,0:T(8,128)S(1)}, f32[2,128,256]{2,1,0:T(8,128)S(1)}, u32[]{:S(2)}, u32[]{:S(2)}) %collective-permute-start.4) | collective-permute-done | bytes 262176 | tf_op jit(solution)/shard_map/ppermute | solution.py:294
  24.6 0.3 prepare.3.refs_1_
  24.9 0.0 copy-done.2
  24.9 0.0 copy-done.4
  24.9 0.0 copy-start.3
  24.9 0.0 copy-start.5
  24.9 3.6 %enter.1 = (f32[2,256,256]{2,1,0:T(8,128)S(1)}, f32[2,2,256,256]{3,2,1,0:T(8,128)S(1)}, f32[2,2,128,256]{3,2,1,0:T(8,128)S(1)}) custom-call(s32[1]{0:T(128)} %bitcast.place, s32[1,2]{1,0:T(1,128)S(1)} %copy-done.6, f32[2,256,256]{2,1,0:T(8,128)S(1)} %copy-done.4, bf16[6,256,256]{2,1,0:T(8,128)(2,1)S(1)} %copy-done.2, ...), custom_call_target="tpu_custom_call" | custom-call | tf_op jit(solution)/shard_map/enter/pallas_call | solution.py:95
  28.6 0.0 collective-permute-done.5.refs_3_
  28.6 0.0 copy-done.3
  28.6 0.0 copy-done.5
  28.6 7.5 %solve.1 = (f32[2,128,256]{2,1,0:T(8,128)S(1)}, f32[2,128,256]{2,1,0:T(8,128)S(1)}) custom-call(s32[1]{0:T(128)} %bitcast.place, f32[2,256,256]{2,1,0:T(8,128)S(1)} %get-tuple-element.14.wave_in, f32[2,2,256,256]{3,2,1,0:T(8,128)S(1)} %get-tuple-element.15.saved_in, f32[1,256,256]{2,1,0:T(8,128)S(1)} %copy-done.5, bf16[6,256,256]{2,1,0:T(8,128)(2,1)S(1)} %copy-done.2, ...), custom_call_target="tpu_custom_call" | custom-call | tf_op jit(solution)/shard_map/solve/pallas_call | solution.py:95
  36.1 3.6 %collective-permute-start.7 = (f32[2,128,256]{2,1,0:T(8,128)S(1)}, f32[2,128,256]{2,1,0:T(8,128)S(1)}, u32[]{:S(2)}, u32[]{:S(2)}) collective-permute-start(f32[2,128,256]{2,1,0:T(8,128)S(1)} %get-tuple-element.18), channel_id=1, source_target_pairs={{0,30},{2,0},{4,2},{6,4},{8,6},{10,8},{12,10},{14,12},{16,14},{18,... | collective-permute-start | bytes 786440 | tf_op jit(solution)/shard_map/ppermute | solution.py:326
  39.7 0.0 collective-permute-start.6
  39.7 3.9 %collective-permute-done.7.from_after = f32[2,128,256]{2,1,0:T(8,128)S(1)} collective-permute-done((f32[2,128,256]{2,1,0:T(8,128)S(1)}, f32[2,128,256]{2,1,0:T(8,128)S(1)}, u32[]{:S(2)}, u32[]{:S(2)}) %collective-permute-start.7) | collective-permute-done | bytes 262176 | tf_op jit(solution)/shard_map/ppermute | solution.py:326
  43.6 4.6 %collective-permute-done.6.from_before = f32[2,128,256]{2,1,0:T(8,128)S(1)} collective-permute-done((f32[2,128,256]{2,1,0:T(8,128)S(1)}, f32[2,128,256]{2,1,0:T(8,128)S(1)}, u32[]{:S(2)}, u32[]{:S(2)}) %collective-permute-start.6) | collective-permute-done | bytes 262176 | tf_op jit(solution)/shard_map/ppermute | solution.py:325
  48.2 1.3 %place.1 = f32[2,128,1024]{2,1,0:T(8,128)} custom-call(s32[1,2]{1,0:T(1,128)S(1)} %copy-done.6, s32[1,2]{1,0:T(1,128)S(1)} %collective-permute-done.refs_1_.before, s32[1,2]{1,0:T(1,128)S(1)} %collective-permute-done.1.refs_0_.after, f32[2,128,256]{2,1,0:T(8,128)S(1)} %get-tuple-element.17.own, f32[2,128,256]{2,1,0:T(8,128)S(1)} %collective-permute-done.6.from_before, ...), custom_call_target="tpu_custom_call" | custom-call | tf_op jit(solution)/shard_map/place/pallas_call | solution.py:329
Async XLA Ops:
  0.0 6.9 %collective-permute-start.1 = (s32[1,2]{1,0:T(1,128)}, s32[1,2]{1,0:T(1,128)S(1)}, u32[]{:S(2)}, u32[]{:S(2)}) collective-permute-start(s32[1,2]{1,0:T(1,128)} %position.5), channel_id=1, source_target_pairs={{0,30},{2,0},{4,2},{6,4},{8,6},{10,8},{12,10},{14,12},{16,14},{18,... | collective-permute-start | bytes 32 | tf_op jit(solution)/shard_map/ppermute | solution.py:288
  5.4 5.8 %collective-permute-start = (s32[1,2]{1,0:T(1,128)}, s32[1,2]{1,0:T(1,128)S(1)}, u32[]{:S(2)}, u32[]{:S(2)}) collective-permute-start(s32[1,2]{1,0:T(1,128)} %position.5), channel_id=1, source_target_pairs={{0,2},{2,4},{4,6},{6,8},{8,10},{10,12},{12,14},{14,16},{16,18},{18... | collective-permute-start | bytes 32 | tf_op jit(solution)/shard_map/ppermute | solution.py:287
  11.3 1.2 %copy-start = (f32[2,128,1024]{2,1,0:T(8,128)S(1)}, f32[2,128,1024]{2,1,0:T(8,128)}, u32[]{:S(2)}) copy-start(f32[2,128,1024]{2,1,0:T(8,128)} %refs_2_.1) | copy-start | bytes 3145732
  12.5 4.7 %copy-start.1 = (f32[2,128,1024]{2,1,0:T(8,128)S(1)}, f32[2,128,1024]{2,1,0:T(8,128)}, u32[]{:S(2)}) copy-start(f32[2,128,1024]{2,1,0:T(8,128)} %refs_2_.1) | copy-start | bytes 3145732
  12.7 4.5 %copy-start.6 = (s32[1,2]{1,0:T(1,128)S(1)}, s32[1,2]{1,0:T(1,128)}, u32[]{:S(2)}) copy-start(s32[1,2]{1,0:T(1,128)} %position.5) | copy-start | bytes 28
  12.7 8.5 %collective-permute-start.2 = (f32[2,128,256]{2,1,0:T(8,128)S(1)}, f32[2,128,256]{2,1,0:T(8,128)S(1)}, u32[]{:S(2)}, u32[]{:S(2)}) collective-permute-start(f32[2,128,256]{2,1,0:T(8,128)S(1)} %get-tuple-element.12), channel_id=1, source_target_pairs={{0,2},{2,4},{4,6},{6,8},{8,10},{10,12},{12,14},{14,16},{16,18},{18... | collective-permute-start | bytes 786440 | tf_op jit(solution)/shard_map/ppermute | solution.py:300
  12.8 8.5 %collective-permute-start.3 = (f32[2,128,256]{2,1,0:T(8,128)S(1)}, f32[2,128,256]{2,1,0:T(8,128)S(1)}, u32[]{:S(2)}, u32[]{:S(2)}) collective-permute-start(f32[2,128,256]{2,1,0:T(8,128)S(1)} %get-tuple-element.13), channel_id=1, source_target_pairs={{0,30},{2,0},{4,2},{6,4},{8,6},{10,8},{12,10},{14,12},{16,14},{18,... | collective-permute-start | bytes 786440 | tf_op jit(solution)/shard_map/ppermute | solution.py:301
  17.4 7.2 %collective-permute-start.4 = (f32[2,128,256]{2,1,0:T(8,128)S(1)}, f32[2,128,256]{2,1,0:T(8,128)S(1)}, u32[]{:S(2)}, u32[]{:S(2)}) collective-permute-start(f32[2,128,256]{2,1,0:T(8,128)S(1)} %cut.2.refs_0_), channel_id=1, source_target_pairs={{0,1},{1,0},{2,3},{3,2},{4,5},{5,4},{6,7},{7,6},{8,9},{9,8},{10,11... | collective-permute-start | bytes 786440 | tf_op jit(solution)/shard_map/ppermute | solution.py:294
  21.4 7.2 %collective-permute-start.5 = (f32[2,128,256]{2,1,0:T(8,128)S(1)}, f32[2,128,256]{2,1,0:T(8,128)S(1)}, u32[]{:S(2)}, u32[]{:S(2)}) collective-permute-start(f32[2,128,256]{2,1,0:T(8,128)S(1)} %merge.1.other), channel_id=1, source_target_pairs={{0,1},{1,0},{2,3},{3,2},{4,5},{5,4},{6,7},{7,6},{8,9},{9,8},{10,11... | collective-permute-start | bytes 786440 | tf_op jit(solution)/shard_map/ppermute | solution.py:294
  23.0 1.9 %copy-start.2 = (bf16[6,256,256]{2,1,0:T(8,128)(2,1)S(1)}, bf16[6,256,256]{2,1,0:T(8,128)(2,1)}, u32[]{:S(2)}) copy-start(bf16[6,256,256]{2,1,0:T(8,128)(2,1)} %constant.8.clone.prop) | copy-start | bytes 2359300
  23.3 1.6 %copy-start.4 = (f32[2,256,256]{2,1,0:T(8,128)S(1)}, f32[2,256,256]{2,1,0:T(8,128)}, u32[]{:S(2)}) copy-start(f32[2,256,256]{2,1,0:T(8,128)} %probe.1) | copy-start | bytes 1572868
  24.9 3.7 %copy-start.3 = (bf16[6,256,256]{2,1,0:T(8,128)(2,1)S(1)}, bf16[6,256,256]{2,1,0:T(8,128)(2,1)}, u32[]{:S(2)}) copy-start(bf16[6,256,256]{2,1,0:T(8,128)(2,1)} %constant.9.clone.dft) | copy-start | bytes 2359300
  24.9 3.7 %copy-start.5 = (f32[1,256,256]{2,1,0:T(8,128)S(1)}, f32[1,256,256]{2,1,0:T(8,128)}, u32[]{:S(2)}) copy-start(f32[1,256,256]{2,1,0:T(8,128)} %intensity.1) | copy-start | bytes 786436
  36.1 7.5 %collective-permute-start.7 = (f32[2,128,256]{2,1,0:T(8,128)S(1)}, f32[2,128,256]{2,1,0:T(8,128)S(1)}, u32[]{:S(2)}, u32[]{:S(2)}) collective-permute-start(f32[2,128,256]{2,1,0:T(8,128)S(1)} %get-tuple-element.18), channel_id=1, source_target_pairs={{0,30},{2,0},{4,2},{6,4},{8,6},{10,8},{12,10},{14,12},{16,14},{18,... | collective-permute-start | bytes 786440 | tf_op jit(solution)/shard_map/ppermute | solution.py:326
  39.7 8.5 %collective-permute-start.6 = (f32[2,128,256]{2,1,0:T(8,128)S(1)}, f32[2,128,256]{2,1,0:T(8,128)S(1)}, u32[]{:S(2)}, u32[]{:S(2)}) collective-permute-start(f32[2,128,256]{2,1,0:T(8,128)S(1)} %get-tuple-element.18), channel_id=1, source_target_pairs={{0,2},{2,4},{4,6},{6,8},{8,10},{10,12},{12,14},{14,16},{16,18},{18... | collective-permute-start | bytes 786440 | tf_op jit(solution)/shard_map/ppermute | solution.py:325

commit v2 on v1

v2 whole, which is shorter than its diff:
```python
import functools

import jax
import jax.numpy as jnp
import numpy as np
from jax import lax
from jax.experimental import pallas as pl
from jax.experimental.pallas import tpu as pltpu
from jax.sharding import PartitionSpec as P

interaction = 0.5
fresnel_phase = 60.0
f32 = jnp.float32
bf16 = jnp.bfloat16

VMEM = pl.BlockSpec(memory_space=pltpu.VMEM)
SMEM = pl.BlockSpec(memory_space=pltpu.SMEM)
ANY = pl.BlockSpec(memory_space=pl.ANY)


def poly_tables():
    x = np.cos(np.linspace(0.0, np.pi / 2, 4001)) * (np.pi / 2) * 1.0005
    z = x * x
    fit = np.polynomial.chebyshev.Chebyshev.fit
    kind = np.polynomial.Polynomial
    sine = fit(z, np.sinc(x / np.pi), 5).convert(kind=kind).coef
    cosine = fit(z, np.cos(x), 5).convert(kind=kind).coef
    return [float(v) for v in sine], [float(v) for v in cosine]


def split_table(matrix):
    parts = []
    for real in (matrix.real, matrix.imag, -matrix.imag):
        wide = real.astype(np.float32)
        high = wide.astype(bf16)
        parts.append(high)
        parts.append((real - high.astype(np.float64)).astype(np.float32).astype(bf16))
    return np.stack(parts)


def tables(extent):
    index = np.arange(extent)
    dft = np.exp(-2j * np.pi * ((index[:, None] * index[None, :]) % extent) / extent)
    dft = dft / np.sqrt(extent)
    frequency = ((index + extent // 2) % extent - extent // 2) / extent
    chirp = np.exp(-1j * fresnel_phase * frequency**2)
    propagator = np.conj(dft) @ (chirp[:, None] * dft)
    return split_table(propagator), split_table(dft)


def sin_cos(window):
    sine, cosine = poly_tables()
    half = window * (interaction / 2)
    turns = jnp.round(half * (1.0 / np.pi))
    pi_high = float(np.float32(3.140625))
    pi_low = float(np.pi - 3.140625)
    x = (half - turns * pi_high) - turns * pi_low
    z = x * x
    s = sine[5]
    c = cosine[5]
    for k in range(4, -1, -1):
        s = s * z + sine[k]
        c = c * z + cosine[k]
    s = s * x
    return 2.0 * s * c, 1.0 - 2.0 * (s * s)


def parts_of(x):
    high = x.astype(bf16)
    return high, (x - high.astype(f32)).astype(bf16)


def dot(a, b):
    return jnp.dot(a, b, preferred_element_type=f32)


def sandwich(m, real, imag):
    m = [m[k] for k in range(6)]
    rows = jnp.concatenate
    rh, rl = parts_of(real)
    ih, il = parts_of(imag)
    left = rows([rh, rl, rh, ih, il, ih], axis=1)
    yr = dot(left, rows([m[0], m[0], m[1], m[4], m[4], m[5]], axis=0))
    yi = dot(left, rows([m[2], m[2], m[3], m[0], m[0], m[1]], axis=0))
    rh, rl = parts_of(yr)
    ih, il = parts_of(yi)
    right = rows([rh, rl, rh, ih, il, ih], axis=0)
    zr = dot(rows([m[0], m[0], m[1], m[4], m[4], m[5]], axis=1), right)
    zi = dot(rows([m[2], m[2], m[3], m[0], m[0], m[1]], axis=1), right)
    return zr, zi


def call(kernel, name, results, scalars, arrays, aliases=(), scratch=(), limit=16):
    arrays = [pltpu.with_memory_space_constraint(x, pltpu.VMEM) for x in arrays]
    return pl.pallas_call(
        kernel,
        out_shape=[pltpu.VMEM(shape, f32) for shape in results],
        in_specs=[SMEM] * len(scalars) + [VMEM] * len(arrays),
        out_specs=[VMEM] * len(results),
        input_output_aliases={len(scalars) + i: o for i, o in aliases},
        scratch_shapes=list(scratch),
        compiler_params=pltpu.CompilerParams(vmem_limit_bytes=limit * 2**20),
        name=name,
    )(*scalars, *arrays)


def entry(position, k):
    return position[0:1, k : k + 1]


def covered(column, block, shape):
    lane = lax.broadcasted_iota(jnp.int32, shape, 1) + block * shape[1]
    return (lane >= column) & (lane < column + shape[1])


def fold_columns(potential, position, out):
    layers, strip, columns = potential.shape
    extent = 2 * strip
    column = entry(position, 1)
    for layer in range(layers):
        value = potential[layer, :, :extent]
        for block in range(1, columns // extent):
            mask = covered(column, block, value.shape)
            next_value = potential[layer, :, block * extent : (block + 1) * extent]
            value = jnp.where(mask, next_value, value)
        out[layer] = value


def own_kernel(position, potential, tile, own, sem):
    copy = pltpu.make_async_copy(potential, tile, sem)
    copy.start()
    copy.wait()
    fold_columns(tile, position, own)


def cut_kernel(fast, slow, tile, for_fast, for_slow):
    fold_columns(tile, slow, for_slow)
    fold_columns(tile, fast, for_fast)


def fill(table, owner, piece, rows):
    layers = piece.shape[0]
    for layer in range(layers):
        s, c = sin_cos(piece[layer])
        table[owner * layers + layer, 0, rows] = c
        table[owner * layers + layer, 1, rows] = s


def first_kernel(place, position, own, probe, table, wave):
    strip = own.shape[1]
    row_shift = position[0, 0] % strip + strip
    column_shift = position[0, 1] % (2 * strip)
    for k in range(2):
        wave[k] = pltpu.roll(pltpu.roll(probe[k], row_shift, 0), column_shift, 1)
    fill(table, place[0], own, slice(0, strip))


def second_kernel(count, place, *refs):
    owns, table = refs[: count - 1], refs[-1]
    strip = owns[0].shape[1]
    for k in range(1, count):
        fill(table, (place[0] - k + count) % count, owns[k - 1], slice(0, strip))


def merge_kernel(parity, position, fast, slow, _, out):
    layers, strip, extent = out.shape
    row = lax.broadcasted_iota(jnp.int32, (strip, extent), 0)
    above = (row >= entry(position, 0) % strip).astype(jnp.int32)
    mask = above != parity[0]
    for layer in range(layers):
        out[layer] = jnp.where(mask, slow[layer], fast[layer])


def transmit(trans, real, imag):
    c, s = trans
    return c * real - s * imag, c * imag + s * real


def enter_kernel(place, wave_in, other, prop, table_in, wave_out, table, saved):
    layers, strip, _ = other.shape
    fill(table, place[0], other, slice(strip, 2 * strip))

    def forward(layer, wave):
        wave = transmit((table[layer, 0], table[layer, 1]), *wave)
        saved[layer, 0] = wave[0]
        saved[layer, 1] = wave[1]
        return sandwich(prop, *wave)

    @pl.when(place[0] == 0)
    def _():
        wave = lax.fori_loop(0, layers, forward, (wave_in[0], wave_in[1]))
        wave_out[0] = wave[0]
        wave_out[1] = wave[1]


def solve_kernel(count, place, wave_in, saved_in, intensity, prop, dft, table_in, *refs):
    others = refs[: count - 1]
    mine, outer, table, saved = refs[count - 1 :]
    layers, strip, extent = mine.shape
    slices = layers * count
    last = slices - 1
    depth = place[0]
    first = depth * layers
    for k in range(1, count):
        fill(table, (depth - k + count) % count, others[k - 1], slice(strip, extent))

    def enter(s, wave):
        wave = transmit((table[s, 0], table[s, 1]), *wave)

        @pl.when((s >= first) & (s < first + layers))
        def _():
            saved[s - first, 0] = wave[0]
            saved[s - first, 1] = wave[1]

        return wave

    wave = (wave_in[0], wave_in[1])
    start = jnp.where(depth == 0, layers, 0)
    wave = lax.fori_loop(start, last, lambda s, w: sandwich(prop, *enter(s, w)), wave)
    far_real, far_imag = sandwich(dft, *enter(last, wave))
    misfit = far_real * far_real + far_imag * far_imag - intensity[0]
    wave = sandwich(dft, misfit * far_real, -(misfit * far_imag))

    def term(s, wave):
        @pl.when(s < first + layers)
        def _():
            value = wave[1] * saved[s - first, 0] + wave[0] * saved[s - first, 1]
            value = -interaction * value
            mine[s - first] = value[:strip]
            outer[s - first] = value[strip:]

    term(last, wave)

    def backward(step, wave):
        s = last - step
        wave = sandwich(prop, *transmit((table[s, 0], table[s, 1]), *wave))
        term(s - 1, wave)
        return wave

    lax.fori_loop(0, last - first, backward, wave)


def covers(position, block, shape, odd):
    strip = shape[0]
    row = lax.broadcasted_iota(jnp.int32, shape, 0)
    rows = (row >= entry(position, 0) % strip).astype(jnp.int32) != odd
    return covered(entry(position, 1), block, shape) & rows


def stage_kernel(parity, position, fast_position, mine, fast, staged):
    layers, strip, columns = staged.shape
    extent = 2 * strip
    shape = (strip, extent)
    for block in range(columns // extent):
        at = slice(block * extent, (block + 1) * extent)
        own = covered(entry(position, 1), block, shape)
        near = covers(fast_position, block, shape, parity[0])
        for layer in range(layers):
            value = jnp.where(own, mine[layer], 0.0) + jnp.where(near, fast[layer], 0.0)
            staged[layer, :, at] = value


def place_kernel(parity, slow_position, slow, staged, out, final, sems):
    layers, strip, columns = out.shape
    extent = 2 * strip
    copies = []
    for block in range(columns // extent):
        at = slice(block * extent, (block + 1) * extent)
        far = covers(slow_position, block, (strip, extent), 1 - parity[0])
        for layer in range(layers):
            value = staged[layer, :, at] + jnp.where(far, slow[layer], 0.0)
            final[layer, :, at] = value
        copy = pltpu.make_async_copy(final.at[:, :, at], out.at[:, :, at], sems.at[block])
        copy.start()
        copies.append(copy)
    for copy in copies:
        copy.wait()


def local(potential, probe, positions, intensity):
    layers, strip, columns = potential.shape
    extent = probe.shape[1]
    count = lax.axis_size("probe")
    depth_count = lax.axis_size("depth")
    assert positions.shape[0] == 1 and extent == 2 * strip and columns % extent == 0
    assert count % 2 == 0
    slices = layers * depth_count
    half = (layers, strip, extent)
    field = (2, extent, extent)
    fast_pairs = [(i, i ^ 1) for i in range(count)]
    slow_pairs = [(i, (i + 1 if i % 2 else i - 1) % count) for i in range(count)]

    def swapped(fast, slow):
        slow = lax.ppermute(slow, "probe", slow_pairs)
        return lax.ppermute(fast, "probe", fast_pairs), slow

    def from_depths(x):
        out = []
        for k in range(1, depth_count):
            pairs = [(i, (i + k) % depth_count) for i in range(depth_count)]
            out.append(lax.ppermute(x, "depth", pairs))
        return out

    place = lax.axis_index("depth").astype(jnp.int32).reshape(1)
    parity = (lax.axis_index("probe").astype(jnp.int32) % 2).reshape(1)
    prop, dft = [jnp.asarray(x) for x in tables(extent)]

    fast_position, slow_position = swapped(positions, positions)
    tile, own = pl.pallas_call(
        own_kernel,
        out_shape=[pltpu.VMEM(potential.shape, f32), pltpu.VMEM(half, f32)],
        in_specs=[VMEM, ANY],
        out_specs=[VMEM] * 2,
        scratch_shapes=[pltpu.SemaphoreType.DMA],
        name="own",
    )(positions, potential)
    owns = from_depths(own)
    pieces = call(cut_kernel, "cut", [half] * 2, [], [fast_position, slow_position, tile])
    fast, slow = swapped(*pieces)
    table, wave = call(
        first_kernel, "first", [(slices, *field), field], [place, positions], [own, probe]
    )
    (table,) = call(
        functools.partial(second_kernel, depth_count),
        "second",
        [table.shape],
        [place],
        [*owns, table],
        aliases=[(depth_count - 1, 0)],
    )
    (other,) = call(merge_kernel, "merge", [half], [parity], [positions, fast, slow, table])
    others = from_depths(other)
    wave, table, saved = call(
        enter_kernel,
        "enter",
        [field, table.shape, (layers, *field)],
        [place],
        [wave, other, prop, table],
        aliases=[(0, 0), (3, 1)],
    )
    mine, outer, _, _ = call(
        functools.partial(solve_kernel, depth_count),
        "solve",
        [half, half, table.shape, saved.shape],
        [place],
        [wave, saved, intensity, prop, dft, table, *others],
        aliases=[(5, 2), (1, 3)],
    )
    fast, slow = swapped(outer, outer)
    (staged,) = call(
        stage_kernel, "stage", [potential.shape], [parity], [positions, fast_position, mine, fast]
    )
    arrays = [slow_position, slow, staged]
    arrays = [pltpu.with_memory_space_constraint(x, pltpu.VMEM) for x in arrays]
    return pl.pallas_call(
        place_kernel,
        out_shape=jax.ShapeDtypeStruct(potential.shape, f32),
        in_specs=[SMEM] + [VMEM] * 3,
        out_specs=ANY,
        scratch_shapes=[
            pltpu.VMEM(potential.shape, f32),
            pltpu.SemaphoreType.DMA((columns // extent,)),
        ],
        name="place",
    )(parity, *arrays)


def solution(mesh):
    in_specs = (P("depth", "probe", None), P(), P("probe", None), P("probe", None, None))
    out_specs = P("depth", "probe", None)
    return jax.shard_map(local, mesh=mesh, in_specs=in_specs, out_specs=out_specs, check_vma=False)
```

time: 49.7 us -> 45.4 us (0.913)
  starting transfers between devices: 16.8 us -> 11 us
  Pallas kernels: 13.4 us -> 15.8 us
  local copies, waits for them, and re-layouts: 1.26 us -> 0.03 us
    ppermute x2, waiting for transfers between devices: 1.31 us -> 6.51 us  [from_depths(): out.append(lax.ppermute(x, 'depth', pairs))]
    ppermute x6, waiting for transfers between devices: 16.6 us -> 11.7 us  [the longest x3 10.6 us: swapped(): slow = lax.ppermute(slow, 'probe', slow_pairs)]
    ppermute x6, starting transfers between devices: 13.6 us -> 8.87 us  [the longest x3 8.23 us: swapped(): slow = lax.ppermute(slow, 'probe', slow_pairs)]
    pallas_call x0 -> x1, Pallas kernels: none -> 2.05 us  [local(): pl.pallas_call(own_kernel, out_shape=[pltpu.VMEM(potential.shape, f32), p...]
    unnamed x14 -> x10, local copies, waits for them, and re-layouts: 1.26 us -> 0.03 us
    ppermute x2, starting transfers between devices: 3.17 us -> 2.16 us  [from_depths(): out.append(lax.ppermute(x, 'depth', pairs))]
  transfers between devices with their start and end apart: 8 -> 8, of which waited for: 6 -> 5; matrix products, arithmetic and copies ran while one was open for 0% -> 0% of each run, Pallas kernels for 9% -> 15%
where the time goes in v2:
time: 45.4 us; the launch traced here: 45.2 us
  waiting for transfers between devices  18.3 us (40%)
  Pallas kernels  15.8 us (35%)
  starting transfers between devices  11 us (24%)
    pallas_call x7, Pallas kernels, call(): pl.pallas_call(kernel, out_shape=[pltpu.VMEM(shape, f32) for shape in res...  12.6 us
    ppermute x3, waiting for transfers between devices, swapped(): slow = lax.ppermute(slow, 'probe', slow_pairs)  10.6 us
    ppermute x3, starting transfers between devices, swapped(): slow = lax.ppermute(slow, 'probe', slow_pairs)  8.23 us
    ppermute x2, waiting for transfers between devices, from_depths(): out.append(lax.ppermute(x, 'depth', pairs))  6.51 us
    ppermute x2, starting transfers between devices, from_depths(): out.append(lax.ppermute(x, 'depth', pairs))  2.16 us
    pallas_call x1, Pallas kernels, local(): pl.pallas_call(own_kernel, out_shape=[pltpu.VMEM(potential.shape, f32), p...  2.05 us
    ppermute x3, waiting for transfers between devices, swapped(): return (lax.ppermute(fast, 'probe', fast_pairs), slow)  1.16 us
    pallas_call x1, Pallas kernels, local(): pl.pallas_call(place_kernel, out_shape=jax.ShapeDtypeStruct(potential.sha...  1.15 us
  transfers between devices with their start and end apart: 8, of which 5 were waited for; matrix products, arithmetic and copies ran while one was open for 0% of the time, Pallas kernels for 15%

profile of v2, /device:TPU:0, one launch (start us, length us, event | category | flops | bytes accessed | tf_op | source)
XLA Modules:
  0.0 45.2 jit_solution(12381101102106225535)
XLA Ops:
  0.0 0.0 copy-start.4
  0.0 0.0 copy-start.2
  0.0 0.5 %collective-permute-start.1 = (s32[1,2]{1,0:T(1,128)}, s32[1,2]{1,0:T(1,128)S(1)}, u32[]{:S(2)}, u32[]{:S(2)}) collective-permute-start(s32[1,2]{1,0:T(1,128)} %position.7), channel_id=1, source_target_pairs={{0,2},{2,0},{4,6},{6,4},{8,10},{10,8},{12,14},{14,12},{16,18},{18,... | collective-permute-start | bytes 32 | tf_op jit(solution)/shard_map/ppermute | solution.py:295
  0.5 5.6 %collective-permute-start = (s32[1,2]{1,0:T(1,128)}, s32[1,2]{1,0:T(1,128)S(1)}, u32[]{:S(2)}, u32[]{:S(2)}) collective-permute-start(s32[1,2]{1,0:T(1,128)} %position.7), channel_id=1, source_target_pairs={{0,30},{2,4},{4,2},{6,8},{8,6},{10,12},{12,10},{14,16},{16,14},{18... | collective-permute-start | bytes 32 | tf_op jit(solution)/shard_map/ppermute | solution.py:294
  6.1 2.1 %own.1 = (f32[2,128,1024]{2,1,0:T(8,128)S(1)}, f32[2,128,256]{2,1,0:T(8,128)S(1)}) custom-call(s32[1,2]{1,0:T(1,128)} %position.7, f32[2,128,1024]{2,1,0:T(8,128)} %potential.1), custom_call_target="tpu_custom_call" | custom-call | tf_op jit(solution)/shard_map/own/pallas_call | solution.py:309
  8.2 1.6 %collective-permute-start.4 = (f32[2,128,256]{2,1,0:T(8,128)S(1)}, f32[2,128,256]{2,1,0:T(8,128)S(1)}, u32[]{:S(2)}, u32[]{:S(2)}) collective-permute-start(f32[2,128,256]{2,1,0:T(8,128)S(1)} %get-tuple-element.16.own), channel_id=1, source_target_pairs={{0,1},{1,0},{2,3},{3,2},{4,5},{5,4},{6,7},{7,6},{8,9},{9,8},{10,11... | collective-permute-start | bytes 786440 | tf_op jit(solution)/shard_map/ppermute | solution.py:301
  9.8 0.0 collective-permute-done.1.fast.fast_position
  9.8 0.0 collective-permute-done.slow.slow_position
  9.8 0.2 cut.1
  10.0 0.1 collective-permute-start.2
  10.1 2.2 %collective-permute-start.3 = (f32[2,128,256]{2,1,0:T(8,128)S(1)}, f32[2,128,256]{2,1,0:T(8,128)S(1)}, u32[]{:S(2)}, u32[]{:S(2)}) collective-permute-start(f32[2,128,256]{2,1,0:T(8,128)S(1)} %get-tuple-element.20), channel_id=1, source_target_pairs={{0,30},{2,4},{4,2},{6,8},{8,6},{10,12},{12,10},{14,16},{16,14},{18... | collective-permute-start | bytes 786440 | tf_op jit(solution)/shard_map/ppermute | solution.py:294
  12.3 0.0 copy-done.4
  12.3 0.0 copy-done.2
  12.3 1.1 %first.1 = (f32[4,2,256,256]{3,2,1,0:T(8,128)S(1)}, f32[2,256,256]{2,1,0:T(8,128)S(1)}) custom-call(s32[1]{0:T(128)} %bitcast.1.place, s32[1,2]{1,0:T(1,128)S(1)} %copy-done.4, f32[2,128,256]{2,1,0:T(8,128)S(1)} %get-tuple-element.16.own, f32[2,256,256]{2,1,0:T(8,128)S(1)} %copy-done.2), custom_call_target="tpu_custom_call" | custom-call | tf_op jit(solution)/shard_map/first/pallas_call | solution.py:95
  13.4 1.2 %collective-permute-done.4.refs_0_ = f32[2,128,256]{2,1,0:T(8,128)S(1)} collective-permute-done((f32[2,128,256]{2,1,0:T(8,128)S(1)}, f32[2,128,256]{2,1,0:T(8,128)S(1)}, u32[]{:S(2)}, u32[]{:S(2)}) %collective-permute-start.4) | collective-permute-done | bytes 262176 | tf_op jit(solution)/shard_map/ppermute | solution.py:301
  14.6 0.3 second.1._.table_in
  14.9 0.0 copy-start
  14.9 0.0 collective-permute-done.2.fast
  14.9 3.8 %collective-permute-done.3.slow = f32[2,128,256]{2,1,0:T(8,128)S(1)} collective-permute-done((f32[2,128,256]{2,1,0:T(8,128)S(1)}, f32[2,128,256]{2,1,0:T(8,128)S(1)}, u32[]{:S(2)}, u32[]{:S(2)}) %collective-permute-start.3) | collective-permute-done | bytes 262176 | tf_op jit(solution)/shard_map/ppermute | solution.py:294
  18.7 0.1 merge.1.other
  18.8 0.0 copy-start.1
  18.9 0.0 copy-start.3
  18.9 0.6 %collective-permute-start.5 = (f32[2,128,256]{2,1,0:T(8,128)S(1)}, f32[2,128,256]{2,1,0:T(8,128)S(1)}, u32[]{:S(2)}, u32[]{:S(2)}) collective-permute-start(f32[2,128,256]{2,1,0:T(8,128)S(1)} %merge.1.other), channel_id=1, source_target_pairs={{0,1},{1,0},{2,3},{3,2},{4,5},{5,4},{6,7},{7,6},{8,9},{9,8},{10,11... | collective-permute-start | bytes 786440 | tf_op jit(solution)/shard_map/ppermute | solution.py:301
  19.4 0.0 copy-done
  19.4 2.8 %enter.1 = (f32[2,256,256]{2,1,0:T(8,128)S(1)}, f32[4,2,256,256]{3,2,1,0:T(8,128)S(1)}, f32[2,2,256,256]{3,2,1,0:T(8,128)S(1)}) custom-call(s32[1]{0:T(128)} %bitcast.1.place, f32[2,256,256]{2,1,0:T(8,128)S(1)} %get-tuple-element.17.wave_in, f32[2,128,256]{2,1,0:T(8,128)S(1)} %merge.1.other, ...), custom_call_target="tpu_custom_call", output_to_operand_aliasing={{0}: (1, {}), {1}: (4, {})} | custom-call | tf_op jit(solution)/shard_map/enter/pallas_call | solution.py:95
  22.3 5.3 %collective-permute-done.5.refs_0_ = f32[2,128,256]{2,1,0:T(8,128)S(1)} collective-permute-done((f32[2,128,256]{2,1,0:T(8,128)S(1)}, f32[2,128,256]{2,1,0:T(8,128)S(1)}, u32[]{:S(2)}, u32[]{:S(2)}) %collective-permute-start.5) | collective-permute-done | bytes 262176 | tf_op jit(solution)/shard_map/ppermute | solution.py:301
  27.6 0.0 copy-done.1
  27.6 0.0 copy-done.3
  27.6 7.7 %solve.1 = (f32[2,128,256]{2,1,0:T(8,128)S(1)}, f32[2,128,256]{2,1,0:T(8,128)S(1)}, f32[4,2,256,256]{3,2,1,0:T(8,128)S(1)}, f32[2,2,256,256]{3,2,1,0:T(8,128)S(1)}) custom-call(s32[1]{0:T(128)} %bitcast.1.place, f32[2,256,256]{2,1,0:T(8,128)S(1)} %get-tuple-element.22.wave_in, ...), custom_call_target="tpu_custom_call", output_to_operand_aliasing={{2}: (6, {}), {3}: (2, {})} | custom-call | tf_op jit(solution)/shard_map/solve/pallas_call | solution.py:95
  35.3 0.1 collective-permute-start.7
  35.4 0.4 collective-permute-start.6
  35.8 1.2 %collective-permute-done.7.fast = f32[2,128,256]{2,1,0:T(8,128)S(1)} collective-permute-done((f32[2,128,256]{2,1,0:T(8,128)S(1)}, f32[2,128,256]{2,1,0:T(8,128)S(1)}, u32[]{:S(2)}, u32[]{:S(2)}) %collective-permute-start.7) | collective-permute-done | bytes 262176 | tf_op jit(solution)/shard_map/ppermute | solution.py:295
  36.9 0.3 stage.1.staged
  37.3 6.8 %collective-permute-done.6.slow = f32[2,128,256]{2,1,0:T(8,128)S(1)} collective-permute-done((f32[2,128,256]{2,1,0:T(8,128)S(1)}, f32[2,128,256]{2,1,0:T(8,128)S(1)}, u32[]{:S(2)}, u32[]{:S(2)}) %collective-permute-start.6) | collective-permute-done | bytes 262176 | tf_op jit(solution)/shard_map/ppermute | solution.py:294
  44.1 1.1 %place.1 = f32[2,128,1024]{2,1,0:T(8,128)} custom-call(s32[1]{0:T(128)} %bitcast.parity, s32[1,2]{1,0:T(1,128)S(1)} %collective-permute-done.slow.slow_position, f32[2,128,256]{2,1,0:T(8,128)S(1)} %collective-permute-done.6.slow, f32[2,128,1024]{2,1,0:T(8,128)S(1)} %stage.1.staged), custom_call_target="tpu_custom_call" | custom-call | tf_op jit(solution)/shard_map/place/pallas_call | solution.py:355
Async XLA Ops:
  0.0 12.3 %copy-start.4 = (s32[1,2]{1,0:T(1,128)S(1)}, s32[1,2]{1,0:T(1,128)}, u32[]{:S(2)}) copy-start(s32[1,2]{1,0:T(1,128)} %position.7) | copy-start | bytes 28
  0.0 12.3 %copy-start.2 = (f32[2,256,256]{2,1,0:T(8,128)S(1)}, f32[2,256,256]{2,1,0:T(8,128)}, u32[]{:S(2)}) copy-start(f32[2,256,256]{2,1,0:T(8,128)} %probe.1) | copy-start | bytes 1572868
  0.0 9.8 %collective-permute-start.1 = (s32[1,2]{1,0:T(1,128)}, s32[1,2]{1,0:T(1,128)S(1)}, u32[]{:S(2)}, u32[]{:S(2)}) collective-permute-start(s32[1,2]{1,0:T(1,128)} %position.7), channel_id=1, source_target_pairs={{0,2},{2,0},{4,6},{6,4},{8,10},{10,8},{12,14},{14,12},{16,18},{18,... | collective-permute-start | bytes 32 | tf_op jit(solution)/shard_map/ppermute | solution.py:295
  0.5 9.3 %collective-permute-start = (s32[1,2]{1,0:T(1,128)}, s32[1,2]{1,0:T(1,128)S(1)}, u32[]{:S(2)}, u32[]{:S(2)}) collective-permute-start(s32[1,2]{1,0:T(1,128)} %position.7), channel_id=1, source_target_pairs={{0,30},{2,4},{4,2},{6,8},{8,6},{10,12},{12,10},{14,16},{16,14},{18... | collective-permute-start | bytes 32 | tf_op jit(solution)/shard_map/ppermute | solution.py:294
  8.2 6.4 %collective-permute-start.4 = (f32[2,128,256]{2,1,0:T(8,128)S(1)}, f32[2,128,256]{2,1,0:T(8,128)S(1)}, u32[]{:S(2)}, u32[]{:S(2)}) collective-permute-start(f32[2,128,256]{2,1,0:T(8,128)S(1)} %get-tuple-element.16.own), channel_id=1, source_target_pairs={{0,1},{1,0},{2,3},{3,2},{4,5},{5,4},{6,7},{7,6},{8,9},{9,8},{10,11... | collective-permute-start | bytes 786440 | tf_op jit(solution)/shard_map/ppermute | solution.py:301
  10.0 4.9 %collective-permute-start.2 = (f32[2,128,256]{2,1,0:T(8,128)S(1)}, f32[2,128,256]{2,1,0:T(8,128)S(1)}, u32[]{:S(2)}, u32[]{:S(2)}) collective-permute-start(f32[2,128,256]{2,1,0:T(8,128)S(1)} %get-tuple-element.19), channel_id=1, source_target_pairs={{0,2},{2,0},{4,6},{6,4},{8,10},{10,8},{12,14},{14,12},{16,18},{18,... | collective-permute-start | bytes 786440 | tf_op jit(solution)/shard_map/ppermute | solution.py:295
  10.1 8.7 %collective-permute-start.3 = (f32[2,128,256]{2,1,0:T(8,128)S(1)}, f32[2,128,256]{2,1,0:T(8,128)S(1)}, u32[]{:S(2)}, u32[]{:S(2)}) collective-permute-start(f32[2,128,256]{2,1,0:T(8,128)S(1)} %get-tuple-element.20), channel_id=1, source_target_pairs={{0,30},{2,4},{4,2},{6,8},{8,6},{10,12},{12,10},{14,16},{16,14},{18... | collective-permute-start | bytes 786440 | tf_op jit(solution)/shard_map/ppermute | solution.py:294
  14.9 4.5 %copy-start = (bf16[6,256,256]{2,1,0:T(8,128)(2,1)S(1)}, bf16[6,256,256]{2,1,0:T(8,128)(2,1)}, u32[]{:S(2)}) copy-start(bf16[6,256,256]{2,1,0:T(8,128)(2,1)} %constant.25.clone.prop) | copy-start | bytes 2359300
  18.8 8.7 %copy-start.1 = (bf16[6,256,256]{2,1,0:T(8,128)(2,1)S(1)}, bf16[6,256,256]{2,1,0:T(8,128)(2,1)}, u32[]{:S(2)}) copy-start(bf16[6,256,256]{2,1,0:T(8,128)(2,1)} %constant.26.clone.dft) | copy-start | bytes 2359300
  18.9 8.7 %copy-start.3 = (f32[1,256,256]{2,1,0:T(8,128)S(1)}, f32[1,256,256]{2,1,0:T(8,128)}, u32[]{:S(2)}) copy-start(f32[1,256,256]{2,1,0:T(8,128)} %intensity.1) | copy-start | bytes 786436
  18.9 8.7 %collective-permute-start.5 = (f32[2,128,256]{2,1,0:T(8,128)S(1)}, f32[2,128,256]{2,1,0:T(8,128)S(1)}, u32[]{:S(2)}, u32[]{:S(2)}) collective-permute-start(f32[2,128,256]{2,1,0:T(8,128)S(1)} %merge.1.other), channel_id=1, source_target_pairs={{0,1},{1,0},{2,3},{3,2},{4,5},{5,4},{6,7},{7,6},{8,9},{9,8},{10,11... | collective-permute-start | bytes 786440 | tf_op jit(solution)/shard_map/ppermute | solution.py:301
  35.3 1.6 %collective-permute-start.7 = (f32[2,128,256]{2,1,0:T(8,128)S(1)}, f32[2,128,256]{2,1,0:T(8,128)S(1)}, u32[]{:S(2)}, u32[]{:S(2)}) collective-permute-start(f32[2,128,256]{2,1,0:T(8,128)S(1)} %get-tuple-element.25), channel_id=1, source_target_pairs={{0,2},{2,0},{4,6},{6,4},{8,10},{10,8},{12,14},{14,12},{16,18},{18,... | collective-permute-start | bytes 786440 | tf_op jit(solution)/shard_map/ppermute | solution.py:295
  35.4 8.7 %collective-permute-start.6 = (f32[2,128,256]{2,1,0:T(8,128)S(1)}, f32[2,128,256]{2,1,0:T(8,128)S(1)}, u32[]{:S(2)}, u32[]{:S(2)}) collective-permute-start(f32[2,128,256]{2,1,0:T(8,128)S(1)} %get-tuple-element.25), channel_id=1, source_target_pairs={{0,30},{2,4},{4,2},{6,8},{8,6},{10,12},{12,10},{14,16},{16,14},{18... | collective-permute-start | bytes 786440 | tf_op jit(solution)/shard_map/ppermute | solution.py:294

commit v3 on v2

--- a/solution.py
+++ b/solution.py
@@ -90,7 +90,7 @@
     return zr, zi
 
 
-def call(kernel, name, results, scalars, arrays, aliases=(), scratch=(), limit=16):
+def call(kernel, results, scalars, arrays, aliases=(), scratch=(), limit=6):
     arrays = [pltpu.with_memory_space_constraint(x, pltpu.VMEM) for x in arrays]
     return pl.pallas_call(
         kernel,
@@ -100,7 +100,6 @@
         input_output_aliases={len(scalars) + i: o for i, o in aliases},
         scratch_shapes=list(scratch),
         compiler_params=pltpu.CompilerParams(vmem_limit_bytes=limit * 2**20),
-        name=name,
     )(*scalars, *arrays)
 
 
@@ -126,49 +125,54 @@
         out[layer] = value
 
 
-def own_kernel(position, potential, tile, own, sem):
-    copy = pltpu.make_async_copy(potential, tile, sem)
-    copy.start()
-    copy.wait()
-    fold_columns(tile, position, own)
-
-
-def cut_kernel(fast, slow, tile, for_fast, for_slow):
-    fold_columns(tile, slow, for_slow)
-    fold_columns(tile, fast, for_fast)
-
-
-def fill(table, owner, piece, rows):
-    layers = piece.shape[0]
-    for layer in range(layers):
-        s, c = sin_cos(piece[layer])
-        table[owner * layers + layer, 0, rows] = c
-        table[owner * layers + layer, 1, rows] = s
-
-
-def first_kernel(place, position, own, probe, table, wave):
+def tile_kernel(potential, tile, sems):
+    layers, strip, _ = potential.shape
+    copies = []
+    for k in range(8):
+        at = (k // (8 // layers), slice(k % (8 // layers) * strip * layers // 8, (k % (8 // layers) + 1) * strip * layers // 8))
+        copies.append(pltpu.make_async_copy(potential.at[at], tile.at[at], sems.at[k]))
+        copies[k].start()
+    for copy in copies:
+        copy.wait()
+
+
+def cut_kernel(position, tile, *refs):
+    fold_columns(tile, position, refs[-1])
+
+
+def fill(table, slices, rows, piece):
+    for layer, at in enumerate(slices):
+        s, c = sin_cos(piece(layer))
+        table[at, 0, rows] = c
+        table[at, 1, rows] = s
+
+
+def slices_of(depth, k, count, layers):
+    first = (depth - k + count) % count * layers
+    return [first + layer for layer in range(layers)]
+
+
+def outside(position, above, below):
+    row = lax.broadcasted_iota(jnp.int32, above.shape[1:], 0)
+    mask = row >= entry(position, 0) % above.shape[1]
+    return lambda layer: jnp.where(mask, above[layer], below[layer])
+
+
+def first_kernel(place, position, own, probe, prop, dft, table, wave):
     strip = own.shape[1]
     row_shift = position[0, 0] % strip + strip
     column_shift = position[0, 1] % (2 * strip)
     for k in range(2):
         wave[k] = pltpu.roll(pltpu.roll(probe[k], row_shift, 0), column_shift, 1)
-    fill(table, place[0], own, slice(0, strip))
-
-
-def second_kernel(count, place, *refs):
-    owns, table = refs[: count - 1], refs[-1]
-    strip = owns[0].shape[1]
-    for k in range(1, count):
-        fill(table, (place[0] - k + count) % count, owns[k - 1], slice(0, strip))
-
-
-def merge_kernel(parity, position, fast, slow, _, out):
-    layers, strip, extent = out.shape
-    row = lax.broadcasted_iota(jnp.int32, (strip, extent), 0)
-    above = (row >= entry(position, 0) % strip).astype(jnp.int32)
-    mask = above != parity[0]
-    for layer in range(layers):
-        out[layer] = jnp.where(mask, slow[layer], fast[layer])
+    layers = own.shape[0]
+    slices = [place[0] * layers + layer for layer in range(layers)]
+    fill(table, slices, slice(0, strip), lambda layer: own[layer])
+
+
+def merge_kernel(position, above, below, _, *out):
+    piece = outside(position, above, below)
+    for layer in range(above.shape[0]):
+        out[layer][...] = piece(layer)
 
 
 def transmit(trans, real, imag):
@@ -176,9 +180,12 @@
     return c * real - s * imag, c * imag + s * real
 
 
-def enter_kernel(place, wave_in, other, prop, table_in, wave_out, table, saved):
-    layers, strip, _ = other.shape
-    fill(table, place[0], other, slice(strip, 2 * strip))
+def enter_kernel(layers, place, wave_in, prop, table_in, *refs):
+    others = refs[:layers]
+    wave_out, table, saved = refs[layers:]
+    strip, extent = others[0].shape
+    slices = [place[0] * layers + layer for layer in range(layers)]
+    fill(table, slices, slice(strip, extent), lambda layer: others[layer][...])
 
     def forward(layer, wave):
         wave = transmit((table[layer, 0], table[layer, 1]), *wave)
@@ -193,16 +200,32 @@
         wave_out[1] = wave[1]
 
 
+def middle_kernel(count, layers, place, wave_in, prop, table_in, *refs):
+    owns = refs[: count - 1]
+    others = refs[count - 1 : 2 * count - 2]
+    wave_out, table = refs[2 * count - 2 :]
+    strip, extent = others[0].shape
+    owners = [slices_of(place[0], k, count, layers)[0] for k in range(1, count)]
+    fill(table, owners, slice(0, strip), lambda k: owns[k][0])
+    fill(table, owners, slice(strip, extent), lambda k: others[k][...])
+    s = jnp.where(place[0] == 0, layers, 0)
+    wave = transmit((table[s, 0], table[s, 1]), wave_in[0], wave_in[1])
+    wave_out[0], wave_out[1] = sandwich(prop, *wave)
+
+
 def solve_kernel(count, place, wave_in, saved_in, intensity, prop, dft, table_in, *refs):
-    others = refs[: count - 1]
-    mine, outer, table, saved = refs[count - 1 :]
+    mine, outer, table, saved = refs[-4:]
     layers, strip, extent = mine.shape
     slices = layers * count
     last = slices - 1
     depth = place[0]
     first = depth * layers
     for k in range(1, count):
-        fill(table, (depth - k + count) % count, others[k - 1], slice(strip, extent))
+        own = refs[k - 1]
+        others = refs[count - 1 + (k - 1) * (layers - 1) : count - 1 + k * (layers - 1)]
+        owners = slices_of(depth, k, count, layers)[1:]
+        fill(table, owners, slice(0, strip), lambda layer: own[layer + 1])
+        fill(table, owners, slice(strip, extent), lambda layer: others[layer][...])
 
     def enter(s, wave):
         wave = transmit((table[s, 0], table[s, 1]), *wave)
@@ -215,7 +238,7 @@
         return wave
 
     wave = (wave_in[0], wave_in[1])
-    start = jnp.where(depth == 0, layers, 0)
+    start = jnp.where(depth == 0, layers + 1, 1)
     wave = lax.fori_loop(start, last, lambda s, w: sandwich(prop, *enter(s, w)), wave)
     far_real, far_imag = sandwich(dft, *enter(last, wave))
     misfit = far_real * far_real + far_imag * far_imag - intensity[0]
@@ -283,7 +306,7 @@
     count = lax.axis_size("probe")
     depth_count = lax.axis_size("depth")
     assert positions.shape[0] == 1 and extent == 2 * strip and columns % extent == 0
-    assert count % 2 == 0
+    assert count % 2 == 0 and layers * (depth_count - 1) > 1
     slices = layers * depth_count
     half = (layers, strip, extent)
     field = (2, extent, extent)
@@ -294,61 +317,77 @@
         slow = lax.ppermute(slow, "probe", slow_pairs)
         return lax.ppermute(fast, "probe", fast_pairs), slow
 
-    def from_depths(x):
+    def step(x, by):
+        return lax.ppermute(x, "probe", [(i, (i + by) % count) for i in range(count)])
+
+    def to_depths(x):
         out = []
         for k in range(1, depth_count):
             pairs = [(i, (i + k) % depth_count) for i in range(depth_count)]
             out.append(lax.ppermute(x, "depth", pairs))
         return out
 
+    def cut(position, *after):
+        return call(cut_kernel, [half], [], [position, tile, *after])[0]
+
     place = lax.axis_index("depth").astype(jnp.int32).reshape(1)
-    parity = (lax.axis_index("probe").astype(jnp.int32) % 2).reshape(1)
+    parity = (lax.axis_index("probe").astype(jnp.int32) & 1).reshape(1)
     prop, dft = [jnp.asarray(x) for x in tables(extent)]
 
-    fast_position, slow_position = swapped(positions, positions)
-    tile, own = pl.pallas_call(
-        own_kernel,
-        out_shape=[pltpu.VMEM(potential.shape, f32), pltpu.VMEM(half, f32)],
-        in_specs=[VMEM, ANY],
-        out_specs=[VMEM] * 2,
-        scratch_shapes=[pltpu.SemaphoreType.DMA],
-        name="own",
-    )(positions, potential)
-    owns = from_depths(own)
-    pieces = call(cut_kernel, "cut", [half] * 2, [], [fast_position, slow_position, tile])
-    fast, slow = swapped(*pieces)
+    before = step(positions, 1)
+    after = step(positions, -1)
+    (tile,) = pl.pallas_call(
+        tile_kernel,
+        out_shape=[pltpu.VMEM(potential.shape, f32)],
+        in_specs=[ANY],
+        out_specs=[VMEM],
+        scratch_shapes=[pltpu.SemaphoreType.DMA((8,))],
+        name="tile",
+    )(potential)
+    for_before = cut(before)
+    below = step(for_before, -1)
+    for_after = cut(after, for_before)
+    above = step(for_after, 1)
+    own = cut(positions, for_after)
+    owns = to_depths(own)
     table, wave = call(
-        first_kernel, "first", [(slices, *field), field], [place, positions], [own, probe]
-    )
-    (table,) = call(
-        functools.partial(second_kernel, depth_count),
-        "second",
-        [table.shape],
-        [place],
-        [*owns, table],
-        aliases=[(depth_count - 1, 0)],
-    )
-    (other,) = call(merge_kernel, "merge", [half], [parity], [positions, fast, slow, table])
-    others = from_depths(other)
+        first_kernel,
+        [(slices, *field), field],
+        [place, positions],
+        [own, probe, prop, dft],
+    )
+    other = call(merge_kernel, [half[1:]] * layers, [], [positions, above, below, wave])
+    others = []
+    for layer in range(layers):
+        others.append(to_depths(other[layer]))
     wave, table, saved = call(
-        enter_kernel,
-        "enter",
+        functools.partial(enter_kernel, layers),
         [field, table.shape, (layers, *field)],
         [place],
-        [wave, other, prop, table],
-        aliases=[(0, 0), (3, 1)],
-    )
+        [wave, prop, table, *other],
+        aliases=[(0, 0), (2, 1)],
+    )
+    wave, table = call(
+        functools.partial(middle_kernel, depth_count, layers),
+        [field, table.shape],
+        [place],
+        [wave, prop, table, *owns, *others[0]],
+        aliases=[(0, 0), (2, 1)],
+    )
+    rest = [others[layer][k] for k in range(depth_count - 1) for layer in range(1, layers)]
     mine, outer, _, _ = call(
         functools.partial(solve_kernel, depth_count),
-        "solve",
         [half, half, table.shape, saved.shape],
         [place],
-        [wave, saved, intensity, prop, dft, table, *others],
+        [wave, saved, intensity, prop, dft, table, *owns, *rest],
         aliases=[(5, 2), (1, 3)],
     )
+    odd = parity[0] == 1
+    fast_position = jnp.where(odd, before, after)
+    slow_position = jnp.where(odd, after, before)
     fast, slow = swapped(outer, outer)
     (staged,) = call(
-        stage_kernel, "stage", [potential.shape], [parity], [positions, fast_position, mine, fast]
+        stage_kernel, [potential.shape], [parity], [positions, fast_position, mine, fast]
     )
     arrays = [slow_position, slow, staged]
     arrays = [pltpu.with_memory_space_constraint(x, pltpu.VMEM) for x in arrays]
@@ -368,4 +407,7 @@
 def solution(mesh):
     in_specs = (P("depth", "probe", None), P(), P("probe", None), P("probe", None, None))
     out_specs = P("depth", "probe", None)
-    return jax.shard_map(local, mesh=mesh, in_specs=in_specs, out_specs=out_specs, check_vma=False)
+
+    return jax.shard_map(
+        local, mesh=mesh, in_specs=in_specs, out_specs=out_specs, check_vma=False
+    )

time: 45.4 us -> 42 us (0.925)
  waiting for transfers between devices: 18.3 us -> 7.9 us
  starting transfers between devices: 11 us -> 16.6 us
  local copies, waits for them, and re-layouts: 0.03 us -> 1.07 us
    ppermute x2 -> x7, starting transfers between devices: 2.16 us -> 14.1 us  [the longest x4 9.98 us: step(): lax.ppermute(x, 'probe', [(i, (i + by) % count) for i in range(count)])]
    ppermute x3 -> x1, starting transfers between devices: 8.23 us -> 2.44 us  [swapped(): slow = lax.ppermute(slow, 'probe', slow_pairs)]
    ppermute x3 -> x1, waiting for transfers between devices: 10.6 us -> 5.88 us  [swapped(): slow = lax.ppermute(slow, 'probe', slow_pairs)]
    ppermute x2 -> x7, waiting for transfers between devices: 6.51 us -> 2.02 us  [the longest x3 1.99 us: to_depths(): out.append(lax.ppermute(x, 'depth', pairs))]
    ppermute x3 -> x1, waiting for transfers between devices: 1.16 us -> 0.01 us  [swapped(): return (lax.ppermute(fast, 'probe', fast_pairs), slow)]
    unnamed x10, local copies, waits for them, and re-layouts: 0.03 us -> 1.07 us
    pallas_call x7 -> x9, Pallas kernels: 12.6 us -> 13.6 us  [call(): pl.pallas_call(kernel, out_shape=[pltpu.VMEM(shape, f32) for shape in res...]
    pallas_call x1, Pallas kernels: 2.05 us -> 1.35 us  [local(): pl.pallas_call(tile_kernel, out_shape=[pltpu.VMEM(potential.shape, f32)],...]
  transfers between devices with their start and end apart: 8 -> 9, of which waited for: 5 -> 3; matrix products, arithmetic and copies ran while one was open for 0% -> 0% of each run, Pallas kernels for 15% -> 20%
where the time goes in v3:
time: 42 us; the launch traced here: 41.8 us
  starting transfers between devices  16.6 us (40%)
  Pallas kernels  16.1 us (38%)
  waiting for transfers between devices  7.9 us (19%)
  local copies, waits for them, and re-layouts  1.07 us (3%)
    pallas_call x9, Pallas kernels, call(): pl.pallas_call(kernel, out_shape=[pltpu.VMEM(shape, f32) for shape in res...  13.6 us
    ppermute x4, starting transfers between devices, step(): lax.ppermute(x, 'probe', [(i, (i + by) % count) for i in range(count)])  9.98 us
    ppermute x1, waiting for transfers between devices, swapped(): slow = lax.ppermute(slow, 'probe', slow_pairs)  5.88 us
    ppermute x3, starting transfers between devices, to_depths(): out.append(lax.ppermute(x, 'depth', pairs))  4.09 us
    ppermute x1, starting transfers between devices, swapped(): slow = lax.ppermute(slow, 'probe', slow_pairs)  2.44 us
    ppermute x3, waiting for transfers between devices, to_depths(): out.append(lax.ppermute(x, 'depth', pairs))  1.99 us
    pallas_call x1, Pallas kernels, local(): pl.pallas_call(tile_kernel, out_shape=[pltpu.VMEM(potential.shape, f32)],...  1.35 us
    pallas_call x1, Pallas kernels, local(): pl.pallas_call(place_kernel, out_shape=jax.ShapeDtypeStruct(potential.sha...  1.15 us
  transfers between devices with their start and end apart: 9, of which 3 were waited for; matrix products, arithmetic and copies ran while one was open for 0% of the time, Pallas kernels for 20%

profile of v3, /device:TPU:0, one launch (start us, length us, event | category | flops | bytes accessed | tf_op | source)
XLA Modules:
  0.0 41.8 jit_solution(1228526348688874565)
XLA Ops:
  0.0 0.0 copy-start.4
  0.0 0.5 %collective-permute-start.1 = (s32[1,2]{1,0:T(1,128)}, s32[1,2]{1,0:T(1,128)S(1)}, u32[]{:S(2)}, u32[]{:S(2)}) collective-permute-start(s32[1,2]{1,0:T(1,128)} %position.7), channel_id=1, source_target_pairs={{0,2},{2,4},{4,6},{6,8},{8,10},{10,12},{12,14},{14,16},{16,18},{18... | collective-permute-start | bytes 32 | tf_op jit(solution)/shard_map/ppermute | solution.py:321
  0.5 5.0 %collective-permute-start = (s32[1,2]{1,0:T(1,128)}, s32[1,2]{1,0:T(1,128)S(1)}, u32[]{:S(2)}, u32[]{:S(2)}) collective-permute-start(s32[1,2]{1,0:T(1,128)} %position.7), channel_id=1, source_target_pairs={{0,30},{2,0},{4,2},{6,4},{8,6},{10,8},{12,10},{14,12},{16,14},{18,... | collective-permute-start | bytes 32 | tf_op jit(solution)/shard_map/ppermute | solution.py:321
  5.5 1.3 %tile.1 = f32[2,128,1024]{2,1,0:T(8,128)S(1)} custom-call(f32[2,128,1024]{2,1,0:T(8,128)} %potential.1), custom_call_target="tpu_custom_call" | custom-call | tf_op jit(solution)/shard_map/tile/pallas_call | solution.py:339
  6.9 0.0 copy-start
  6.9 0.0 copy-start.1
  6.9 0.0 collective-permute-done.1.position
  6.9 0.1 shard_map.64.refs_0_
  7.0 0.0 collective-permute-done.position
  7.0 0.1 shard_map.65.refs_0_
  7.2 0.1 collective-permute-start.2
  7.2 4.4 %collective-permute-start.3 = (f32[2,128,256]{2,1,0:T(8,128)S(1)}, f32[2,128,256]{2,1,0:T(8,128)}, u32[]{:S(2)}, u32[]{:S(2)}) collective-permute-start(f32[2,128,256]{2,1,0:T(8,128)S(1)} %shard_map.64.refs_0_), channel_id=1, source_target_pairs={{0,30},{2,0},{4,2},{6,4},{8,6},{10,8},{12,10},{14,12},{16,14},{18,... | collective-permute-start | bytes 786440 | tf_op jit(solution)/shard_map/ppermute | solution.py:321
  11.7 0.0 copy-done.4
  11.7 0.1 shard_map.66.own
  11.8 2.0 %collective-permute-start.4 = (f32[2,128,256]{2,1,0:T(8,128)S(1)}, f32[2,128,256]{2,1,0:T(8,128)S(1)}, u32[]{:S(2)}, u32[]{:S(2)}) collective-permute-start(f32[2,128,256]{2,1,0:T(8,128)S(1)} %shard_map.66.own), channel_id=1, source_target_pairs={{0,1},{1,0},{2,3},{3,2},{4,5},{5,4},{6,7},{7,6},{8,9},{9,8},{10,11... | collective-permute-start | bytes 786440 | tf_op jit(solution)/shard_map/ppermute | solution.py:327
  13.8 0.0 copy-done
  13.8 0.0 copy-done.1
  13.8 0.0 copy-start.2
  13.8 1.0 %copy-done.2 = f32[2,256,256]{2,1,0:T(8,128)S(1)} copy-done((f32[2,256,256]{2,1,0:T(8,128)S(1)}, f32[2,256,256]{2,1,0:T(8,128)}, u32[]{:S(2)}) %copy-start.2) | copy-done | bytes 524312
  14.9 1.1 %shard_map.67 = (f32[4,2,256,256]{3,2,1,0:T(8,128)S(1)}, f32[2,256,256]{2,1,0:T(8,128)S(1)}) custom-call(s32[1]{0:T(128)} %bitcast.1.place, s32[1,2]{1,0:T(1,128)S(1)} %copy-done.4, f32[2,128,256]{2,1,0:T(8,128)S(1)} %shard_map.66.own, f32[2,256,256]{2,1,0:T(8,128)S(1)} %copy-done.2, bf16[6,256,256]{2,1,0:T(8,128)(2,1)S(1)} %copy-done, ...), custom_call_target="tpu_custom_call" | custom-call | tf_op jit(solution)/shard_map/pallas_call | solution.py:95
  16.0 0.0 collective-permute-done.2.above
  16.0 0.0 collective-permute-done.3.below
  16.0 1.1 %shard_map.68 = (f32[128,256]{1,0:T(8,128)S(1)}, f32[128,256]{1,0:T(8,128)S(1)}) custom-call(s32[1,2]{1,0:T(1,128)S(1)} %copy-done.4, f32[2,128,256]{2,1,0:T(8,128)} %collective-permute-done.2.above, f32[2,128,256]{2,1,0:T(8,128)} %collective-permute-done.3.below, f32[2,256,256]{2,1,0:T(8,128)S(1)} %get-tuple-element.16._.wave_in), custom_call_target="tpu_custom_call" | custom-call | tf_op jit(solution)/shard_map/pallas_call | solution.py:95
  17.1 1.8 %collective-permute-start.5 = (f32[128,256]{1,0:T(8,128)S(1)}, f32[128,256]{1,0:T(8,128)S(1)}, u32[]{:S(2)}, u32[]{:S(2)}) collective-permute-start(f32[128,256]{1,0:T(8,128)S(1)} %get-tuple-element.18.refs_0_), channel_id=1, source_target_pairs={{0,1},{1,0},{2,3},{3,2},{4,5},{5,4},{6,7},{7,6},{8,9},{9,8},{10,11... | collective-permute-start | bytes 393224 | tf_op jit(solution)/shard_map/ppermute | solution.py:327
  19.0 0.3 collective-permute-start.6
  19.2 2.9 %shard_map.69 = (f32[2,256,256]{2,1,0:T(8,128)S(1)}, f32[4,2,256,256]{3,2,1,0:T(8,128)S(1)}, f32[2,2,256,256]{3,2,1,0:T(8,128)S(1)}) custom-call(s32[1]{0:T(128)} %bitcast.1.place, f32[2,256,256]{2,1,0:T(8,128)S(1)} %get-tuple-element.16._.wave_in, bf16[6,256,256]{2,1,0:T(8,128)(2,1)S(1)} %copy-done, ...), custom_call_target="tpu_custom_call", output_to_operand_aliasing={{0}: (1, {}), {1}: (3, {})} | custom-call | tf_op jit(solution)/shard_map/pallas_call | solution.py:95
  22.1 0.0 copy-start.3
  22.1 0.0 collective-permute-done.4.refs_0_
  22.1 1.5 %collective-permute-done.5.refs_1_ = f32[128,256]{1,0:T(8,128)S(1)} collective-permute-done((f32[128,256]{1,0:T(8,128)S(1)}, f32[128,256]{1,0:T(8,128)S(1)}, u32[]{:S(2)}, u32[]{:S(2)}) %collective-permute-start.5) | collective-permute-done | bytes 131104 | tf_op jit(solution)/shard_map/ppermute | solution.py:327
  23.6 1.4 %shard_map.70 = (f32[2,256,256]{2,1,0:T(8,128)S(1)}, f32[4,2,256,256]{3,2,1,0:T(8,128)S(1)}) custom-call(s32[1]{0:T(128)} %bitcast.1.place, f32[2,256,256]{2,1,0:T(8,128)S(1)} %get-tuple-element.20.wave_in, bf16[6,256,256]{2,1,0:T(8,128)(2,1)S(1)} %copy-done, ...), custom_call_target="tpu_custom_call", output_to_operand_aliasing={{0}: (1, {}), {1}: (3, {})} | custom-call | tf_op jit(solution)/shard_map/pallas_call | solution.py:95
  25.0 0.5 %collective-permute-done.6.refs_1_ = f32[128,256]{1,0:T(8,128)S(1)} collective-permute-done((f32[128,256]{1,0:T(8,128)S(1)}, f32[128,256]{1,0:T(8,128)S(1)}, u32[]{:S(2)}, u32[]{:S(2)}) %collective-permute-start.6) | collective-permute-done | bytes 131104 | tf_op jit(solution)/shard_map/ppermute | solution.py:327
  25.5 0.0 copy-done.3
  25.5 6.4 %shard_map.71 = (f32[2,128,256]{2,1,0:T(8,128)S(1)}, f32[2,128,256]{2,1,0:T(8,128)S(1)}, f32[4,2,256,256]{3,2,1,0:T(8,128)S(1)}, f32[2,2,256,256]{3,2,1,0:T(8,128)S(1)}) custom-call(s32[1]{0:T(128)} %bitcast.1.place, f32[2,256,256]{2,1,0:T(8,128)S(1)} %get-tuple-element.22.wave_in, ...), custom_call_target="tpu_custom_call", output_to_operand_aliasing={{2}: (6, {}), {3}: (2, {})} | custom-call | tf_op jit(solution)/shard_map/pallas_call | solution.py:95
  31.9 0.1 collective-permute-start.8
  32.0 2.4 %collective-permute-start.7 = (f32[2,128,256]{2,1,0:T(8,128)S(1)}, f32[2,128,256]{2,1,0:T(8,128)S(1)}, u32[]{:S(2)}, u32[]{:S(2)}) collective-permute-start(f32[2,128,256]{2,1,0:T(8,128)S(1)} %get-tuple-element.25), channel_id=1, source_target_pairs={{0,30},{2,4},{4,2},{6,8},{8,6},{10,12},{12,10},{14,16},{16,14},{18... | collective-permute-start | bytes 786440 | tf_op jit(solution)/shard_map/ppermute | solution.py:317
  34.4 0.0 collective-permute-done.8.fast
  34.4 0.3 shard_map.72.staged
  34.8 5.9 %collective-permute-done.7.slow = f32[2,128,256]{2,1,0:T(8,128)S(1)} collective-permute-done((f32[2,128,256]{2,1,0:T(8,128)S(1)}, f32[2,128,256]{2,1,0:T(8,128)S(1)}, u32[]{:S(2)}, u32[]{:S(2)}) %collective-permute-start.7) | collective-permute-done | bytes 262176 | tf_op jit(solution)/shard_map/ppermute | solution.py:317
  40.7 1.1 %place.1 = f32[2,128,1024]{2,1,0:T(8,128)} custom-call(s32[1]{0:T(128)} %bitcast.parity, s32[1,2]{1,0:T(1,128)S(1)} %get-tuple-element.28.slow_position, f32[2,128,256]{2,1,0:T(8,128)S(1)} %collective-permute-done.7.slow, f32[2,128,1024]{2,1,0:T(8,128)S(1)} %shard_map.72.staged), custom_call_target="tpu_custom_call" | custom-call | tf_op jit(solution)/shard_map/place/pallas_call | solution.py:394
  (1 shorter events, 0.0 us)
Async XLA Ops:
  0.0 11.7 %copy-start.4 = (s32[1,2]{1,0:T(1,128)S(1)}, s32[1,2]{1,0:T(1,128)}, u32[]{:S(2)}) copy-start(s32[1,2]{1,0:T(1,128)} %position.7) | copy-start | bytes 28
  0.0 6.9 %collective-permute-start.1 = (s32[1,2]{1,0:T(1,128)}, s32[1,2]{1,0:T(1,128)S(1)}, u32[]{:S(2)}, u32[]{:S(2)}) collective-permute-start(s32[1,2]{1,0:T(1,128)} %position.7), channel_id=1, source_target_pairs={{0,2},{2,4},{4,6},{6,8},{8,10},{10,12},{12,14},{14,16},{16,18},{18... | collective-permute-start | bytes 32 | tf_op jit(solution)/shard_map/ppermute | solution.py:321
  0.5 6.5 %collective-permute-start = (s32[1,2]{1,0:T(1,128)}, s32[1,2]{1,0:T(1,128)S(1)}, u32[]{:S(2)}, u32[]{:S(2)}) collective-permute-start(s32[1,2]{1,0:T(1,128)} %position.7), channel_id=1, source_target_pairs={{0,30},{2,0},{4,2},{6,4},{8,6},{10,8},{12,10},{14,12},{16,14},{18,... | collective-permute-start | bytes 32 | tf_op jit(solution)/shard_map/ppermute | solution.py:321
  6.9 7.0 %copy-start = (bf16[6,256,256]{2,1,0:T(8,128)(2,1)S(1)}, bf16[6,256,256]{2,1,0:T(8,128)(2,1)}, u32[]{:S(2)}) copy-start(bf16[6,256,256]{2,1,0:T(8,128)(2,1)} %constant.14.clone.prop) | copy-start | bytes 2359300
  6.9 6.9 %copy-start.1 = (bf16[6,256,256]{2,1,0:T(8,128)(2,1)S(1)}, bf16[6,256,256]{2,1,0:T(8,128)(2,1)}, u32[]{:S(2)}) copy-start(bf16[6,256,256]{2,1,0:T(8,128)(2,1)} %constant.15.clone.dft) | copy-start | bytes 2359300
  7.2 8.8 %collective-permute-start.2 = (f32[2,128,256]{2,1,0:T(8,128)S(1)}, f32[2,128,256]{2,1,0:T(8,128)}, u32[]{:S(2)}, u32[]{:S(2)}) collective-permute-start(f32[2,128,256]{2,1,0:T(8,128)S(1)} %shard_map.65.refs_0_), channel_id=1, source_target_pairs={{0,2},{2,4},{4,6},{6,8},{8,10},{10,12},{12,14},{14,16},{16,18},{18... | collective-permute-start | bytes 786440 | tf_op jit(solution)/shard_map/ppermute | solution.py:321
  7.2 8.7 %collective-permute-start.3 = (f32[2,128,256]{2,1,0:T(8,128)S(1)}, f32[2,128,256]{2,1,0:T(8,128)}, u32[]{:S(2)}, u32[]{:S(2)}) collective-permute-start(f32[2,128,256]{2,1,0:T(8,128)S(1)} %shard_map.64.refs_0_), channel_id=1, source_target_pairs={{0,30},{2,0},{4,2},{6,4},{8,6},{10,8},{12,10},{14,12},{16,14},{18,... | collective-permute-start | bytes 786440 | tf_op jit(solution)/shard_map/ppermute | solution.py:321
  11.8 10.3 %collective-permute-start.4 = (f32[2,128,256]{2,1,0:T(8,128)S(1)}, f32[2,128,256]{2,1,0:T(8,128)S(1)}, u32[]{:S(2)}, u32[]{:S(2)}) collective-permute-start(f32[2,128,256]{2,1,0:T(8,128)S(1)} %shard_map.66.own), channel_id=1, source_target_pairs={{0,1},{1,0},{2,3},{3,2},{4,5},{5,4},{6,7},{7,6},{8,9},{9,8},{10,11... | collective-permute-start | bytes 786440 | tf_op jit(solution)/shard_map/ppermute | solution.py:327
  13.8 1.0 %copy-start.2 = (f32[2,256,256]{2,1,0:T(8,128)S(1)}, f32[2,256,256]{2,1,0:T(8,128)}, u32[]{:S(2)}) copy-start(f32[2,256,256]{2,1,0:T(8,128)} %probe.1) | copy-start | bytes 1572868
  17.1 6.4 %collective-permute-start.5 = (f32[128,256]{1,0:T(8,128)S(1)}, f32[128,256]{1,0:T(8,128)S(1)}, u32[]{:S(2)}, u32[]{:S(2)}) collective-permute-start(f32[128,256]{1,0:T(8,128)S(1)} %get-tuple-element.18.refs_0_), channel_id=1, source_target_pairs={{0,1},{1,0},{2,3},{3,2},{4,5},{5,4},{6,7},{7,6},{8,9},{9,8},{10,11... | collective-permute-start | bytes 393224 | tf_op jit(solution)/shard_map/ppermute | solution.py:327
  19.0 6.6 %collective-permute-start.6 = (f32[128,256]{1,0:T(8,128)S(1)}, f32[128,256]{1,0:T(8,128)S(1)}, u32[]{:S(2)}, u32[]{:S(2)}) collective-permute-start(f32[128,256]{1,0:T(8,128)S(1)} %get-tuple-element.19.refs_1_), channel_id=1, source_target_pairs={{0,1},{1,0},{2,3},{3,2},{4,5},{5,4},{6,7},{7,6},{8,9},{9,8},{10,11... | collective-permute-start | bytes 393224 | tf_op jit(solution)/shard_map/ppermute | solution.py:327
  22.1 3.4 %copy-start.3 = (f32[1,256,256]{2,1,0:T(8,128)S(1)}, f32[1,256,256]{2,1,0:T(8,128)}, u32[]{:S(2)}) copy-start(f32[1,256,256]{2,1,0:T(8,128)} %intensity.1) | copy-start | bytes 786436
  31.9 2.5 %collective-permute-start.8 = (f32[2,128,256]{2,1,0:T(8,128)S(1)}, f32[2,128,256]{2,1,0:T(8,128)S(1)}, u32[]{:S(2)}, u32[]{:S(2)}) collective-permute-start(f32[2,128,256]{2,1,0:T(8,128)S(1)} %get-tuple-element.25), channel_id=1, source_target_pairs={{0,2},{2,0},{4,6},{6,4},{8,10},{10,8},{12,14},{14,12},{16,18},{18,... | collective-permute-start | bytes 786440 | tf_op jit(solution)/shard_map/ppermute | solution.py:318
  32.0 8.7 %collective-permute-start.7 = (f32[2,128,256]{2,1,0:T(8,128)S(1)}, f32[2,128,256]{2,1,0:T(8,128)S(1)}, u32[]{:S(2)}, u32[]{:S(2)}) collective-permute-start(f32[2,128,256]{2,1,0:T(8,128)S(1)} %get-tuple-element.25), channel_id=1, source_target_pairs={{0,30},{2,4},{4,2},{6,8},{8,6},{10,12},{12,10},{14,16},{16,14},{18... | collective-permute-start | bytes 786440 | tf_op jit(solution)/shard_map/ppermute | solution.py:317

commit v4 on v3

--- a/solution.py
+++ b/solution.py
@@ -19,13 +19,13 @@
 
 
 def poly_tables():
-    x = np.cos(np.linspace(0.0, np.pi / 2, 4001)) * (np.pi / 2) * 1.0005
-    z = x * x
+    v = np.cos(np.linspace(0.0, np.pi / 2, 4001)) * 6.01
+    h = interaction * v / 2
     fit = np.polynomial.chebyshev.Chebyshev.fit
     kind = np.polynomial.Polynomial
-    sine = fit(z, np.sinc(x / np.pi), 5).convert(kind=kind).coef
-    cosine = fit(z, np.cos(x), 5).convert(kind=kind).coef
-    return [float(v) for v in sine], [float(v) for v in cosine]
+    sine = fit(v * v, interaction * np.sinc(h / np.pi), 4).convert(kind=kind).coef
+    cosine = fit(v * v, np.cos(h), 5).convert(kind=kind).coef
+    return [float(x) for x in sine], [float(x) for x in cosine]
 
 
 def split_table(matrix):
@@ -50,19 +50,15 @@
 
 def sin_cos(window):
     sine, cosine = poly_tables()
-    half = window * (interaction / 2)
-    turns = jnp.round(half * (1.0 / np.pi))
-    pi_high = float(np.float32(3.140625))
-    pi_low = float(np.pi - 3.140625)
-    x = (half - turns * pi_high) - turns * pi_low
-    z = x * x
-    s = sine[5]
-    c = cosine[5]
-    for k in range(4, -1, -1):
-        s = s * z + sine[k]
-        c = c * z + cosine[k]
-    s = s * x
-    return 2.0 * s * c, 1.0 - 2.0 * (s * s)
+    z = window * window
+    s = sine[-1]
+    for k in sine[-2::-1]:
+        s = s * z + k
+    s = s * window
+    c = cosine[-1]
+    for k in cosine[-2::-1]:
+        c = c * z + k
+    return s * c, 1.0 - (0.5 * s) * s
 
 
 def parts_of(x):
@@ -90,7 +86,7 @@
     return zr, zi
 
 
-def call(kernel, results, scalars, arrays, aliases=(), scratch=(), limit=6):
+def call(kernel, results, scalars, arrays, aliases=(), scratch=(), limit=4):
     arrays = [pltpu.with_memory_space_constraint(x, pltpu.VMEM) for x in arrays]
     return pl.pallas_call(
         kernel,
@@ -158,15 +154,13 @@
     return lambda layer: jnp.where(mask, above[layer], below[layer])
 
 
-def first_kernel(place, position, own, probe, prop, dft, table, wave):
-    strip = own.shape[1]
+def first_kernel(position, own, probe, _, upper, wave):
+    layers, strip, _ = own.shape
     row_shift = position[0, 0] % strip + strip
     column_shift = position[0, 1] % (2 * strip)
     for k in range(2):
         wave[k] = pltpu.roll(pltpu.roll(probe[k], row_shift, 0), column_shift, 1)
-    layers = own.shape[0]
-    slices = [place[0] * layers + layer for layer in range(layers)]
-    fill(table, slices, slice(0, strip), lambda layer: own[layer])
+    fill(upper, range(layers), slice(0, strip), lambda layer: own[layer])
 
 
 def merge_kernel(position, above, below, _, *out):
@@ -180,11 +174,14 @@
     return c * real - s * imag, c * imag + s * real
 
 
-def enter_kernel(layers, place, wave_in, prop, table_in, *refs):
+def enter_kernel(layers, place, wave_in, prop, upper, *refs):
     others = refs[:layers]
     wave_out, table, saved = refs[layers:]
     strip, extent = others[0].shape
     slices = [place[0] * layers + layer for layer in range(layers)]
+    for layer in range(layers):
+        for part in range(2):
+            table[slices[layer], part, :strip] = upper[layer, part]
     fill(table, slices, slice(strip, extent), lambda layer: others[layer][...])
 
     def forward(layer, wave):
@@ -350,11 +347,11 @@
     above = step(for_after, 1)
     own = cut(positions, for_after)
     owns = to_depths(own)
-    table, wave = call(
+    upper, wave = call(
         first_kernel,
-        [(slices, *field), field],
-        [place, positions],
-        [own, probe, prop, dft],
+        [(layers, 2, strip, extent), field],
+        [positions],
+        [own, probe, prop],
     )
     other = call(merge_kernel, [half[1:]] * layers, [], [positions, above, below, wave])
     others = []
@@ -362,10 +359,10 @@
         others.append(to_depths(other[layer]))
     wave, table, saved = call(
         functools.partial(enter_kernel, layers),
-        [field, table.shape, (layers, *field)],
+        [field, (slices, *field), (layers, *field)],
         [place],
-        [wave, prop, table, *other],
-        aliases=[(0, 0), (2, 1)],
+        [wave, prop, upper, *other],
+        aliases=[(0, 0)],
     )
     wave, table = call(
         functools.partial(middle_kernel, depth_count, layers),

time: 42 us -> 40.8 us (0.971)
  waiting for transfers between devices: 7.9 us -> 9.31 us
  Pallas kernels: 16.1 us -> 14.7 us
  local copies, waits for them, and re-layouts: 1.07 us -> 0.03 us
    pallas_call x9, Pallas kernels: 13.6 us -> 12.2 us  [call(): pl.pallas_call(kernel, out_shape=[pltpu.VMEM(shape, f32) for shape in res...]
    ppermute x4, waiting for transfers between devices: 0.03 us -> 1.08 us  [step(): lax.ppermute(x, 'probe', [(i, (i + by) % count) for i in range(count)])]
    unnamed x10, local copies, waits for them, and re-layouts: 1.07 us -> 0.03 us
  transfers between devices with their start and end apart: 9 -> 9, of which waited for: 3 -> 4; matrix products, arithmetic and copies ran while one was open for 0% -> 0% of each run, Pallas kernels for 20% -> 17%
where the time goes in v4:
time: 40.8 us; the launch traced here: 40.7 us
  starting transfers between devices  16.5 us (40%)
  Pallas kernels  14.7 us (36%)
  waiting for transfers between devices  9.31 us (23%)
    pallas_call x9, Pallas kernels, call(): pl.pallas_call(kernel, out_shape=[pltpu.VMEM(shape, f32) for shape in res...  12.2 us
    ppermute x4, starting transfers between devices, step(): lax.ppermute(x, 'probe', [(i, (i + by) % count) for i in range(count)])  9.98 us
    ppermute x1, waiting for transfers between devices, swapped(): slow = lax.ppermute(slow, 'probe', slow_pairs)  5.93 us
    ppermute x3, starting transfers between devices, to_depths(): out.append(lax.ppermute(x, 'depth', pairs))  4.09 us
    ppermute x1, starting transfers between devices, swapped(): slow = lax.ppermute(slow, 'probe', slow_pairs)  2.39 us
    ppermute x3, waiting for transfers between devices, to_depths(): out.append(lax.ppermute(x, 'depth', pairs))  2.3 us
    pallas_call x1, Pallas kernels, local(): pl.pallas_call(tile_kernel, out_shape=[pltpu.VMEM(potential.shape, f32)],...  1.35 us
    pallas_call x1, Pallas kernels, local(): pl.pallas_call(place_kernel, out_shape=jax.ShapeDtypeStruct(potential.sha...  1.15 us
  transfers between devices with their start and end apart: 9, of which 4 were waited for; matrix products, arithmetic and copies ran while one was open for 0% of the time, Pallas kernels for 17%

profile of v4, /device:TPU:0, one launch (start us, length us, event | category | flops | bytes accessed | tf_op | source)
XLA Modules:
  0.0 40.7 jit_solution(16809597501086403139)
XLA Ops:
  0.0 0.0 copy-start.4
  0.0 0.5 %collective-permute-start.1 = (s32[1,2]{1,0:T(1,128)}, s32[1,2]{1,0:T(1,128)S(1)}, u32[]{:S(2)}, u32[]{:S(2)}) collective-permute-start(s32[1,2]{1,0:T(1,128)} %position.7), channel_id=1, source_target_pairs={{0,2},{2,4},{4,6},{6,8},{8,10},{10,12},{12,14},{14,16},{16,18},{18... | collective-permute-start | bytes 32 | tf_op jit(solution)/shard_map/ppermute | solution.py:318
  0.5 5.0 %collective-permute-start = (s32[1,2]{1,0:T(1,128)}, s32[1,2]{1,0:T(1,128)S(1)}, u32[]{:S(2)}, u32[]{:S(2)}) collective-permute-start(s32[1,2]{1,0:T(1,128)} %position.7), channel_id=1, source_target_pairs={{0,30},{2,0},{4,2},{6,4},{8,6},{10,8},{12,10},{14,12},{16,14},{18,... | collective-permute-start | bytes 32 | tf_op jit(solution)/shard_map/ppermute | solution.py:318
  5.5 1.3 %tile.1 = f32[2,128,1024]{2,1,0:T(8,128)S(1)} custom-call(f32[2,128,1024]{2,1,0:T(8,128)} %potential.1), custom_call_target="tpu_custom_call" | custom-call | tf_op jit(solution)/shard_map/tile/pallas_call | solution.py:336
  6.9 0.0 copy-start
  6.9 0.0 copy-start.2
  6.9 0.0 collective-permute-done.1.position
  6.9 0.1 shard_map.64.refs_0_
  7.0 0.0 collective-permute-done.position
  7.0 0.1 shard_map.65.refs_0_
  7.2 0.1 collective-permute-start.2
  7.2 4.4 %collective-permute-start.3 = (f32[2,128,256]{2,1,0:T(8,128)S(1)}, f32[2,128,256]{2,1,0:T(8,128)S(1)}, u32[]{:S(2)}, u32[]{:S(2)}) collective-permute-start(f32[2,128,256]{2,1,0:T(8,128)S(1)} %shard_map.64.refs_0_), channel_id=1, source_target_pairs={{0,30},{2,0},{4,2},{6,4},{8,6},{10,8},{12,10},{14,12},{16,14},{18,... | collective-permute-start | bytes 786440 | tf_op jit(solution)/shard_map/ppermute | solution.py:318
  11.7 0.0 copy-done.4
  11.7 0.1 shard_map.66.own
  11.8 2.0 %collective-permute-start.4 = (f32[2,128,256]{2,1,0:T(8,128)S(1)}, f32[2,128,256]{2,1,0:T(8,128)S(1)}, u32[]{:S(2)}, u32[]{:S(2)}) collective-permute-start(f32[2,128,256]{2,1,0:T(8,128)S(1)} %shard_map.66.own), channel_id=1, source_target_pairs={{0,1},{1,0},{2,3},{3,2},{4,5},{5,4},{6,7},{7,6},{8,9},{9,8},{10,11... | collective-permute-start | bytes 786440 | tf_op jit(solution)/shard_map/ppermute | solution.py:324
  13.8 0.0 copy-done
  13.8 0.0 copy-done.2
  13.8 1.0 %shard_map.67 = (f32[2,2,128,256]{3,2,1,0:T(8,128)S(1)}, f32[2,256,256]{2,1,0:T(8,128)S(1)}) custom-call(s32[1,2]{1,0:T(1,128)S(1)} %copy-done.4, f32[2,128,256]{2,1,0:T(8,128)S(1)} %shard_map.66.own, f32[2,256,256]{2,1,0:T(8,128)S(1)} %copy-done.2, bf16[6,256,256]{2,1,0:T(8,128)(2,1)S(1)} %copy-done), custom_call_target="tpu_custom_call" | custom-call | tf_op jit(solution)/shard_map/pallas_call | solution.py:91
  14.8 1.1 %collective-permute-done.2.above = f32[2,128,256]{2,1,0:T(8,128)S(1)} collective-permute-done((f32[2,128,256]{2,1,0:T(8,128)S(1)}, f32[2,128,256]{2,1,0:T(8,128)S(1)}, u32[]{:S(2)}, u32[]{:S(2)}) %collective-permute-start.2) | collective-permute-done | bytes 262176 | tf_op jit(solution)/shard_map/ppermute | solution.py:318
  15.8 0.0 collective-permute-done.3.below
  15.8 0.1 shard_map.68
  15.9 1.9 %collective-permute-start.5 = (f32[128,256]{1,0:T(8,128)S(1)}, f32[128,256]{1,0:T(8,128)S(1)}, u32[]{:S(2)}, u32[]{:S(2)}) collective-permute-start(f32[128,256]{1,0:T(8,128)S(1)} %get-tuple-element.18.refs_0_), channel_id=1, source_target_pairs={{0,1},{1,0},{2,3},{3,2},{4,5},{5,4},{6,7},{7,6},{8,9},{9,8},{10,11... | collective-permute-start | bytes 393224 | tf_op jit(solution)/shard_map/ppermute | solution.py:324
  17.8 0.2 collective-permute-start.6
  18.0 2.8 %shard_map.69 = (f32[2,256,256]{2,1,0:T(8,128)S(1)}, f32[4,2,256,256]{3,2,1,0:T(8,128)S(1)}, f32[2,2,256,256]{3,2,1,0:T(8,128)S(1)}) custom-call(s32[1]{0:T(128)} %bitcast.1.place, f32[2,256,256]{2,1,0:T(8,128)S(1)} %get-tuple-element.16._.wave_in, bf16[6,256,256]{2,1,0:T(8,128)(2,1)S(1)} %copy-done, ...), custom_call_target="tpu_custom_call", output_to_operand_aliasing={{0}: (1, {})} | custom-call | tf_op jit(solution)/shard_map/pallas_call | solution.py:91
  20.8 0.0 copy-start.1
  20.8 0.0 copy-start.3
  20.8 0.0 collective-permute-done.4.refs_0_
  20.9 1.5 %collective-permute-done.5.refs_1_ = f32[128,256]{1,0:T(8,128)S(1)} collective-permute-done((f32[128,256]{1,0:T(8,128)S(1)}, f32[128,256]{1,0:T(8,128)S(1)}, u32[]{:S(2)}, u32[]{:S(2)}) %collective-permute-start.5) | collective-permute-done | bytes 131104 | tf_op jit(solution)/shard_map/ppermute | solution.py:324
  22.4 1.3 %shard_map.70 = (f32[2,256,256]{2,1,0:T(8,128)S(1)}, f32[4,2,256,256]{3,2,1,0:T(8,128)S(1)}) custom-call(s32[1]{0:T(128)} %bitcast.1.place, f32[2,256,256]{2,1,0:T(8,128)S(1)} %get-tuple-element.20.wave_in, bf16[6,256,256]{2,1,0:T(8,128)(2,1)S(1)} %copy-done, ...), custom_call_target="tpu_custom_call", output_to_operand_aliasing={{0}: (1, {}), {1}: (3, {})} | custom-call | tf_op jit(solution)/shard_map/pallas_call | solution.py:91
  23.7 0.8 %collective-permute-done.6.refs_1_ = f32[128,256]{1,0:T(8,128)S(1)} collective-permute-done((f32[128,256]{1,0:T(8,128)S(1)}, f32[128,256]{1,0:T(8,128)S(1)}, u32[]{:S(2)}, u32[]{:S(2)}) %collective-permute-start.6) | collective-permute-done | bytes 131104 | tf_op jit(solution)/shard_map/ppermute | solution.py:324
  24.5 0.0 copy-done.1
  24.5 0.0 copy-done.3
  24.5 6.3 %shard_map.71 = (f32[2,128,256]{2,1,0:T(8,128)S(1)}, f32[2,128,256]{2,1,0:T(8,128)S(1)}, f32[4,2,256,256]{3,2,1,0:T(8,128)S(1)}, f32[2,2,256,256]{3,2,1,0:T(8,128)S(1)}) custom-call(s32[1]{0:T(128)} %bitcast.1.place, f32[2,256,256]{2,1,0:T(8,128)S(1)} %get-tuple-element.22.wave_in, ...), custom_call_target="tpu_custom_call", output_to_operand_aliasing={{2}: (6, {}), {3}: (2, {})} | custom-call | tf_op jit(solution)/shard_map/pallas_call | solution.py:91
  30.8 0.1 collective-permute-start.8
  30.9 2.4 %collective-permute-start.7 = (f32[2,128,256]{2,1,0:T(8,128)S(1)}, f32[2,128,256]{2,1,0:T(8,128)S(1)}, u32[]{:S(2)}, u32[]{:S(2)}) collective-permute-start(f32[2,128,256]{2,1,0:T(8,128)S(1)} %get-tuple-element.25), channel_id=1, source_target_pairs={{0,30},{2,4},{4,2},{6,8},{8,6},{10,12},{12,10},{14,16},{16,14},{18... | collective-permute-start | bytes 786440 | tf_op jit(solution)/shard_map/ppermute | solution.py:314
  33.3 0.0 collective-permute-done.8.fast
  33.3 0.3 shard_map.72.staged
  33.6 5.9 %collective-permute-done.7.slow = f32[2,128,256]{2,1,0:T(8,128)S(1)} collective-permute-done((f32[2,128,256]{2,1,0:T(8,128)S(1)}, f32[2,128,256]{2,1,0:T(8,128)S(1)}, u32[]{:S(2)}, u32[]{:S(2)}) %collective-permute-start.7) | collective-permute-done | bytes 262176 | tf_op jit(solution)/shard_map/ppermute | solution.py:314
  39.5 1.1 %place.1 = f32[2,128,1024]{2,1,0:T(8,128)} custom-call(s32[1]{0:T(128)} %bitcast.parity, s32[1,2]{1,0:T(1,128)S(1)} %get-tuple-element.28.slow_position, f32[2,128,256]{2,1,0:T(8,128)S(1)} %collective-permute-done.7.slow, f32[2,128,1024]{2,1,0:T(8,128)S(1)} %shard_map.72.staged), custom_call_target="tpu_custom_call" | custom-call | tf_op jit(solution)/shard_map/place/pallas_call | solution.py:391
  (1 shorter events, 0.0 us)
Async XLA Ops:
  0.0 11.7 %copy-start.4 = (s32[1,2]{1,0:T(1,128)S(1)}, s32[1,2]{1,0:T(1,128)}, u32[]{:S(2)}) copy-start(s32[1,2]{1,0:T(1,128)} %position.7) | copy-start | bytes 28
  0.0 6.9 %collective-permute-start.1 = (s32[1,2]{1,0:T(1,128)}, s32[1,2]{1,0:T(1,128)S(1)}, u32[]{:S(2)}, u32[]{:S(2)}) collective-permute-start(s32[1,2]{1,0:T(1,128)} %position.7), channel_id=1, source_target_pairs={{0,2},{2,4},{4,6},{6,8},{8,10},{10,12},{12,14},{14,16},{16,18},{18... | collective-permute-start | bytes 32 | tf_op jit(solution)/shard_map/ppermute | solution.py:318
  0.5 6.5 %collective-permute-start = (s32[1,2]{1,0:T(1,128)}, s32[1,2]{1,0:T(1,128)S(1)}, u32[]{:S(2)}, u32[]{:S(2)}) collective-permute-start(s32[1,2]{1,0:T(1,128)} %position.7), channel_id=1, source_target_pairs={{0,30},{2,0},{4,2},{6,4},{8,6},{10,8},{12,10},{14,12},{16,14},{18,... | collective-permute-start | bytes 32 | tf_op jit(solution)/shard_map/ppermute | solution.py:318
  6.9 7.0 %copy-start = (bf16[6,256,256]{2,1,0:T(8,128)(2,1)S(1)}, bf16[6,256,256]{2,1,0:T(8,128)(2,1)}, u32[]{:S(2)}) copy-start(bf16[6,256,256]{2,1,0:T(8,128)(2,1)} %constant.14.clone._.prop) | copy-start | bytes 2359300
  6.9 6.9 %copy-start.2 = (f32[2,256,256]{2,1,0:T(8,128)S(1)}, f32[2,256,256]{2,1,0:T(8,128)}, u32[]{:S(2)}) copy-start(f32[2,256,256]{2,1,0:T(8,128)} %probe.1) | copy-start | bytes 1572868
  7.2 8.6 %collective-permute-start.2 = (f32[2,128,256]{2,1,0:T(8,128)S(1)}, f32[2,128,256]{2,1,0:T(8,128)S(1)}, u32[]{:S(2)}, u32[]{:S(2)}) collective-permute-start(f32[2,128,256]{2,1,0:T(8,128)S(1)} %shard_map.65.refs_0_), channel_id=1, source_target_pairs={{0,2},{2,4},{4,6},{6,8},{8,10},{10,12},{12,14},{14,16},{16,18},{18... | collective-permute-start | bytes 786440 | tf_op jit(solution)/shard_map/ppermute | solution.py:318
  7.2 8.6 %collective-permute-start.3 = (f32[2,128,256]{2,1,0:T(8,128)S(1)}, f32[2,128,256]{2,1,0:T(8,128)S(1)}, u32[]{:S(2)}, u32[]{:S(2)}) collective-permute-start(f32[2,128,256]{2,1,0:T(8,128)S(1)} %shard_map.64.refs_0_), channel_id=1, source_target_pairs={{0,30},{2,0},{4,2},{6,4},{8,6},{10,8},{12,10},{14,12},{16,14},{18,... | collective-permute-start | bytes 786440 | tf_op jit(solution)/shard_map/ppermute | solution.py:318
  11.8 9.0 %collective-permute-start.4 = (f32[2,128,256]{2,1,0:T(8,128)S(1)}, f32[2,128,256]{2,1,0:T(8,128)S(1)}, u32[]{:S(2)}, u32[]{:S(2)}) collective-permute-start(f32[2,128,256]{2,1,0:T(8,128)S(1)} %shard_map.66.own), channel_id=1, source_target_pairs={{0,1},{1,0},{2,3},{3,2},{4,5},{5,4},{6,7},{7,6},{8,9},{9,8},{10,11... | collective-permute-start | bytes 786440 | tf_op jit(solution)/shard_map/ppermute | solution.py:324
  15.9 6.4 %collective-permute-start.5 = (f32[128,256]{1,0:T(8,128)S(1)}, f32[128,256]{1,0:T(8,128)S(1)}, u32[]{:S(2)}, u32[]{:S(2)}) collective-permute-start(f32[128,256]{1,0:T(8,128)S(1)} %get-tuple-element.18.refs_0_), channel_id=1, source_target_pairs={{0,1},{1,0},{2,3},{3,2},{4,5},{5,4},{6,7},{7,6},{8,9},{9,8},{10,11... | collective-permute-start | bytes 393224 | tf_op jit(solution)/shard_map/ppermute | solution.py:324
  17.8 6.7 %collective-permute-start.6 = (f32[128,256]{1,0:T(8,128)S(1)}, f32[128,256]{1,0:T(8,128)S(1)}, u32[]{:S(2)}, u32[]{:S(2)}) collective-permute-start(f32[128,256]{1,0:T(8,128)S(1)} %get-tuple-element.19.refs_1_), channel_id=1, source_target_pairs={{0,1},{1,0},{2,3},{3,2},{4,5},{5,4},{6,7},{7,6},{8,9},{9,8},{10,11... | collective-permute-start | bytes 393224 | tf_op jit(solution)/shard_map/ppermute | solution.py:324
  20.8 3.7 %copy-start.1 = (bf16[6,256,256]{2,1,0:T(8,128)(2,1)S(1)}, bf16[6,256,256]{2,1,0:T(8,128)(2,1)}, u32[]{:S(2)}) copy-start(bf16[6,256,256]{2,1,0:T(8,128)(2,1)} %constant.15.clone.dft) | copy-start | bytes 2359300
  20.8 3.7 %copy-start.3 = (f32[1,256,256]{2,1,0:T(8,128)S(1)}, f32[1,256,256]{2,1,0:T(8,128)}, u32[]{:S(2)}) copy-start(f32[1,256,256]{2,1,0:T(8,128)} %intensity.1) | copy-start | bytes 786436
  30.8 2.5 %collective-permute-start.8 = (f32[2,128,256]{2,1,0:T(8,128)S(1)}, f32[2,128,256]{2,1,0:T(8,128)S(1)}, u32[]{:S(2)}, u32[]{:S(2)}) collective-permute-start(f32[2,128,256]{2,1,0:T(8,128)S(1)} %get-tuple-element.25), channel_id=1, source_target_pairs={{0,2},{2,0},{4,6},{6,4},{8,10},{10,8},{12,14},{14,12},{16,18},{18,... | collective-permute-start | bytes 786440 | tf_op jit(solution)/shard_map/ppermute | solution.py:315
  30.9 8.7 %collective-permute-start.7 = (f32[2,128,256]{2,1,0:T(8,128)S(1)}, f32[2,128,256]{2,1,0:T(8,128)S(1)}, u32[]{:S(2)}, u32[]{:S(2)}) collective-permute-start(f32[2,128,256]{2,1,0:T(8,128)S(1)} %get-tuple-element.25), channel_id=1, source_target_pairs={{0,30},{2,4},{4,2},{6,8},{8,6},{10,12},{12,10},{14,16},{16,14},{18... | collective-permute-start | bytes 786440 | tf_op jit(solution)/shard_map/ppermute | solution.py:314

commit v5 on v4

--- a/solution.py
+++ b/solution.py
@@ -118,22 +118,23 @@
             mask = covered(column, block, value.shape)
             next_value = potential[layer, :, block * extent : (block + 1) * extent]
             value = jnp.where(mask, next_value, value)
-        out[layer] = value
+        out[layer][...] = value
 
 
 def tile_kernel(potential, tile, sems):
-    layers, strip, _ = potential.shape
     copies = []
-    for k in range(8):
-        at = (k // (8 // layers), slice(k % (8 // layers) * strip * layers // 8, (k % (8 // layers) + 1) * strip * layers // 8))
-        copies.append(pltpu.make_async_copy(potential.at[at], tile.at[at], sems.at[k]))
-        copies[k].start()
+    for layer in range(potential.shape[0]):
+        copies.append(pltpu.make_async_copy(potential.at[layer], tile.at[layer], sems.at[layer]))
+        copies[layer].start()
     for copy in copies:
         copy.wait()
 
 
 def cut_kernel(position, tile, *refs):
-    fold_columns(tile, position, refs[-1])
+    layers = tile.shape[0]
+    whole = len(refs[-1].shape) == 3
+    outs = [refs[-1].at[layer] for layer in range(layers)] if whole else refs[-layers:]
+    fold_columns(tile, position, outs)
 
 
 def fill(table, slices, rows, piece):
@@ -148,13 +149,7 @@
     return [first + layer for layer in range(layers)]
 
 
-def outside(position, above, below):
-    row = lax.broadcasted_iota(jnp.int32, above.shape[1:], 0)
-    mask = row >= entry(position, 0) % above.shape[1]
-    return lambda layer: jnp.where(mask, above[layer], below[layer])
-
-
-def first_kernel(position, own, probe, _, upper, wave):
+def first_kernel(position, probe, _, own, upper, wave):
     layers, strip, _ = own.shape
     row_shift = position[0, 0] % strip + strip
     column_shift = position[0, 1] % (2 * strip)
@@ -163,10 +158,10 @@
     fill(upper, range(layers), slice(0, strip), lambda layer: own[layer])
 
 
-def merge_kernel(position, above, below, _, *out):
-    piece = outside(position, above, below)
-    for layer in range(above.shape[0]):
-        out[layer][...] = piece(layer)
+def merge_kernel(layer, position, above, below, _, out):
+    row = lax.broadcasted_iota(jnp.int32, above.shape, 0)
+    mask = row >= entry(position, 0) % above.shape[0]
+    out[...] = jnp.where(mask, above[...], below[layer])
 
 
 def transmit(trans, real, imag):
@@ -218,8 +213,8 @@
     depth = place[0]
     first = depth * layers
     for k in range(1, count):
-        own = refs[k - 1]
-        others = refs[count - 1 + (k - 1) * (layers - 1) : count - 1 + k * (layers - 1)]
+        own = refs[(k - 1) * layers]
+        others = refs[(k - 1) * layers + 1 : k * layers]
         owners = slices_of(depth, k, count, layers)[1:]
         fill(table, owners, slice(0, strip), lambda layer: own[layer + 1])
         fill(table, owners, slice(strip, extent), lambda layer: others[layer][...])
@@ -324,8 +319,8 @@
             out.append(lax.ppermute(x, "depth", pairs))
         return out
 
-    def cut(position, *after):
-        return call(cut_kernel, [half], [], [position, tile, *after])[0]
+    def cut(shapes, position, *after):
+        return call(cut_kernel, shapes, [], [position, tile, *after])
 
     place = lax.axis_index("depth").astype(jnp.int32).reshape(1)
     parity = (lax.axis_index("probe").astype(jnp.int32) & 1).reshape(1)
@@ -338,25 +333,34 @@
         out_shape=[pltpu.VMEM(potential.shape, f32)],
         in_specs=[ANY],
         out_specs=[VMEM],
-        scratch_shapes=[pltpu.SemaphoreType.DMA((8,))],
+        scratch_shapes=[pltpu.SemaphoreType.DMA((layers,))],
         name="tile",
     )(potential)
-    for_before = cut(before)
+
+    def by_layer(pieces, send):
+        out = []
+        for layer in range(layers):
+            out.append(send(pieces[layer]))
+        return out
+
+    (for_before,) = cut([half], before)
     below = step(for_before, -1)
-    for_after = cut(after, for_before)
-    above = step(for_after, 1)
-    own = cut(positions, for_after)
+    for_after = cut([half[1:]] * layers, after, for_before)
+    above = by_layer(for_after, lambda x: step(x, 1))
+    (own,) = cut([half], positions, *for_after)
     owns = to_depths(own)
     upper, wave = call(
         first_kernel,
         [(layers, 2, strip, extent), field],
         [positions],
-        [own, probe, prop],
-    )
-    other = call(merge_kernel, [half[1:]] * layers, [], [positions, above, below, wave])
-    others = []
+        [probe, prop, own],
+    )
+    other = []
     for layer in range(layers):
-        others.append(to_depths(other[layer]))
+        arrays = [positions, above[layer], below, wave]
+        kernel = functools.partial(merge_kernel, layer)
+        other += call(kernel, [half[1:]], [], arrays)
+    others = by_layer(other, to_depths)
     wave, table, saved = call(
         functools.partial(enter_kernel, layers),
         [field, (slices, *field), (layers, *field)],
@@ -371,12 +375,14 @@
         [wave, prop, table, *owns, *others[0]],
         aliases=[(0, 0), (2, 1)],
     )
-    rest = [others[layer][k] for k in range(depth_count - 1) for layer in range(1, layers)]
+    rest = []
+    for k in range(depth_count - 1):
+        rest += [owns[k], *[others[layer][k] for layer in range(1, layers)]]
     mine, outer, _, _ = call(
         functools.partial(solve_kernel, depth_count),
         [half, half, table.shape, saved.shape],
         [place],
-        [wave, saved, intensity, prop, dft, table, *owns, *rest],
+        [wave, saved, intensity, prop, dft, table, *rest],
         aliases=[(5, 2), (1, 3)],
     )
     odd = parity[0] == 1

time: 40.8 us -> 42.6 us (1.044)
  waiting for transfers between devices: 9.31 us -> 14.9 us
  starting transfers between devices: 16.5 us -> 12.6 us
    ppermute x4 -> x5, waiting for transfers between devices: 1.08 us -> 11 us  [step(): lax.ppermute(x, 'probe', [(i, (i + by) % count) for i in range(count)])]
    ppermute x4 -> x5, starting transfers between devices: 9.98 us -> 2.94 us  [step(): lax.ppermute(x, 'probe', [(i, (i + by) % count) for i in range(count)])]
    ppermute x3, waiting for transfers between devices: 2.3 us -> 0.01 us  [to_depths(): out.append(lax.ppermute(x, 'depth', pairs))]
    ppermute x1, waiting for transfers between devices: 5.93 us -> 3.96 us  [swapped(): slow = lax.ppermute(slow, 'probe', slow_pairs)]
    ppermute x1, starting transfers between devices: 2.39 us -> 4.35 us  [swapped(): slow = lax.ppermute(slow, 'probe', slow_pairs)]
    ppermute x3, starting transfers between devices: 4.09 us -> 5.27 us  [to_depths(): out.append(lax.ppermute(x, 'depth', pairs))]
    pallas_call x9 -> x10, Pallas kernels: 12.2 us -> 12.3 us  [call(): pl.pallas_call(kernel, out_shape=[pltpu.VMEM(shape, f32) for shape in res...]
  transfers between devices with their start and end apart: 9 -> 10, of which waited for: 4 -> 4; matrix products, arithmetic and copies ran while one was open for 0% -> 0% of each run, Pallas kernels for 17% -> 17%
where the time goes in v5:
time: 42.6 us; the launch traced here: 42.4 us
  waiting for transfers between devices  14.9 us (35%)
  Pallas kernels  14.6 us (34%)
  starting transfers between devices  12.6 us (30%)
    pallas_call x10, Pallas kernels, call(): pl.pallas_call(kernel, out_shape=[pltpu.VMEM(shape, f32) for shape in res...  12.3 us
    ppermute x5, waiting for transfers between devices, step(): lax.ppermute(x, 'probe', [(i, (i + by) % count) for i in range(count)])  11 us
    ppermute x3, starting transfers between devices, to_depths(): out.append(lax.ppermute(x, 'depth', pairs))  5.27 us
    ppermute x1, starting transfers between devices, swapped(): slow = lax.ppermute(slow, 'probe', slow_pairs)  4.35 us
    ppermute x1, waiting for transfers between devices, swapped(): slow = lax.ppermute(slow, 'probe', slow_pairs)  3.96 us
    ppermute x5, starting transfers between devices, step(): lax.ppermute(x, 'probe', [(i, (i + by) % count) for i in range(count)])  2.94 us
    pallas_call x1, Pallas kernels, local(): pl.pallas_call(tile_kernel, out_shape=[pltpu.VMEM(potential.shape, f32)],...  1.22 us
    pallas_call x1, Pallas kernels, local(): pl.pallas_call(place_kernel, out_shape=jax.ShapeDtypeStruct(potential.sha...  1.15 us
  transfers between devices with their start and end apart: 10, of which 4 were waited for; matrix products, arithmetic and copies ran while one was open for 0% of the time, Pallas kernels for 17%

profile of v5, /device:TPU:0, one launch (start us, length us, event | category | flops | bytes accessed | tf_op | source)
XLA Modules:
  0.0 42.4 jit_solution(86854891547294371)
XLA Ops:
  0.0 0.0 copy-start.4
  0.0 0.5 %collective-permute-start.1 = (s32[1,2]{1,0:T(1,128)}, s32[1,2]{1,0:T(1,128)S(1)}, u32[]{:S(2)}, u32[]{:S(2)}) collective-permute-start(s32[1,2]{1,0:T(1,128)} %position.9), channel_id=1, source_target_pairs={{0,2},{2,4},{4,6},{6,8},{8,10},{10,12},{12,14},{14,16},{16,18},{18... | collective-permute-start | bytes 32 | tf_op jit(solution)/shard_map/ppermute | solution.py:313
  0.5 1.2 %tile.1 = f32[2,128,1024]{2,1,0:T(8,128)S(1)} custom-call(f32[2,128,1024]{2,1,0:T(8,128)} %potential.1), custom_call_target="tpu_custom_call" | custom-call | tf_op jit(solution)/shard_map/tile/pallas_call | solution.py:331
  1.7 0.0 copy-start
  1.7 0.0 copy-start.2
  1.7 5.2 %collective-permute-done.1.position = s32[1,2]{1,0:T(1,128)S(1)} collective-permute-done((s32[1,2]{1,0:T(1,128)}, s32[1,2]{1,0:T(1,128)S(1)}, u32[]{:S(2)}, u32[]{:S(2)}) %collective-permute-start.1) | collective-permute-done | bytes 40 | tf_op jit(solution)/shard_map/ppermute | solution.py:313
  6.9 0.1 shard_map.64.refs_0_
  7.0 0.1 collective-permute-start.3
  7.1 0.0 copy-done.4
  7.1 2.3 %collective-permute-start = (s32[1,2]{1,0:T(1,128)S(1)}, s32[1,2]{1,0:T(1,128)S(1)}, u32[]{:S(2)}, u32[]{:S(2)}) collective-permute-start(s32[1,2]{1,0:T(1,128)S(1)} %copy-done.4), channel_id=1, source_target_pairs={{0,30},{2,0},{4,2},{6,4},{8,6},{10,8},{12,10},{14,12},{16,14},{18,... | collective-permute-start | bytes 32 | tf_op jit(solution)/shard_map/ppermute | solution.py:313
  9.4 1.6 %collective-permute-done.position = s32[1,2]{1,0:T(1,128)S(1)} collective-permute-done((s32[1,2]{1,0:T(1,128)S(1)}, s32[1,2]{1,0:T(1,128)S(1)}, u32[]{:S(2)}, u32[]{:S(2)}) %collective-permute-start) | collective-permute-done | bytes 40 | tf_op jit(solution)/shard_map/ppermute | solution.py:313
  11.0 0.1 shard_map.65
  11.2 0.1 collective-permute-start.2
  11.2 0.1 shard_map.66.own
  11.4 2.0 %collective-permute-start.5 = (f32[2,128,256]{2,1,0:T(8,128)S(1)}, f32[2,128,256]{2,1,0:T(8,128)S(1)}, u32[]{:S(2)}, u32[]{:S(2)}) collective-permute-start(f32[2,128,256]{2,1,0:T(8,128)S(1)} %shard_map.66.own), channel_id=1, source_target_pairs={{0,1},{1,0},{2,3},{3,2},{4,5},{5,4},{6,7},{7,6},{8,9},{9,8},{10,11... | collective-permute-start | bytes 786440 | tf_op jit(solution)/shard_map/ppermute | solution.py:319
  13.3 0.0 collective-permute-start.4
  13.3 0.0 copy-done
  13.4 0.0 copy-done.2
  13.4 1.0 %shard_map.67 = (f32[2,2,128,256]{3,2,1,0:T(8,128)S(1)}, f32[2,256,256]{2,1,0:T(8,128)S(1)}) custom-call(s32[1,2]{1,0:T(1,128)S(1)} %copy-done.4, f32[2,256,256]{2,1,0:T(8,128)S(1)} %copy-done.2, bf16[6,256,256]{2,1,0:T(8,128)(2,1)S(1)} %copy-done, f32[2,128,256]{2,1,0:T(8,128)S(1)} %shard_map.66.own), custom_call_target="tpu_custom_call" | custom-call | tf_op jit(solution)/shard_map/pallas_call | solution.py:91
  14.3 4.2 %collective-permute-done.2.above = f32[128,256]{1,0:T(8,128)S(1)} collective-permute-done((f32[128,256]{1,0:T(8,128)S(1)}, f32[128,256]{1,0:T(8,128)S(1)}, u32[]{:S(2)}, u32[]{:S(2)}) %collective-permute-start.2) | collective-permute-done | bytes 131104 | tf_op jit(solution)/shard_map/ppermute | solution.py:313
  18.5 0.0 collective-permute-done.3.below
  18.5 0.1 shard_map.68.refs_0_
  18.6 2.0 %collective-permute-start.6 = (f32[128,256]{1,0:T(8,128)S(1)}, f32[128,256]{1,0:T(8,128)S(1)}, u32[]{:S(2)}, u32[]{:S(2)}) collective-permute-start(f32[128,256]{1,0:T(8,128)S(1)} %shard_map.68.refs_0_), channel_id=1, source_target_pairs={{0,1},{1,0},{2,3},{3,2},{4,5},{5,4},{6,7},{7,6},{8,9},{9,8},{10,11... | collective-permute-start | bytes 393224 | tf_op jit(solution)/shard_map/ppermute | solution.py:319
  20.6 0.0 collective-permute-done.4.above
  20.6 0.1 shard_map.69.refs_1_
  20.7 1.3 %collective-permute-start.7 = (f32[128,256]{1,0:T(8,128)S(1)}, f32[128,256]{1,0:T(8,128)S(1)}, u32[]{:S(2)}, u32[]{:S(2)}) collective-permute-start(f32[128,256]{1,0:T(8,128)S(1)} %shard_map.69.refs_1_), channel_id=1, source_target_pairs={{0,1},{1,0},{2,3},{3,2},{4,5},{5,4},{6,7},{7,6},{8,9},{9,8},{10,11... | collective-permute-start | bytes 393224 | tf_op jit(solution)/shard_map/ppermute | solution.py:319
  22.0 2.8 %shard_map.70 = (f32[2,256,256]{2,1,0:T(8,128)S(1)}, f32[4,2,256,256]{3,2,1,0:T(8,128)S(1)}, f32[2,2,256,256]{3,2,1,0:T(8,128)S(1)}) custom-call(s32[1]{0:T(128)} %bitcast.1.place, f32[2,256,256]{2,1,0:T(8,128)S(1)} %get-tuple-element.18._.wave_in, bf16[6,256,256]{2,1,0:T(8,128)(2,1)S(1)} %copy-done, ...), custom_call_target="tpu_custom_call", output_to_operand_aliasing={{0}: (1, {})} | custom-call | tf_op jit(solution)/shard_map/pallas_call | solution.py:91
  24.8 0.0 copy-start.1
  24.8 0.0 copy-start.3
  24.8 0.0 collective-permute-done.5.refs_0_
  24.8 0.0 collective-permute-done.6.refs_1_
  24.8 1.3 %shard_map.71 = (f32[2,256,256]{2,1,0:T(8,128)S(1)}, f32[4,2,256,256]{3,2,1,0:T(8,128)S(1)}) custom-call(s32[1]{0:T(128)} %bitcast.1.place, f32[2,256,256]{2,1,0:T(8,128)S(1)} %get-tuple-element.20.wave_in, bf16[6,256,256]{2,1,0:T(8,128)(2,1)S(1)} %copy-done, ...), custom_call_target="tpu_custom_call", output_to_operand_aliasing={{0}: (1, {}), {1}: (3, {})} | custom-call | tf_op jit(solution)/shard_map/pallas_call | solution.py:91
  26.2 0.0 collective-permute-done.7.refs_1_
  26.2 0.0 copy-done.1
  26.2 0.0 copy-done.3
  26.2 6.3 %shard_map.72 = (f32[2,128,256]{2,1,0:T(8,128)S(1)}, f32[2,128,256]{2,1,0:T(8,128)S(1)}, f32[4,2,256,256]{3,2,1,0:T(8,128)S(1)}, f32[2,2,256,256]{3,2,1,0:T(8,128)S(1)}) custom-call(s32[1]{0:T(128)} %bitcast.1.place, f32[2,256,256]{2,1,0:T(8,128)S(1)} %get-tuple-element.22.wave_in, ...), custom_call_target="tpu_custom_call", output_to_operand_aliasing={{2}: (6, {}), {3}: (2, {})} | custom-call | tf_op jit(solution)/shard_map/pallas_call | solution.py:91
  32.5 0.1 collective-permute-start.9
  32.6 4.4 %collective-permute-start.8 = (f32[2,128,256]{2,1,0:T(8,128)S(1)}, f32[2,128,256]{2,1,0:T(8,128)S(1)}, u32[]{:S(2)}, u32[]{:S(2)}) collective-permute-start(f32[2,128,256]{2,1,0:T(8,128)S(1)} %get-tuple-element.25), channel_id=1, source_target_pairs={{0,30},{2,4},{4,2},{6,8},{8,6},{10,12},{12,10},{14,16},{16,14},{18... | collective-permute-start | bytes 786440 | tf_op jit(solution)/shard_map/ppermute | solution.py:309
  37.0 0.0 collective-permute-done.9.fast
  37.0 0.3 shard_map.73.staged
  37.3 4.0 %collective-permute-done.8.slow = f32[2,128,256]{2,1,0:T(8,128)S(1)} collective-permute-done((f32[2,128,256]{2,1,0:T(8,128)S(1)}, f32[2,128,256]{2,1,0:T(8,128)S(1)}, u32[]{:S(2)}, u32[]{:S(2)}) %collective-permute-start.8) | collective-permute-done | bytes 262176 | tf_op jit(solution)/shard_map/ppermute | solution.py:309
  41.3 1.1 %place.1 = f32[2,128,1024]{2,1,0:T(8,128)} custom-call(s32[1]{0:T(128)} %bitcast.parity, s32[1,2]{1,0:T(1,128)S(1)} %get-tuple-element.28.slow_position, f32[2,128,256]{2,1,0:T(8,128)S(1)} %collective-permute-done.8.slow, f32[2,128,1024]{2,1,0:T(8,128)S(1)} %shard_map.73.staged), custom_call_target="tpu_custom_call" | custom-call | tf_op jit(solution)/shard_map/place/pallas_call | solution.py:397
  (1 shorter events, 0.0 us)
Async XLA Ops:
  0.0 7.1 %copy-start.4 = (s32[1,2]{1,0:T(1,128)S(1)}, s32[1,2]{1,0:T(1,128)}, u32[]{:S(2)}) copy-start(s32[1,2]{1,0:T(1,128)} %position.9) | copy-start | bytes 28
  0.0 6.9 %collective-permute-start.1 = (s32[1,2]{1,0:T(1,128)}, s32[1,2]{1,0:T(1,128)S(1)}, u32[]{:S(2)}, u32[]{:S(2)}) collective-permute-start(s32[1,2]{1,0:T(1,128)} %position.9), channel_id=1, source_target_pairs={{0,2},{2,4},{4,6},{6,8},{8,10},{10,12},{12,14},{14,16},{16,18},{18... | collective-permute-start | bytes 32 | tf_op jit(solution)/shard_map/ppermute | solution.py:313
  1.7 11.6 %copy-start = (bf16[6,256,256]{2,1,0:T(8,128)(2,1)S(1)}, bf16[6,256,256]{2,1,0:T(8,128)(2,1)}, u32[]{:S(2)}) copy-start(bf16[6,256,256]{2,1,0:T(8,128)(2,1)} %constant.14.clone._.prop) | copy-start | bytes 2359300
  1.7 11.6 %copy-start.2 = (f32[2,256,256]{2,1,0:T(8,128)S(1)}, f32[2,256,256]{2,1,0:T(8,128)}, u32[]{:S(2)}) copy-start(f32[2,256,256]{2,1,0:T(8,128)} %probe.1) | copy-start | bytes 1572868
  7.0 11.5 %collective-permute-start.3 = (f32[2,128,256]{2,1,0:T(8,128)S(1)}, f32[2,128,256]{2,1,0:T(8,128)S(1)}, u32[]{:S(2)}, u32[]{:S(2)}) collective-permute-start(f32[2,128,256]{2,1,0:T(8,128)S(1)} %shard_map.64.refs_0_), channel_id=1, source_target_pairs={{0,30},{2,0},{4,2},{6,4},{8,6},{10,8},{12,10},{14,12},{16,14},{18,... | collective-permute-start | bytes 786440 | tf_op jit(solution)/shard_map/ppermute | solution.py:313
  7.1 3.9 %collective-permute-start = (s32[1,2]{1,0:T(1,128)S(1)}, s32[1,2]{1,0:T(1,128)S(1)}, u32[]{:S(2)}, u32[]{:S(2)}) collective-permute-start(s32[1,2]{1,0:T(1,128)S(1)} %copy-done.4), channel_id=1, source_target_pairs={{0,30},{2,0},{4,2},{6,4},{8,6},{10,8},{12,10},{14,12},{16,14},{18,... | collective-permute-start | bytes 32 | tf_op jit(solution)/shard_map/ppermute | solution.py:313
  11.2 7.4 %collective-permute-start.2 = (f32[128,256]{1,0:T(8,128)S(1)}, f32[128,256]{1,0:T(8,128)S(1)}, u32[]{:S(2)}, u32[]{:S(2)}) collective-permute-start(f32[128,256]{1,0:T(8,128)S(1)} %get-tuple-element.16.refs_0_), channel_id=1, source_target_pairs={{0,2},{2,4},{4,6},{6,8},{8,10},{10,12},{12,14},{14,16},{16,18},{18... | collective-permute-start | bytes 393224 | tf_op jit(solution)/shard_map/ppermute | solution.py:313
  11.4 13.5 %collective-permute-start.5 = (f32[2,128,256]{2,1,0:T(8,128)S(1)}, f32[2,128,256]{2,1,0:T(8,128)S(1)}, u32[]{:S(2)}, u32[]{:S(2)}) collective-permute-start(f32[2,128,256]{2,1,0:T(8,128)S(1)} %shard_map.66.own), channel_id=1, source_target_pairs={{0,1},{1,0},{2,3},{3,2},{4,5},{5,4},{6,7},{7,6},{8,9},{9,8},{10,11... | collective-permute-start | bytes 786440 | tf_op jit(solution)/shard_map/ppermute | solution.py:319
  13.3 7.3 %collective-permute-start.4 = (f32[128,256]{1,0:T(8,128)S(1)}, f32[128,256]{1,0:T(8,128)S(1)}, u32[]{:S(2)}, u32[]{:S(2)}) collective-permute-start(f32[128,256]{1,0:T(8,128)S(1)} %get-tuple-element.17.refs_1_), channel_id=1, source_target_pairs={{0,2},{2,4},{4,6},{6,8},{8,10},{10,12},{12,14},{14,16},{16,18},{18... | collective-permute-start | bytes 393224 | tf_op jit(solution)/shard_map/ppermute | solution.py:313
  18.6 6.2 %collective-permute-start.6 = (f32[128,256]{1,0:T(8,128)S(1)}, f32[128,256]{1,0:T(8,128)S(1)}, u32[]{:S(2)}, u32[]{:S(2)}) collective-permute-start(f32[128,256]{1,0:T(8,128)S(1)} %shard_map.68.refs_0_), channel_id=1, source_target_pairs={{0,1},{1,0},{2,3},{3,2},{4,5},{5,4},{6,7},{7,6},{8,9},{9,8},{10,11... | collective-permute-start | bytes 393224 | tf_op jit(solution)/shard_map/ppermute | solution.py:319
  20.7 5.5 %collective-permute-start.7 = (f32[128,256]{1,0:T(8,128)S(1)}, f32[128,256]{1,0:T(8,128)S(1)}, u32[]{:S(2)}, u32[]{:S(2)}) collective-permute-start(f32[128,256]{1,0:T(8,128)S(1)} %shard_map.69.refs_1_), channel_id=1, source_target_pairs={{0,1},{1,0},{2,3},{3,2},{4,5},{5,4},{6,7},{7,6},{8,9},{9,8},{10,11... | collective-permute-start | bytes 393224 | tf_op jit(solution)/shard_map/ppermute | solution.py:319
  24.8 1.4 %copy-start.1 = (bf16[6,256,256]{2,1,0:T(8,128)(2,1)S(1)}, bf16[6,256,256]{2,1,0:T(8,128)(2,1)}, u32[]{:S(2)}) copy-start(bf16[6,256,256]{2,1,0:T(8,128)(2,1)} %constant.15.clone.dft) | copy-start | bytes 2359300
  24.8 1.4 %copy-start.3 = (f32[1,256,256]{2,1,0:T(8,128)S(1)}, f32[1,256,256]{2,1,0:T(8,128)}, u32[]{:S(2)}) copy-start(f32[1,256,256]{2,1,0:T(8,128)} %intensity.1) | copy-start | bytes 786436
  32.5 4.4 %collective-permute-start.9 = (f32[2,128,256]{2,1,0:T(8,128)S(1)}, f32[2,128,256]{2,1,0:T(8,128)S(1)}, u32[]{:S(2)}, u32[]{:S(2)}) collective-permute-start(f32[2,128,256]{2,1,0:T(8,128)S(1)} %get-tuple-element.25), channel_id=1, source_target_pairs={{0,2},{2,0},{4,6},{6,4},{8,10},{10,8},{12,14},{14,12},{16,18},{18,... | collective-permute-start | bytes 786440 | tf_op jit(solution)/shard_map/ppermute | solution.py:310
  32.6 8.7 %collective-permute-start.8 = (f32[2,128,256]{2,1,0:T(8,128)S(1)}, f32[2,128,256]{2,1,0:T(8,128)S(1)}, u32[]{:S(2)}, u32[]{:S(2)}) collective-permute-start(f32[2,128,256]{2,1,0:T(8,128)S(1)} %get-tuple-element.25), channel_id=1, source_target_pairs={{0,30},{2,4},{4,2},{6,8},{8,6},{10,12},{12,10},{14,16},{16,14},{18... | collective-permute-start | bytes 786440 | tf_op jit(solution)/shard_map/ppermute | solution.py:309

commit v6 on v5

--- a/solution.py
+++ b/solution.py
@@ -7,6 +7,7 @@
 from jax.experimental import pallas as pl
 from jax.experimental.pallas import tpu as pltpu
 from jax.sharding import PartitionSpec as P
+
 
 interaction = 0.5
 fresnel_phase = 60.0
@@ -205,54 +206,63 @@
     wave_out[0], wave_out[1] = sandwich(prop, *wave)
 
 
-def solve_kernel(count, place, wave_in, saved_in, intensity, prop, dft, table_in, *refs):
+def solve_kernel(count, turn, place, parity, wave_in, saved_in, intensity, prop, dft, table_in, *refs):
     mine, outer, table, saved = refs[-4:]
-    layers, strip, extent = mine.shape
-    slices = layers * count
-    last = slices - 1
-    depth = place[0]
-    first = depth * layers
-    for k in range(1, count):
-        own = refs[(k - 1) * layers]
-        others = refs[(k - 1) * layers + 1 : k * layers]
-        owners = slices_of(depth, k, count, layers)[1:]
-        fill(table, owners, slice(0, strip), lambda layer: own[layer + 1])
-        fill(table, owners, slice(strip, extent), lambda layer: others[layer][...])
-
-    def enter(s, wave):
-        wave = transmit((table[s, 0], table[s, 1]), *wave)
-
-        @pl.when((s >= first) & (s < first + layers))
+    if turn == 0:
+        before = refs[-5]
+
+        @pl.when(parity[0] != turn)
         def _():
-            saved[s - first, 0] = wave[0]
-            saved[s - first, 1] = wave[1]
-
-        return wave
-
-    wave = (wave_in[0], wave_in[1])
-    start = jnp.where(depth == 0, layers + 1, 1)
-    wave = lax.fori_loop(start, last, lambda s, w: sandwich(prop, *enter(s, w)), wave)
-    far_real, far_imag = sandwich(dft, *enter(last, wave))
-    misfit = far_real * far_real + far_imag * far_imag - intensity[0]
-    wave = sandwich(dft, misfit * far_real, -(misfit * far_imag))
-
-    def term(s, wave):
-        @pl.when(s < first + layers)
-        def _():
-            value = wave[1] * saved[s - first, 0] + wave[0] * saved[s - first, 1]
-            value = -interaction * value
-            mine[s - first] = value[:strip]
-            outer[s - first] = value[strip:]
-
-    term(last, wave)
-
-    def backward(step, wave):
-        s = last - step
-        wave = sandwich(prop, *transmit((table[s, 0], table[s, 1]), *wave))
-        term(s - 1, wave)
-        return wave
-
-    lax.fori_loop(0, last - first, backward, wave)
+            outer[...] = before[...]
+
+    @pl.when(parity[0] == turn)
+    def _():
+        layers, strip, extent = mine.shape
+        slices = layers * count
+        last = slices - 1
+        depth = place[0]
+        first = depth * layers
+        for k in range(1, count):
+            own = refs[(k - 1) * layers]
+            others = refs[(k - 1) * layers + 1 : k * layers]
+            owners = slices_of(depth, k, count, layers)[1:]
+            fill(table, owners, slice(0, strip), lambda layer: own[layer + 1])
+            fill(table, owners, slice(strip, extent), lambda layer: others[layer][...])
+
+        def enter(s, wave):
+            wave = transmit((table[s, 0], table[s, 1]), *wave)
+
+            @pl.when((s >= first) & (s < first + layers))
+            def _():
+                saved[s - first, 0] = wave[0]
+                saved[s - first, 1] = wave[1]
+
+            return wave
+
+        wave = (wave_in[0], wave_in[1])
+        start = jnp.where(depth == 0, layers + 1, 1)
+        wave = lax.fori_loop(start, last, lambda s, w: sandwich(prop, *enter(s, w)), wave)
+        far_real, far_imag = sandwich(dft, *enter(last, wave))
+        misfit = far_real * far_real + far_imag * far_imag - intensity[0]
+        wave = sandwich(dft, misfit * far_real, -(misfit * far_imag))
+
+        def term(s, wave):
+            @pl.when(s < first + layers)
+            def _():
+                value = wave[1] * saved[s - first, 0] + wave[0] * saved[s - first, 1]
+                value = -interaction * value
+                mine[s - first] = value[:strip]
+                outer[s - first] = value[strip:]
+
+        term(last, wave)
+
+        def backward(step, wave):
+            s = last - step
+            wave = sandwich(prop, *transmit((table[s, 0], table[s, 1]), *wave))
+            term(s - 1, wave)
+            return wave
+
+        lax.fori_loop(0, last - first, backward, wave)
 
 
 def covers(position, block, shape, odd):
@@ -275,9 +285,10 @@
             staged[layer, :, at] = value
 
 
-def place_kernel(parity, slow_position, slow, staged, out, final, sems):
+def place_kernel(parity, slow_position, from_odd, from_even, staged, out, final, sems):
     layers, strip, columns = out.shape
     extent = 2 * strip
+    slow = [from_odd[layer] + from_even[layer] for layer in range(layers)]
     copies = []
     for block in range(columns // extent):
         at = slice(block * extent, (block + 1) * extent)
@@ -305,10 +316,6 @@
     fast_pairs = [(i, i ^ 1) for i in range(count)]
     slow_pairs = [(i, (i + 1 if i % 2 else i - 1) % count) for i in range(count)]
 
-    def swapped(fast, slow):
-        slow = lax.ppermute(slow, "probe", slow_pairs)
-        return lax.ppermute(fast, "probe", fast_pairs), slow
-
     def step(x, by):
         return lax.ppermute(x, "probe", [(i, (i + by) % count) for i in range(count)])
 
@@ -345,10 +352,10 @@
 
     (for_before,) = cut([half], before)
     below = step(for_before, -1)
-    for_after = cut([half[1:]] * layers, after, for_before)
+    (own,) = cut([half], positions, for_before)
+    owns = to_depths(own)
+    for_after = cut([half[1:]] * layers, after, own)
     above = by_layer(for_after, lambda x: step(x, 1))
-    (own,) = cut([half], positions, *for_after)
-    owns = to_depths(own)
     upper, wave = call(
         first_kernel,
         [(layers, 2, strip, extent), field],
@@ -378,26 +385,37 @@
     rest = []
     for k in range(depth_count - 1):
         rest += [owns[k], *[others[layer][k] for layer in range(1, layers)]]
-    mine, outer, _, _ = call(
-        functools.partial(solve_kernel, depth_count),
-        [half, half, table.shape, saved.shape],
-        [place],
-        [wave, saved, intensity, prop, dft, table, *rest],
-        aliases=[(5, 2), (1, 3)],
-    )
+
+    def solve(turn, table, saved, *earlier):
+        rest_refs = 6 + len(rest)
+        return call(
+            functools.partial(solve_kernel, depth_count, turn),
+            [half, half, table.shape, saved.shape],
+            [place, parity],
+            [wave, saved, intensity, prop, dft, table, *rest, *earlier],
+            aliases=[(5, 2), (1, 3)] + ([(rest_refs, 0)] if earlier else []),
+            limit=4 * (depth_count - 1),
+        )
+
+    odd_groups = [(i, j) for i, j in slow_pairs if i % 2 == 1]
+    even_groups = [(i, j) for i, j in slow_pairs if i % 2 == 0]
+    mine, outer, table, saved = solve(1, table, saved)
+    from_odd = lax.ppermute(outer, "probe", odd_groups)
+    mine, outer, _, _ = solve(0, table, saved, mine, outer)
+    from_even = lax.ppermute(outer, "probe", even_groups)
+    fast = lax.ppermute(outer, "probe", fast_pairs)
     odd = parity[0] == 1
     fast_position = jnp.where(odd, before, after)
     slow_position = jnp.where(odd, after, before)
-    fast, slow = swapped(outer, outer)
     (staged,) = call(
         stage_kernel, [potential.shape], [parity], [positions, fast_position, mine, fast]
     )
-    arrays = [slow_position, slow, staged]
+    arrays = [slow_position, from_odd, from_even, staged]
     arrays = [pltpu.with_memory_space_constraint(x, pltpu.VMEM) for x in arrays]
     return pl.pallas_call(
         place_kernel,
         out_shape=jax.ShapeDtypeStruct(potential.shape, f32),
-        in_specs=[SMEM] + [VMEM] * 3,
+        in_specs=[SMEM] + [VMEM] * 4,
         out_specs=ANY,
         scratch_shapes=[
             pltpu.VMEM(potential.shape, f32),

time: 42.6 us -> 50.5 us (1.19)
  waiting for transfers between devices: 14.9 us -> 19.7 us
  starting transfers between devices: 12.6 us -> 15.7 us
    ppermute x2 -> x3, waiting for transfers between devices: 3.97 us -> 8.73 us  [the longest x1 6.53 us: local(): from_odd = lax.ppermute(outer, 'probe', odd_groups)]
    ppermute x2 -> x3, starting transfers between devices: 4.42 us -> 7.45 us  [the longest x1 6.08 us: local(): from_even = lax.ppermute(outer, 'probe', even_groups)]
    pallas_call x10 -> x11, Pallas kernels: 12.3 us -> 12.3 us  [call(): pl.pallas_call(kernel, out_shape=[pltpu.VMEM(shape, f32) for shape in res...]
  transfers between devices with their start and end apart: 10 -> 11, of which waited for: 4 -> 5; matrix products, arithmetic and copies ran while one was open for 0% -> 0% of each run, Pallas kernels for 17% -> 14%
where the time goes in v6:
time: 50.5 us; the launch traced here: 50.3 us
  waiting for transfers between devices  19.7 us (39%)
  starting transfers between devices  15.7 us (31%)
  Pallas kernels  14.7 us (29%)
    pallas_call x11, Pallas kernels, call(): pl.pallas_call(kernel, out_shape=[pltpu.VMEM(shape, f32) for shape in res...  12.3 us
    ppermute x5, waiting for transfers between devices, step(): lax.ppermute(x, 'probe', [(i, (i + by) % count) for i in range(count)])  11 us
    ppermute x1, waiting for transfers between devices, local(): from_odd = lax.ppermute(outer, 'probe', odd_groups)  6.53 us
    ppermute x1, starting transfers between devices, local(): from_even = lax.ppermute(outer, 'probe', even_groups)  6.08 us
    ppermute x3, starting transfers between devices, to_depths(): out.append(lax.ppermute(x, 'depth', pairs))  5.27 us
    ppermute x5, starting transfers between devices, step(): lax.ppermute(x, 'probe', [(i, (i + by) % count) for i in range(count)])  2.94 us
    ppermute x1, waiting for transfers between devices, local(): from_even = lax.ppermute(outer, 'probe', even_groups)  2.19 us
    ppermute x1, starting transfers between devices, local(): from_odd = lax.ppermute(outer, 'probe', odd_groups)  1.29 us
  transfers between devices with their start and end apart: 11, of which 5 were waited for; matrix products, arithmetic and copies ran while one was open for 0% of the time, Pallas kernels for 14%

profile of v6, /device:TPU:0, one launch (start us, length us, event | category | flops | bytes accessed | tf_op | source)
XLA Modules:
  0.0 50.3 jit_solution(9042812488660096837)
XLA Ops:
  0.0 0.0 copy-start.4
  0.0 0.5 collective-permute-start.1
  0.5 1.2 %tile.1 = f32[2,128,1024]{2,1,0:T(8,128)S(1)} custom-call(f32[2,128,1024]{2,1,0:T(8,128)} %potential.1), custom_call_target="tpu_custom_call" | custom-call | tf_op jit(solution)/shard_map/tile/pallas_call | solution.py:338
  1.7 0.0 copy-start
  1.7 0.0 copy-start.3
  1.7 5.2 %collective-permute-done.1.position = s32[1,2]{1,0:T(1,128)S(1)} collective-permute-done((s32[1,2]{1,0:T(1,128)}, s32[1,2]{1,0:T(1,128)S(1)}, u32[]{:S(2)}, u32[]{:S(2)}) %collective-permute-start.1) | collective-permute-done | bytes 40 | tf_op jit(solution)/shard_map/ppermute | solution.py:320
  6.9 0.1 shard_map.64.refs_0_
  7.0 0.1 collective-permute-start.3
  7.1 0.0 copy-done.4
  7.1 2.3 %collective-permute-start = (s32[1,2]{1,0:T(1,128)S(1)}, s32[1,2]{1,0:T(1,128)S(1)}, u32[]{:S(2)}, u32[]{:S(2)}) collective-permute-start(s32[1,2]{1,0:T(1,128)S(1)} %copy-done.4), channel_id=1, source_target_pairs={{0,30},{2,0},{4,2},{6,4},{8,6},{10,8},{12,10},{14,12},{16,14},{18,... | collective-permute-start | bytes 32 | tf_op jit(solution)/shard_map/ppermute | solution.py:320
  9.4 0.1 shard_map.65.own.refs_0_
  9.6 1.5 %collective-permute-done.position = s32[1,2]{1,0:T(1,128)S(1)} collective-permute-done((s32[1,2]{1,0:T(1,128)S(1)}, s32[1,2]{1,0:T(1,128)S(1)}, u32[]{:S(2)}, u32[]{:S(2)}) %collective-permute-start) | collective-permute-done | bytes 40 | tf_op jit(solution)/shard_map/ppermute | solution.py:320
  11.0 0.1 shard_map.67
  11.2 0.1 collective-permute-start.2
  11.2 2.0 %collective-permute-start.5 = (f32[2,128,256]{2,1,0:T(8,128)S(1)}, f32[2,128,256]{2,1,0:T(8,128)S(1)}, u32[]{:S(2)}, u32[]{:S(2)}) collective-permute-start(f32[2,128,256]{2,1,0:T(8,128)S(1)} %shard_map.65.own.refs_0_), channel_id=1, source_target_pairs={{0,1},{1,0},{2,3},{3,2},{4,5},{5,4},{6,7},{7,6},{8,9},{9,8},{10,11... | collective-permute-start | bytes 786440 | tf_op jit(solution)/shard_map/ppermute | solution.py:326
  13.2 0.0 collective-permute-start.4
  13.2 0.0 copy-done
  13.2 0.0 copy-done.3
  13.2 1.0 %shard_map.66 = (f32[2,2,128,256]{3,2,1,0:T(8,128)S(1)}, f32[2,256,256]{2,1,0:T(8,128)S(1)}) custom-call(s32[1,2]{1,0:T(1,128)S(1)} %copy-done.4, f32[2,256,256]{2,1,0:T(8,128)S(1)} %copy-done.3, bf16[6,256,256]{2,1,0:T(8,128)(2,1)S(1)} %copy-done, f32[2,128,256]{2,1,0:T(8,128)S(1)} %shard_map.65.own.refs_0_), custom_call_target="tpu_custom_call" | custom-call | tf_op jit(solution)/shard_map/pallas_call | solution.py:92
  14.2 4.3 %collective-permute-done.2.above = f32[128,256]{1,0:T(8,128)S(1)} collective-permute-done((f32[128,256]{1,0:T(8,128)S(1)}, f32[128,256]{1,0:T(8,128)S(1)}, u32[]{:S(2)}, u32[]{:S(2)}) %collective-permute-start.2) | collective-permute-done | bytes 131104 | tf_op jit(solution)/shard_map/ppermute | solution.py:320
  18.5 0.0 collective-permute-done.3.below
  18.5 0.1 shard_map.68.refs_0_
  18.6 2.0 %collective-permute-start.6 = (f32[128,256]{1,0:T(8,128)S(1)}, f32[128,256]{1,0:T(8,128)S(1)}, u32[]{:S(2)}, u32[]{:S(2)}) collective-permute-start(f32[128,256]{1,0:T(8,128)S(1)} %shard_map.68.refs_0_), channel_id=1, source_target_pairs={{0,1},{1,0},{2,3},{3,2},{4,5},{5,4},{6,7},{7,6},{8,9},{9,8},{10,11... | collective-permute-start | bytes 393224 | tf_op jit(solution)/shard_map/ppermute | solution.py:326
  20.6 0.0 collective-permute-done.4.above
  20.6 0.1 shard_map.69.refs_1_
  20.7 1.3 %collective-permute-start.7 = (f32[128,256]{1,0:T(8,128)S(1)}, f32[128,256]{1,0:T(8,128)S(1)}, u32[]{:S(2)}, u32[]{:S(2)}) collective-permute-start(f32[128,256]{1,0:T(8,128)S(1)} %shard_map.69.refs_1_), channel_id=1, source_target_pairs={{0,1},{1,0},{2,3},{3,2},{4,5},{5,4},{6,7},{7,6},{8,9},{9,8},{10,11... | collective-permute-start | bytes 393224 | tf_op jit(solution)/shard_map/ppermute | solution.py:326
  22.0 2.8 %shard_map.70 = (f32[2,256,256]{2,1,0:T(8,128)S(1)}, f32[4,2,256,256]{3,2,1,0:T(8,128)S(1)}, f32[2,2,256,256]{3,2,1,0:T(8,128)S(1)}) custom-call(s32[1]{0:T(128)} %bitcast.1.place, f32[2,256,256]{2,1,0:T(8,128)S(1)} %get-tuple-element.20._.wave_in, bf16[6,256,256]{2,1,0:T(8,128)(2,1)S(1)} %copy-done, ...), custom_call_target="tpu_custom_call", output_to_operand_aliasing={{0}: (1, {})} | custom-call | tf_op jit(solution)/shard_map/pallas_call | solution.py:92
  24.8 0.0 copy-start.1
  24.8 0.0 copy-start.2
  24.8 0.0 collective-permute-done.5.refs_0_
  24.9 0.0 collective-permute-done.6.refs_1_
  24.9 1.3 %shard_map.71 = (f32[2,256,256]{2,1,0:T(8,128)S(1)}, f32[4,2,256,256]{3,2,1,0:T(8,128)S(1)}) custom-call(s32[1]{0:T(128)} %bitcast.1.place, f32[2,256,256]{2,1,0:T(8,128)S(1)} %get-tuple-element.24.wave_in, bf16[6,256,256]{2,1,0:T(8,128)(2,1)S(1)} %copy-done, ...), custom_call_target="tpu_custom_call", output_to_operand_aliasing={{0}: (1, {}), {1}: (3, {})} | custom-call | tf_op jit(solution)/shard_map/pallas_call | solution.py:92
  26.2 0.0 collective-permute-done.7.refs_1_
  26.2 0.0 copy-done.1
  26.2 0.0 copy-done.2
  26.3 6.3 %shard_map.73 = (f32[2,128,256]{2,1,0:T(8,128)S(1)}, f32[2,128,256]{2,1,0:T(8,128)S(1)}, f32[4,2,256,256]{3,2,1,0:T(8,128)S(1)}, f32[2,2,256,256]{3,2,1,0:T(8,128)S(1)}) custom-call(s32[1]{0:T(128)} %bitcast.1.place, s32[1]{0:T(128)} %bitcast.parity, ...), custom_call_target="tpu_custom_call", output_to_operand_aliasing={{2}: (7, {}), {3}: (3, {}), {0}: (10, {})} | custom-call | tf_op jit(solution)/shard_map/pallas_call | solution.py:92
  32.6 0.1 collective-permute-start.10
  32.7 6.1 %collective-permute-start.9 = (f32[2,128,256]{2,1,0:T(8,128)S(1)}, f32[2,128,256]{2,1,0:T(8,128)S(1)}, u32[]{:S(2)}, u32[]{:S(2)}) collective-permute-start(f32[2,128,256]{2,1,0:T(8,128)S(1)} %get-tuple-element.33), channel_id=1, source_target_pairs={{0,30},{4,2},{8,6},{12,10},{16,14},{20,18},{24,22},{28,26},{1,31},... | collective-permute-start | bytes 786440 | tf_op jit(solution)/shard_map/ppermute | solution.py:405
  38.8 1.3 %collective-permute-start.8 = (f32[2,128,256]{2,1,0:T(8,128)S(1)}, f32[2,128,256]{2,1,0:T(8,128)S(1)}, u32[]{:S(2)}, u32[]{:S(2)}) collective-permute-start(f32[2,128,256]{2,1,0:T(8,128)S(1)} %get-tuple-element.29.refs_3_), channel_id=1, source_target_pairs={{2,4},{6,8},{10,12},{14,16},{18,20},{22,24},{26,28},{30,0},{3,5},{... | collective-permute-start | bytes 786440 | tf_op jit(solution)/shard_map/ppermute | solution.py:403
  40.1 0.0 collective-permute-done.10.fast
  40.1 0.3 shard_map.74.staged
  40.4 2.2 %collective-permute-done.9.from_even = f32[2,128,256]{2,1,0:T(8,128)S(1)} collective-permute-done((f32[2,128,256]{2,1,0:T(8,128)S(1)}, f32[2,128,256]{2,1,0:T(8,128)S(1)}, u32[]{:S(2)}, u32[]{:S(2)}) %collective-permute-start.9) | collective-permute-done | bytes 262176 | tf_op jit(solution)/shard_map/ppermute | solution.py:405
  42.6 6.5 %collective-permute-done.8.from_odd = f32[2,128,256]{2,1,0:T(8,128)S(1)} collective-permute-done((f32[2,128,256]{2,1,0:T(8,128)S(1)}, f32[2,128,256]{2,1,0:T(8,128)S(1)}, u32[]{:S(2)}, u32[]{:S(2)}) %collective-permute-start.8) | collective-permute-done | bytes 262176 | tf_op jit(solution)/shard_map/ppermute | solution.py:403
  49.2 1.1 %place.1 = f32[2,128,1024]{2,1,0:T(8,128)} custom-call(s32[1]{0:T(128)} %bitcast.parity, s32[1,2]{1,0:T(1,128)S(1)} %get-tuple-element.36.slow_position, f32[2,128,256]{2,1,0:T(8,128)S(1)} %collective-permute-done.8.from_odd, f32[2,128,256]{2,1,0:T(8,128)S(1)} %collective-permute-done.9.from_even, f32[2,128,1024]{2,1,0:T(8,128)S(1)} %shard_map.74.staged), custom_call_target="tpu_custom_call" | custom-call | tf_op jit(solution)/shard_map/place/pallas_call | solution.py:415
  (2 shorter events, 0.0 us)
Async XLA Ops:
  0.0 7.1 %copy-start.4 = (s32[1,2]{1,0:T(1,128)S(1)}, s32[1,2]{1,0:T(1,128)}, u32[]{:S(2)}) copy-start(s32[1,2]{1,0:T(1,128)} %position.9) | copy-start | bytes 28
  0.0 6.9 %collective-permute-start.1 = (s32[1,2]{1,0:T(1,128)}, s32[1,2]{1,0:T(1,128)S(1)}, u32[]{:S(2)}, u32[]{:S(2)}) collective-permute-start(s32[1,2]{1,0:T(1,128)} %position.9), channel_id=1, source_target_pairs={{0,2},{2,4},{4,6},{6,8},{8,10},{10,12},{12,14},{14,16},{16,18},{18... | collective-permute-start | bytes 32 | tf_op jit(solution)/shard_map/ppermute | solution.py:320
  1.7 11.5 %copy-start = (bf16[6,256,256]{2,1,0:T(8,128)(2,1)S(1)}, bf16[6,256,256]{2,1,0:T(8,128)(2,1)}, u32[]{:S(2)}) copy-start(bf16[6,256,256]{2,1,0:T(8,128)(2,1)} %constant.14.clone._.prop) | copy-start | bytes 2359300
  1.7 11.5 %copy-start.3 = (f32[2,256,256]{2,1,0:T(8,128)S(1)}, f32[2,256,256]{2,1,0:T(8,128)}, u32[]{:S(2)}) copy-start(f32[2,256,256]{2,1,0:T(8,128)} %probe.1) | copy-start | bytes 1572868
  7.0 11.5 %collective-permute-start.3 = (f32[2,128,256]{2,1,0:T(8,128)S(1)}, f32[2,128,256]{2,1,0:T(8,128)S(1)}, u32[]{:S(2)}, u32[]{:S(2)}) collective-permute-start(f32[2,128,256]{2,1,0:T(8,128)S(1)} %shard_map.64.refs_0_), channel_id=1, source_target_pairs={{0,30},{2,0},{4,2},{6,4},{8,6},{10,8},{12,10},{14,12},{16,14},{18,... | collective-permute-start | bytes 786440 | tf_op jit(solution)/shard_map/ppermute | solution.py:320
  7.1 3.9 %collective-permute-start = (s32[1,2]{1,0:T(1,128)S(1)}, s32[1,2]{1,0:T(1,128)S(1)}, u32[]{:S(2)}, u32[]{:S(2)}) collective-permute-start(s32[1,2]{1,0:T(1,128)S(1)} %copy-done.4), channel_id=1, source_target_pairs={{0,30},{2,0},{4,2},{6,4},{8,6},{10,8},{12,10},{14,12},{16,14},{18,... | collective-permute-start | bytes 32 | tf_op jit(solution)/shard_map/ppermute | solution.py:320
  11.2 7.4 %collective-permute-start.2 = (f32[128,256]{1,0:T(8,128)S(1)}, f32[128,256]{1,0:T(8,128)S(1)}, u32[]{:S(2)}, u32[]{:S(2)}) collective-permute-start(f32[128,256]{1,0:T(8,128)S(1)} %get-tuple-element.22), channel_id=1, source_target_pairs={{0,2},{2,4},{4,6},{6,8},{8,10},{10,12},{12,14},{14,16},{16,18},{18... | collective-permute-start | bytes 393224 | tf_op jit(solution)/shard_map/ppermute | solution.py:320
  11.2 13.6 %collective-permute-start.5 = (f32[2,128,256]{2,1,0:T(8,128)S(1)}, f32[2,128,256]{2,1,0:T(8,128)S(1)}, u32[]{:S(2)}, u32[]{:S(2)}) collective-permute-start(f32[2,128,256]{2,1,0:T(8,128)S(1)} %shard_map.65.own.refs_0_), channel_id=1, source_target_pairs={{0,1},{1,0},{2,3},{3,2},{4,5},{5,4},{6,7},{7,6},{8,9},{9,8},{10,11... | collective-permute-start | bytes 786440 | tf_op jit(solution)/shard_map/ppermute | solution.py:326
  13.2 7.4 %collective-permute-start.4 = (f32[128,256]{1,0:T(8,128)S(1)}, f32[128,256]{1,0:T(8,128)S(1)}, u32[]{:S(2)}, u32[]{:S(2)}) collective-permute-start(f32[128,256]{1,0:T(8,128)S(1)} %get-tuple-element.23), channel_id=1, source_target_pairs={{0,2},{2,4},{4,6},{6,8},{8,10},{10,12},{12,14},{14,16},{16,18},{18... | collective-permute-start | bytes 393224 | tf_op jit(solution)/shard_map/ppermute | solution.py:320
  18.6 6.2 %collective-permute-start.6 = (f32[128,256]{1,0:T(8,128)S(1)}, f32[128,256]{1,0:T(8,128)S(1)}, u32[]{:S(2)}, u32[]{:S(2)}) collective-permute-start(f32[128,256]{1,0:T(8,128)S(1)} %shard_map.68.refs_0_), channel_id=1, source_target_pairs={{0,1},{1,0},{2,3},{3,2},{4,5},{5,4},{6,7},{7,6},{8,9},{9,8},{10,11... | collective-permute-start | bytes 393224 | tf_op jit(solution)/shard_map/ppermute | solution.py:326
  20.7 5.5 %collective-permute-start.7 = (f32[128,256]{1,0:T(8,128)S(1)}, f32[128,256]{1,0:T(8,128)S(1)}, u32[]{:S(2)}, u32[]{:S(2)}) collective-permute-start(f32[128,256]{1,0:T(8,128)S(1)} %shard_map.69.refs_1_), channel_id=1, source_target_pairs={{0,1},{1,0},{2,3},{3,2},{4,5},{5,4},{6,7},{7,6},{8,9},{9,8},{10,11... | collective-permute-start | bytes 393224 | tf_op jit(solution)/shard_map/ppermute | solution.py:326
  24.8 1.4 %copy-start.1 = (bf16[6,256,256]{2,1,0:T(8,128)(2,1)S(1)}, bf16[6,256,256]{2,1,0:T(8,128)(2,1)}, u32[]{:S(2)}) copy-start(bf16[6,256,256]{2,1,0:T(8,128)(2,1)} %constant.15.clone.dft) | copy-start | bytes 2359300
  24.8 1.4 %copy-start.2 = (f32[1,256,256]{2,1,0:T(8,128)S(1)}, f32[1,256,256]{2,1,0:T(8,128)}, u32[]{:S(2)}) copy-start(f32[1,256,256]{2,1,0:T(8,128)} %intensity.3) | copy-start | bytes 786436
  32.6 7.5 %collective-permute-start.10 = (f32[2,128,256]{2,1,0:T(8,128)S(1)}, f32[2,128,256]{2,1,0:T(8,128)S(1)}, u32[]{:S(2)}, u32[]{:S(2)}) collective-permute-start(f32[2,128,256]{2,1,0:T(8,128)S(1)} %get-tuple-element.33), channel_id=1, source_target_pairs={{0,2},{2,0},{4,6},{6,4},{8,10},{10,8},{12,14},{14,12},{16,18},{18,... | collective-permute-start | bytes 786440 | tf_op jit(solution)/shard_map/ppermute | solution.py:406
  32.7 9.9 %collective-permute-start.9 = (f32[2,128,256]{2,1,0:T(8,128)S(1)}, f32[2,128,256]{2,1,0:T(8,128)S(1)}, u32[]{:S(2)}, u32[]{:S(2)}) collective-permute-start(f32[2,128,256]{2,1,0:T(8,128)S(1)} %get-tuple-element.33), channel_id=1, source_target_pairs={{0,30},{4,2},{8,6},{12,10},{16,14},{20,18},{24,22},{28,26},{1,31},... | collective-permute-start | bytes 786440 | tf_op jit(solution)/shard_map/ppermute | solution.py:405
  38.8 10.4 %collective-permute-start.8 = (f32[2,128,256]{2,1,0:T(8,128)S(1)}, f32[2,128,256]{2,1,0:T(8,128)S(1)}, u32[]{:S(2)}, u32[]{:S(2)}) collective-permute-start(f32[2,128,256]{2,1,0:T(8,128)S(1)} %get-tuple-element.29.refs_3_), channel_id=1, source_target_pairs={{2,4},{6,8},{10,12},{14,16},{18,20},{22,24},{26,28},{30,0},{3,5},{... | collective-permute-start | bytes 786440 | tf_op jit(solution)/shard_map/ppermute | solution.py:403

commit v7 on v6

--- a/solution.py
+++ b/solution.py
@@ -288,7 +288,8 @@
 def place_kernel(parity, slow_position, from_odd, from_even, staged, out, final, sems):
     layers, strip, columns = out.shape
     extent = 2 * strip
-    slow = [from_odd[layer] + from_even[layer] for layer in range(layers)]
+    odd = jnp.broadcast_to(parity[0], (strip, extent)) == 1
+    slow = [jnp.where(odd, from_even[layer], from_odd[layer]) for layer in range(layers)]
     copies = []
     for block in range(columns // extent):
         at = slice(block * extent, (block + 1) * extent)
@@ -398,7 +399,7 @@
         )
 
     odd_groups = [(i, j) for i, j in slow_pairs if i % 2 == 1]
-    even_groups = [(i, j) for i, j in slow_pairs if i % 2 == 0]
+    even_groups = [fast_pairs[i] if i % 2 else slow_pairs[i] for i in range(count)]
     mine, outer, table, saved = solve(1, table, saved)
     from_odd = lax.ppermute(outer, "probe", odd_groups)
     mine, outer, _, _ = solve(0, table, saved, mine, outer)

time: 50.5 us -> 48.5 us (0.960)
  starting transfers between devices: 15.7 us -> 13.7 us
    ppermute x1, starting transfers between devices: 6.08 us -> 4.18 us  [local(): from_even = lax.ppermute(outer, 'probe', even_groups)]
  transfers between devices with their start and end apart: 11 -> 11, of which waited for: 5 -> 5; matrix products, arithmetic and copies ran while one was open for 0% -> 0% of each run, Pallas kernels for 14% -> 15%
where the time goes in v7:
time: 48.5 us; the launch traced here: 48.4 us
  waiting for transfers between devices  19.7 us (41%)
  Pallas kernels  14.7 us (30%)
  starting transfers between devices  13.7 us (28%)
    pallas_call x11, Pallas kernels, call(): pl.pallas_call(kernel, out_shape=[pltpu.VMEM(shape, f32) for shape in res...  12.3 us
    ppermute x5, waiting for transfers between devices, step(): lax.ppermute(x, 'probe', [(i, (i + by) % count) for i in range(count)])  11 us
    ppermute x1, waiting for transfers between devices, local(): from_odd = lax.ppermute(outer, 'probe', odd_groups)  6.48 us
    ppermute x3, starting transfers between devices, to_depths(): out.append(lax.ppermute(x, 'depth', pairs))  5.27 us
    ppermute x1, starting transfers between devices, local(): from_even = lax.ppermute(outer, 'probe', even_groups)  4.18 us
    ppermute x5, starting transfers between devices, step(): lax.ppermute(x, 'probe', [(i, (i + by) % count) for i in range(count)])  2.94 us
    ppermute x1, waiting for transfers between devices, local(): from_even = lax.ppermute(outer, 'probe', even_groups)  2.24 us
    ppermute x1, starting transfers between devices, local(): from_odd = lax.ppermute(outer, 'probe', odd_groups)  1.28 us
  transfers between devices with their start and end apart: 11, of which 5 were waited for; matrix products, arithmetic and copies ran while one was open for 0% of the time, Pallas kernels for 15%

profile of v7, /device:TPU:0, one launch (start us, length us, event | category | flops | bytes accessed | tf_op | source)
XLA Modules:
  0.0 48.4 jit_solution(13351088423231527386)
XLA Ops:
  0.0 0.0 copy-start.4
  0.0 0.5 %collective-permute-start.1 = (s32[1,2]{1,0:T(1,128)}, s32[1,2]{1,0:T(1,128)S(1)}, u32[]{:S(2)}, u32[]{:S(2)}) collective-permute-start(s32[1,2]{1,0:T(1,128)} %position.9), channel_id=1, source_target_pairs={{0,2},{2,4},{4,6},{6,8},{8,10},{10,12},{12,14},{14,16},{16,18},{18... | collective-permute-start | bytes 32 | tf_op jit(solution)/shard_map/ppermute | solution.py:321
  0.5 1.2 %tile.1 = f32[2,128,1024]{2,1,0:T(8,128)S(1)} custom-call(f32[2,128,1024]{2,1,0:T(8,128)} %potential.1), custom_call_target="tpu_custom_call" | custom-call | tf_op jit(solution)/shard_map/tile/pallas_call | solution.py:339
  1.7 0.0 copy-start
  1.7 0.0 copy-start.3
  1.7 5.2 %collective-permute-done.1.position = s32[1,2]{1,0:T(1,128)S(1)} collective-permute-done((s32[1,2]{1,0:T(1,128)}, s32[1,2]{1,0:T(1,128)S(1)}, u32[]{:S(2)}, u32[]{:S(2)}) %collective-permute-start.1) | collective-permute-done | bytes 40 | tf_op jit(solution)/shard_map/ppermute | solution.py:321
  6.9 0.1 shard_map.64.refs_0_
  7.0 0.1 collective-permute-start.3
  7.1 0.0 copy-done.4
  7.1 2.3 %collective-permute-start = (s32[1,2]{1,0:T(1,128)S(1)}, s32[1,2]{1,0:T(1,128)S(1)}, u32[]{:S(2)}, u32[]{:S(2)}) collective-permute-start(s32[1,2]{1,0:T(1,128)S(1)} %copy-done.4), channel_id=1, source_target_pairs={{0,30},{2,0},{4,2},{6,4},{8,6},{10,8},{12,10},{14,12},{16,14},{18,... | collective-permute-start | bytes 32 | tf_op jit(solution)/shard_map/ppermute | solution.py:321
  9.4 0.1 shard_map.65.own.refs_0_
  9.6 1.5 %collective-permute-done.position = s32[1,2]{1,0:T(1,128)S(1)} collective-permute-done((s32[1,2]{1,0:T(1,128)S(1)}, s32[1,2]{1,0:T(1,128)S(1)}, u32[]{:S(2)}, u32[]{:S(2)}) %collective-permute-start) | collective-permute-done | bytes 40 | tf_op jit(solution)/shard_map/ppermute | solution.py:321
  11.0 0.1 shard_map.67
  11.2 0.1 collective-permute-start.2
  11.2 2.0 %collective-permute-start.5 = (f32[2,128,256]{2,1,0:T(8,128)S(1)}, f32[2,128,256]{2,1,0:T(8,128)S(1)}, u32[]{:S(2)}, u32[]{:S(2)}) collective-permute-start(f32[2,128,256]{2,1,0:T(8,128)S(1)} %shard_map.65.own.refs_0_), channel_id=1, source_target_pairs={{0,1},{1,0},{2,3},{3,2},{4,5},{5,4},{6,7},{7,6},{8,9},{9,8},{10,11... | collective-permute-start | bytes 786440 | tf_op jit(solution)/shard_map/ppermute | solution.py:327
  13.2 0.0 collective-permute-start.4
  13.2 0.0 copy-done
  13.2 0.0 copy-done.3
  13.2 1.0 %shard_map.66 = (f32[2,2,128,256]{3,2,1,0:T(8,128)S(1)}, f32[2,256,256]{2,1,0:T(8,128)S(1)}) custom-call(s32[1,2]{1,0:T(1,128)S(1)} %copy-done.4, f32[2,256,256]{2,1,0:T(8,128)S(1)} %copy-done.3, bf16[6,256,256]{2,1,0:T(8,128)(2,1)S(1)} %copy-done, f32[2,128,256]{2,1,0:T(8,128)S(1)} %shard_map.65.own.refs_0_), custom_call_target="tpu_custom_call" | custom-call | tf_op jit(solution)/shard_map/pallas_call | solution.py:92
  14.2 4.3 %collective-permute-done.2.above = f32[128,256]{1,0:T(8,128)S(1)} collective-permute-done((f32[128,256]{1,0:T(8,128)S(1)}, f32[128,256]{1,0:T(8,128)S(1)}, u32[]{:S(2)}, u32[]{:S(2)}) %collective-permute-start.2) | collective-permute-done | bytes 131104 | tf_op jit(solution)/shard_map/ppermute | solution.py:321
  18.5 0.0 collective-permute-done.3.below
  18.5 0.1 shard_map.68.refs_0_
  18.6 2.0 %collective-permute-start.6 = (f32[128,256]{1,0:T(8,128)S(1)}, f32[128,256]{1,0:T(8,128)S(1)}, u32[]{:S(2)}, u32[]{:S(2)}) collective-permute-start(f32[128,256]{1,0:T(8,128)S(1)} %shard_map.68.refs_0_), channel_id=1, source_target_pairs={{0,1},{1,0},{2,3},{3,2},{4,5},{5,4},{6,7},{7,6},{8,9},{9,8},{10,11... | collective-permute-start | bytes 393224 | tf_op jit(solution)/shard_map/ppermute | solution.py:327
  20.6 0.0 collective-permute-done.4.above
  20.6 0.1 shard_map.69.refs_1_
  20.7 1.3 %collective-permute-start.7 = (f32[128,256]{1,0:T(8,128)S(1)}, f32[128,256]{1,0:T(8,128)S(1)}, u32[]{:S(2)}, u32[]{:S(2)}) collective-permute-start(f32[128,256]{1,0:T(8,128)S(1)} %shard_map.69.refs_1_), channel_id=1, source_target_pairs={{0,1},{1,0},{2,3},{3,2},{4,5},{5,4},{6,7},{7,6},{8,9},{9,8},{10,11... | collective-permute-start | bytes 393224 | tf_op jit(solution)/shard_map/ppermute | solution.py:327
  22.0 2.8 %shard_map.70 = (f32[2,256,256]{2,1,0:T(8,128)S(1)}, f32[4,2,256,256]{3,2,1,0:T(8,128)S(1)}, f32[2,2,256,256]{3,2,1,0:T(8,128)S(1)}) custom-call(s32[1]{0:T(128)} %bitcast.1.place, f32[2,256,256]{2,1,0:T(8,128)S(1)} %get-tuple-element.20._.wave_in, bf16[6,256,256]{2,1,0:T(8,128)(2,1)S(1)} %copy-done, ...), custom_call_target="tpu_custom_call", output_to_operand_aliasing={{0}: (1, {})} | custom-call | tf_op jit(solution)/shard_map/pallas_call | solution.py:92
  24.8 0.0 copy-start.1
  24.8 0.0 copy-start.2
  24.8 0.0 collective-permute-done.5.refs_0_
  24.9 0.0 collective-permute-done.6.refs_1_
  24.9 1.3 %shard_map.71 = (f32[2,256,256]{2,1,0:T(8,128)S(1)}, f32[4,2,256,256]{3,2,1,0:T(8,128)S(1)}) custom-call(s32[1]{0:T(128)} %bitcast.1.place, f32[2,256,256]{2,1,0:T(8,128)S(1)} %get-tuple-element.24.wave_in, bf16[6,256,256]{2,1,0:T(8,128)(2,1)S(1)} %copy-done, ...), custom_call_target="tpu_custom_call", output_to_operand_aliasing={{0}: (1, {}), {1}: (3, {})} | custom-call | tf_op jit(solution)/shard_map/pallas_call | solution.py:92
  26.2 0.0 collective-permute-done.7.refs_1_
  26.2 0.0 copy-done.1
  26.2 0.0 copy-done.2
  26.3 6.3 %shard_map.73 = (f32[2,128,256]{2,1,0:T(8,128)S(1)}, f32[2,128,256]{2,1,0:T(8,128)S(1)}, f32[4,2,256,256]{3,2,1,0:T(8,128)S(1)}, f32[2,2,256,256]{3,2,1,0:T(8,128)S(1)}) custom-call(s32[1]{0:T(128)} %bitcast.1.place, s32[1]{0:T(128)} %bitcast.parity, ...), custom_call_target="tpu_custom_call", output_to_operand_aliasing={{2}: (7, {}), {3}: (3, {}), {0}: (10, {})} | custom-call | tf_op jit(solution)/shard_map/pallas_call | solution.py:92
  32.6 0.1 collective-permute-start.10
  32.7 4.2 %collective-permute-start.9 = (f32[2,128,256]{2,1,0:T(8,128)S(1)}, f32[2,128,256]{2,1,0:T(8,128)S(1)}, u32[]{:S(2)}, u32[]{:S(2)}) collective-permute-start(f32[2,128,256]{2,1,0:T(8,128)S(1)} %get-tuple-element.33), channel_id=1, source_target_pairs={{0,30},{2,0},{4,2},{6,4},{8,6},{10,8},{12,10},{14,12},{16,14},{18,... | collective-permute-start | bytes 786440 | tf_op jit(solution)/shard_map/ppermute | solution.py:406
  36.9 1.3 %collective-permute-start.8 = (f32[2,128,256]{2,1,0:T(8,128)S(1)}, f32[2,128,256]{2,1,0:T(8,128)S(1)}, u32[]{:S(2)}, u32[]{:S(2)}) collective-permute-start(f32[2,128,256]{2,1,0:T(8,128)S(1)} %get-tuple-element.29.refs_3_), channel_id=1, source_target_pairs={{2,4},{6,8},{10,12},{14,16},{18,20},{22,24},{26,28},{30,0},{3,5},{... | collective-permute-start | bytes 786440 | tf_op jit(solution)/shard_map/ppermute | solution.py:404
  38.2 0.0 collective-permute-done.10.fast
  38.2 0.3 shard_map.74.staged
  38.5 2.2 %collective-permute-done.9.from_even = f32[2,128,256]{2,1,0:T(8,128)S(1)} collective-permute-done((f32[2,128,256]{2,1,0:T(8,128)S(1)}, f32[2,128,256]{2,1,0:T(8,128)S(1)}, u32[]{:S(2)}, u32[]{:S(2)}) %collective-permute-start.9) | collective-permute-done | bytes 262176 | tf_op jit(solution)/shard_map/ppermute | solution.py:406
  40.7 6.5 %collective-permute-done.8.from_odd = f32[2,128,256]{2,1,0:T(8,128)S(1)} collective-permute-done((f32[2,128,256]{2,1,0:T(8,128)S(1)}, f32[2,128,256]{2,1,0:T(8,128)S(1)}, u32[]{:S(2)}, u32[]{:S(2)}) %collective-permute-start.8) | collective-permute-done | bytes 262176 | tf_op jit(solution)/shard_map/ppermute | solution.py:404
  47.2 1.1 %place.1 = f32[2,128,1024]{2,1,0:T(8,128)} custom-call(s32[1]{0:T(128)} %bitcast.parity, s32[1,2]{1,0:T(1,128)S(1)} %get-tuple-element.36.slow_position, f32[2,128,256]{2,1,0:T(8,128)S(1)} %collective-permute-done.8.from_odd, f32[2,128,256]{2,1,0:T(8,128)S(1)} %collective-permute-done.9.from_even, f32[2,128,1024]{2,1,0:T(8,128)S(1)} %shard_map.74.staged), custom_call_target="tpu_custom_call" | custom-call | tf_op jit(solution)/shard_map/place/pallas_call | solution.py:416
  (2 shorter events, 0.0 us)
Async XLA Ops:
  0.0 7.1 %copy-start.4 = (s32[1,2]{1,0:T(1,128)S(1)}, s32[1,2]{1,0:T(1,128)}, u32[]{:S(2)}) copy-start(s32[1,2]{1,0:T(1,128)} %position.9) | copy-start | bytes 28
  0.0 6.9 %collective-permute-start.1 = (s32[1,2]{1,0:T(1,128)}, s32[1,2]{1,0:T(1,128)S(1)}, u32[]{:S(2)}, u32[]{:S(2)}) collective-permute-start(s32[1,2]{1,0:T(1,128)} %position.9), channel_id=1, source_target_pairs={{0,2},{2,4},{4,6},{6,8},{8,10},{10,12},{12,14},{14,16},{16,18},{18... | collective-permute-start | bytes 32 | tf_op jit(solution)/shard_map/ppermute | solution.py:321
  1.7 11.5 %copy-start = (bf16[6,256,256]{2,1,0:T(8,128)(2,1)S(1)}, bf16[6,256,256]{2,1,0:T(8,128)(2,1)}, u32[]{:S(2)}) copy-start(bf16[6,256,256]{2,1,0:T(8,128)(2,1)} %constant.14.clone._.prop) | copy-start | bytes 2359300
  1.7 11.5 %copy-start.3 = (f32[2,256,256]{2,1,0:T(8,128)S(1)}, f32[2,256,256]{2,1,0:T(8,128)}, u32[]{:S(2)}) copy-start(f32[2,256,256]{2,1,0:T(8,128)} %probe.1) | copy-start | bytes 1572868
  7.0 11.5 %collective-permute-start.3 = (f32[2,128,256]{2,1,0:T(8,128)S(1)}, f32[2,128,256]{2,1,0:T(8,128)S(1)}, u32[]{:S(2)}, u32[]{:S(2)}) collective-permute-start(f32[2,128,256]{2,1,0:T(8,128)S(1)} %shard_map.64.refs_0_), channel_id=1, source_target_pairs={{0,30},{2,0},{4,2},{6,4},{8,6},{10,8},{12,10},{14,12},{16,14},{18,... | collective-permute-start | bytes 786440 | tf_op jit(solution)/shard_map/ppermute | solution.py:321
  7.1 3.9 %collective-permute-start = (s32[1,2]{1,0:T(1,128)S(1)}, s32[1,2]{1,0:T(1,128)S(1)}, u32[]{:S(2)}, u32[]{:S(2)}) collective-permute-start(s32[1,2]{1,0:T(1,128)S(1)} %copy-done.4), channel_id=1, source_target_pairs={{0,30},{2,0},{4,2},{6,4},{8,6},{10,8},{12,10},{14,12},{16,14},{18,... | collective-permute-start | bytes 32 | tf_op jit(solution)/shard_map/ppermute | solution.py:321
  11.2 7.4 %collective-permute-start.2 = (f32[128,256]{1,0:T(8,128)S(1)}, f32[128,256]{1,0:T(8,128)S(1)}, u32[]{:S(2)}, u32[]{:S(2)}) collective-permute-start(f32[128,256]{1,0:T(8,128)S(1)} %get-tuple-element.22), channel_id=1, source_target_pairs={{0,2},{2,4},{4,6},{6,8},{8,10},{10,12},{12,14},{14,16},{16,18},{18... | collective-permute-start | bytes 393224 | tf_op jit(solution)/shard_map/ppermute | solution.py:321
  11.2 13.6 %collective-permute-start.5 = (f32[2,128,256]{2,1,0:T(8,128)S(1)}, f32[2,128,256]{2,1,0:T(8,128)S(1)}, u32[]{:S(2)}, u32[]{:S(2)}) collective-permute-start(f32[2,128,256]{2,1,0:T(8,128)S(1)} %shard_map.65.own.refs_0_), channel_id=1, source_target_pairs={{0,1},{1,0},{2,3},{3,2},{4,5},{5,4},{6,7},{7,6},{8,9},{9,8},{10,11... | collective-permute-start | bytes 786440 | tf_op jit(solution)/shard_map/ppermute | solution.py:327
  13.2 7.4 %collective-permute-start.4 = (f32[128,256]{1,0:T(8,128)S(1)}, f32[128,256]{1,0:T(8,128)S(1)}, u32[]{:S(2)}, u32[]{:S(2)}) collective-permute-start(f32[128,256]{1,0:T(8,128)S(1)} %get-tuple-element.23), channel_id=1, source_target_pairs={{0,2},{2,4},{4,6},{6,8},{8,10},{10,12},{12,14},{14,16},{16,18},{18... | collective-permute-start | bytes 393224 | tf_op jit(solution)/shard_map/ppermute | solution.py:321
  18.6 6.2 %collective-permute-start.6 = (f32[128,256]{1,0:T(8,128)S(1)}, f32[128,256]{1,0:T(8,128)S(1)}, u32[]{:S(2)}, u32[]{:S(2)}) collective-permute-start(f32[128,256]{1,0:T(8,128)S(1)} %shard_map.68.refs_0_), channel_id=1, source_target_pairs={{0,1},{1,0},{2,3},{3,2},{4,5},{5,4},{6,7},{7,6},{8,9},{9,8},{10,11... | collective-permute-start | bytes 393224 | tf_op jit(solution)/shard_map/ppermute | solution.py:327
  20.7 5.5 %collective-permute-start.7 = (f32[128,256]{1,0:T(8,128)S(1)}, f32[128,256]{1,0:T(8,128)S(1)}, u32[]{:S(2)}, u32[]{:S(2)}) collective-permute-start(f32[128,256]{1,0:T(8,128)S(1)} %shard_map.69.refs_1_), channel_id=1, source_target_pairs={{0,1},{1,0},{2,3},{3,2},{4,5},{5,4},{6,7},{7,6},{8,9},{9,8},{10,11... | collective-permute-start | bytes 393224 | tf_op jit(solution)/shard_map/ppermute | solution.py:327
  24.8 1.4 %copy-start.1 = (bf16[6,256,256]{2,1,0:T(8,128)(2,1)S(1)}, bf16[6,256,256]{2,1,0:T(8,128)(2,1)}, u32[]{:S(2)}) copy-start(bf16[6,256,256]{2,1,0:T(8,128)(2,1)} %constant.15.clone.dft) | copy-start | bytes 2359300
  24.8 1.4 %copy-start.2 = (f32[1,256,256]{2,1,0:T(8,128)S(1)}, f32[1,256,256]{2,1,0:T(8,128)}, u32[]{:S(2)}) copy-start(f32[1,256,256]{2,1,0:T(8,128)} %intensity.3) | copy-start | bytes 786436
  32.6 5.6 %collective-permute-start.10 = (f32[2,128,256]{2,1,0:T(8,128)S(1)}, f32[2,128,256]{2,1,0:T(8,128)S(1)}, u32[]{:S(2)}, u32[]{:S(2)}) collective-permute-start(f32[2,128,256]{2,1,0:T(8,128)S(1)} %get-tuple-element.33), channel_id=1, source_target_pairs={{0,2},{2,0},{4,6},{6,4},{8,10},{10,8},{12,14},{14,12},{16,18},{18,... | collective-permute-start | bytes 786440 | tf_op jit(solution)/shard_map/ppermute | solution.py:407
  32.7 8.1 %collective-permute-start.9 = (f32[2,128,256]{2,1,0:T(8,128)S(1)}, f32[2,128,256]{2,1,0:T(8,128)S(1)}, u32[]{:S(2)}, u32[]{:S(2)}) collective-permute-start(f32[2,128,256]{2,1,0:T(8,128)S(1)} %get-tuple-element.33), channel_id=1, source_target_pairs={{0,30},{2,0},{4,2},{6,4},{8,6},{10,8},{12,10},{14,12},{16,14},{18,... | collective-permute-start | bytes 786440 | tf_op jit(solution)/shard_map/ppermute | solution.py:406
  36.9 10.4 %collective-permute-start.8 = (f32[2,128,256]{2,1,0:T(8,128)S(1)}, f32[2,128,256]{2,1,0:T(8,128)S(1)}, u32[]{:S(2)}, u32[]{:S(2)}) collective-permute-start(f32[2,128,256]{2,1,0:T(8,128)S(1)} %get-tuple-element.29.refs_3_), channel_id=1, source_target_pairs={{2,4},{6,8},{10,12},{14,16},{18,20},{22,24},{26,28},{30,0},{3,5},{... | collective-permute-start | bytes 786440 | tf_op jit(solution)/shard_map/ppermute | solution.py:404

commit v8 on v7

--- a/solution.py
+++ b/solution.py
@@ -289,11 +289,14 @@
     layers, strip, columns = out.shape
     extent = 2 * strip
     odd = jnp.broadcast_to(parity[0], (strip, extent)) == 1
+    row = lax.broadcasted_iota(jnp.int32, (strip, extent), 0)
+    rows = (row >= entry(slow_position, 0) % strip).astype(jnp.int32) != 1 - parity[0]
     slow = [jnp.where(odd, from_even[layer], from_odd[layer]) for layer in range(layers)]
+    slow = [jnp.where(rows, value, 0.0) for value in slow]
     copies = []
     for block in range(columns // extent):
         at = slice(block * extent, (block + 1) * extent)
-        far = covers(slow_position, block, (strip, extent), 1 - parity[0])
+        far = covered(entry(slow_position, 1), block, (strip, extent))
         for layer in range(layers):
             value = staged[layer, :, at] + jnp.where(far, slow[layer], 0.0)
             final[layer, :, at] = value

time: 48.5 us -> 48.5 us (level)
  no operation moved by 1% of the time
where the time goes in v8:
time: 48.5 us; the launch traced here: 48.4 us
  waiting for transfers between devices  19.7 us (41%)
  Pallas kernels  14.7 us (30%)
  starting transfers between devices  13.7 us (28%)
    pallas_call x11, Pallas kernels, call(): pl.pallas_call(kernel, out_shape=[pltpu.VMEM(shape, f32) for shape in res...  12.3 us
    ppermute x5, waiting for transfers between devices, step(): lax.ppermute(x, 'probe', [(i, (i + by) % count) for i in range(count)])  11 us
    ppermute x1, waiting for transfers between devices, local(): from_odd = lax.ppermute(outer, 'probe', odd_groups)  6.48 us
    ppermute x3, starting transfers between devices, to_depths(): out.append(lax.ppermute(x, 'depth', pairs))  5.27 us
    ppermute x1, starting transfers between devices, local(): from_even = lax.ppermute(outer, 'probe', even_groups)  4.18 us
    ppermute x5, starting transfers between devices, step(): lax.ppermute(x, 'probe', [(i, (i + by) % count) for i in range(count)])  2.94 us
    ppermute x1, waiting for transfers between devices, local(): from_even = lax.ppermute(outer, 'probe', even_groups)  2.24 us
    ppermute x1, starting transfers between devices, local(): from_odd = lax.ppermute(outer, 'probe', odd_groups)  1.28 us
  transfers between devices with their start and end apart: 11, of which 5 were waited for; matrix products, arithmetic and copies ran while one was open for 0% of the time, Pallas kernels for 15%

profile of v8, /device:TPU:0, one launch (start us, length us, event | category | flops | bytes accessed | tf_op | source)
XLA Modules:
  0.0 48.4 jit_solution(1578343280798214985)
XLA Ops:
  0.0 0.0 copy-start.4
  0.0 0.5 %collective-permute-start.1 = (s32[1,2]{1,0:T(1,128)}, s32[1,2]{1,0:T(1,128)S(1)}, u32[]{:S(2)}, u32[]{:S(2)}) collective-permute-start(s32[1,2]{1,0:T(1,128)} %position.9), channel_id=1, source_target_pairs={{0,2},{2,4},{4,6},{6,8},{8,10},{10,12},{12,14},{14,16},{16,18},{18... | collective-permute-start | bytes 32 | tf_op jit(solution)/shard_map/ppermute | solution.py:324
  0.5 1.2 %tile.1 = f32[2,128,1024]{2,1,0:T(8,128)S(1)} custom-call(f32[2,128,1024]{2,1,0:T(8,128)} %potential.1), custom_call_target="tpu_custom_call" | custom-call | tf_op jit(solution)/shard_map/tile/pallas_call | solution.py:342
  1.7 0.0 copy-start
  1.7 0.0 copy-start.3
  1.7 5.2 %collective-permute-done.1.position = s32[1,2]{1,0:T(1,128)S(1)} collective-permute-done((s32[1,2]{1,0:T(1,128)}, s32[1,2]{1,0:T(1,128)S(1)}, u32[]{:S(2)}, u32[]{:S(2)}) %collective-permute-start.1) | collective-permute-done | bytes 40 | tf_op jit(solution)/shard_map/ppermute | solution.py:324
  6.9 0.1 shard_map.64.refs_0_
  7.0 0.1 collective-permute-start.3
  7.1 0.0 copy-done.4
  7.1 2.3 %collective-permute-start = (s32[1,2]{1,0:T(1,128)S(1)}, s32[1,2]{1,0:T(1,128)S(1)}, u32[]{:S(2)}, u32[]{:S(2)}) collective-permute-start(s32[1,2]{1,0:T(1,128)S(1)} %copy-done.4), channel_id=1, source_target_pairs={{0,30},{2,0},{4,2},{6,4},{8,6},{10,8},{12,10},{14,12},{16,14},{18,... | collective-permute-start | bytes 32 | tf_op jit(solution)/shard_map/ppermute | solution.py:324
  9.4 0.1 shard_map.65.own.refs_0_
  9.6 1.5 %collective-permute-done.position = s32[1,2]{1,0:T(1,128)S(1)} collective-permute-done((s32[1,2]{1,0:T(1,128)S(1)}, s32[1,2]{1,0:T(1,128)S(1)}, u32[]{:S(2)}, u32[]{:S(2)}) %collective-permute-start) | collective-permute-done | bytes 40 | tf_op jit(solution)/shard_map/ppermute | solution.py:324
  11.0 0.1 shard_map.67
  11.2 0.1 collective-permute-start.2
  11.2 2.0 %collective-permute-start.5 = (f32[2,128,256]{2,1,0:T(8,128)S(1)}, f32[2,128,256]{2,1,0:T(8,128)S(1)}, u32[]{:S(2)}, u32[]{:S(2)}) collective-permute-start(f32[2,128,256]{2,1,0:T(8,128)S(1)} %shard_map.65.own.refs_0_), channel_id=1, source_target_pairs={{0,1},{1,0},{2,3},{3,2},{4,5},{5,4},{6,7},{7,6},{8,9},{9,8},{10,11... | collective-permute-start | bytes 786440 | tf_op jit(solution)/shard_map/ppermute | solution.py:330
  13.2 0.0 collective-permute-start.4
  13.2 0.0 copy-done
  13.2 0.0 copy-done.3
  13.2 1.0 %shard_map.66 = (f32[2,2,128,256]{3,2,1,0:T(8,128)S(1)}, f32[2,256,256]{2,1,0:T(8,128)S(1)}) custom-call(s32[1,2]{1,0:T(1,128)S(1)} %copy-done.4, f32[2,256,256]{2,1,0:T(8,128)S(1)} %copy-done.3, bf16[6,256,256]{2,1,0:T(8,128)(2,1)S(1)} %copy-done, f32[2,128,256]{2,1,0:T(8,128)S(1)} %shard_map.65.own.refs_0_), custom_call_target="tpu_custom_call" | custom-call | tf_op jit(solution)/shard_map/pallas_call | solution.py:92
  14.2 4.3 %collective-permute-done.2.above = f32[128,256]{1,0:T(8,128)S(1)} collective-permute-done((f32[128,256]{1,0:T(8,128)S(1)}, f32[128,256]{1,0:T(8,128)S(1)}, u32[]{:S(2)}, u32[]{:S(2)}) %collective-permute-start.2) | collective-permute-done | bytes 131104 | tf_op jit(solution)/shard_map/ppermute | solution.py:324
  18.5 0.0 collective-permute-done.3.below
  18.5 0.1 shard_map.68.refs_0_
  18.6 2.0 %collective-permute-start.6 = (f32[128,256]{1,0:T(8,128)S(1)}, f32[128,256]{1,0:T(8,128)S(1)}, u32[]{:S(2)}, u32[]{:S(2)}) collective-permute-start(f32[128,256]{1,0:T(8,128)S(1)} %shard_map.68.refs_0_), channel_id=1, source_target_pairs={{0,1},{1,0},{2,3},{3,2},{4,5},{5,4},{6,7},{7,6},{8,9},{9,8},{10,11... | collective-permute-start | bytes 393224 | tf_op jit(solution)/shard_map/ppermute | solution.py:330
  20.6 0.0 collective-permute-done.4.above
  20.6 0.1 shard_map.69.refs_1_
  20.7 1.3 %collective-permute-start.7 = (f32[128,256]{1,0:T(8,128)S(1)}, f32[128,256]{1,0:T(8,128)S(1)}, u32[]{:S(2)}, u32[]{:S(2)}) collective-permute-start(f32[128,256]{1,0:T(8,128)S(1)} %shard_map.69.refs_1_), channel_id=1, source_target_pairs={{0,1},{1,0},{2,3},{3,2},{4,5},{5,4},{6,7},{7,6},{8,9},{9,8},{10,11... | collective-permute-start | bytes 393224 | tf_op jit(solution)/shard_map/ppermute | solution.py:330
  22.0 2.8 %shard_map.70 = (f32[2,256,256]{2,1,0:T(8,128)S(1)}, f32[4,2,256,256]{3,2,1,0:T(8,128)S(1)}, f32[2,2,256,256]{3,2,1,0:T(8,128)S(1)}) custom-call(s32[1]{0:T(128)} %bitcast.1.place, f32[2,256,256]{2,1,0:T(8,128)S(1)} %get-tuple-element.20._.wave_in, bf16[6,256,256]{2,1,0:T(8,128)(2,1)S(1)} %copy-done, ...), custom_call_target="tpu_custom_call", output_to_operand_aliasing={{0}: (1, {})} | custom-call | tf_op jit(solution)/shard_map/pallas_call | solution.py:92
  24.8 0.0 copy-start.1
  24.8 0.0 copy-start.2
  24.8 0.0 collective-permute-done.5.refs_0_
  24.9 0.0 collective-permute-done.6.refs_1_
  24.9 1.3 %shard_map.71 = (f32[2,256,256]{2,1,0:T(8,128)S(1)}, f32[4,2,256,256]{3,2,1,0:T(8,128)S(1)}) custom-call(s32[1]{0:T(128)} %bitcast.1.place, f32[2,256,256]{2,1,0:T(8,128)S(1)} %get-tuple-element.24.wave_in, bf16[6,256,256]{2,1,0:T(8,128)(2,1)S(1)} %copy-done, ...), custom_call_target="tpu_custom_call", output_to_operand_aliasing={{0}: (1, {}), {1}: (3, {})} | custom-call | tf_op jit(solution)/shard_map/pallas_call | solution.py:92
  26.2 0.0 collective-permute-done.7.refs_1_
  26.2 0.0 copy-done.1
  26.2 0.0 copy-done.2
  26.3 6.3 %shard_map.73 = (f32[2,128,256]{2,1,0:T(8,128)S(1)}, f32[2,128,256]{2,1,0:T(8,128)S(1)}, f32[4,2,256,256]{3,2,1,0:T(8,128)S(1)}, f32[2,2,256,256]{3,2,1,0:T(8,128)S(1)}) custom-call(s32[1]{0:T(128)} %bitcast.1.place, s32[1]{0:T(128)} %bitcast.parity, ...), custom_call_target="tpu_custom_call", output_to_operand_aliasing={{2}: (7, {}), {3}: (3, {}), {0}: (10, {})} | custom-call | tf_op jit(solution)/shard_map/pallas_call | solution.py:92
  32.6 0.1 collective-permute-start.10
  32.7 4.2 %collective-permute-start.9 = (f32[2,128,256]{2,1,0:T(8,128)S(1)}, f32[2,128,256]{2,1,0:T(8,128)S(1)}, u32[]{:S(2)}, u32[]{:S(2)}) collective-permute-start(f32[2,128,256]{2,1,0:T(8,128)S(1)} %get-tuple-element.33), channel_id=1, source_target_pairs={{0,30},{2,0},{4,2},{6,4},{8,6},{10,8},{12,10},{14,12},{16,14},{18,... | collective-permute-start | bytes 786440 | tf_op jit(solution)/shard_map/ppermute | solution.py:409
  36.9 1.3 %collective-permute-start.8 = (f32[2,128,256]{2,1,0:T(8,128)S(1)}, f32[2,128,256]{2,1,0:T(8,128)S(1)}, u32[]{:S(2)}, u32[]{:S(2)}) collective-permute-start(f32[2,128,256]{2,1,0:T(8,128)S(1)} %get-tuple-element.29.refs_3_), channel_id=1, source_target_pairs={{2,4},{6,8},{10,12},{14,16},{18,20},{22,24},{26,28},{30,0},{3,5},{... | collective-permute-start | bytes 786440 | tf_op jit(solution)/shard_map/ppermute | solution.py:407
  38.2 0.0 collective-permute-done.10.fast
  38.2 0.3 shard_map.74.staged
  38.5 2.2 %collective-permute-done.9.from_even = f32[2,128,256]{2,1,0:T(8,128)S(1)} collective-permute-done((f32[2,128,256]{2,1,0:T(8,128)S(1)}, f32[2,128,256]{2,1,0:T(8,128)S(1)}, u32[]{:S(2)}, u32[]{:S(2)}) %collective-permute-start.9) | collective-permute-done | bytes 262176 | tf_op jit(solution)/shard_map/ppermute | solution.py:409
  40.7 6.5 %collective-permute-done.8.from_odd = f32[2,128,256]{2,1,0:T(8,128)S(1)} collective-permute-done((f32[2,128,256]{2,1,0:T(8,128)S(1)}, f32[2,128,256]{2,1,0:T(8,128)S(1)}, u32[]{:S(2)}, u32[]{:S(2)}) %collective-permute-start.8) | collective-permute-done | bytes 262176 | tf_op jit(solution)/shard_map/ppermute | solution.py:407
  47.2 1.1 %place.1 = f32[2,128,1024]{2,1,0:T(8,128)} custom-call(s32[1]{0:T(128)} %bitcast.parity, s32[1,2]{1,0:T(1,128)S(1)} %get-tuple-element.36.slow_position, f32[2,128,256]{2,1,0:T(8,128)S(1)} %collective-permute-done.8.from_odd, f32[2,128,256]{2,1,0:T(8,128)S(1)} %collective-permute-done.9.from_even, f32[2,128,1024]{2,1,0:T(8,128)S(1)} %shard_map.74.staged), custom_call_target="tpu_custom_call" | custom-call | tf_op jit(solution)/shard_map/place/pallas_call | solution.py:419
  (2 shorter events, 0.0 us)
Async XLA Ops:
  0.0 7.1 %copy-start.4 = (s32[1,2]{1,0:T(1,128)S(1)}, s32[1,2]{1,0:T(1,128)}, u32[]{:S(2)}) copy-start(s32[1,2]{1,0:T(1,128)} %position.9) | copy-start | bytes 28
  0.0 6.9 %collective-permute-start.1 = (s32[1,2]{1,0:T(1,128)}, s32[1,2]{1,0:T(1,128)S(1)}, u32[]{:S(2)}, u32[]{:S(2)}) collective-permute-start(s32[1,2]{1,0:T(1,128)} %position.9), channel_id=1, source_target_pairs={{0,2},{2,4},{4,6},{6,8},{8,10},{10,12},{12,14},{14,16},{16,18},{18... | collective-permute-start | bytes 32 | tf_op jit(solution)/shard_map/ppermute | solution.py:324
  1.7 11.5 %copy-start = (bf16[6,256,256]{2,1,0:T(8,128)(2,1)S(1)}, bf16[6,256,256]{2,1,0:T(8,128)(2,1)}, u32[]{:S(2)}) copy-start(bf16[6,256,256]{2,1,0:T(8,128)(2,1)} %constant.14.clone._.prop) | copy-start | bytes 2359300
  1.7 11.5 %copy-start.3 = (f32[2,256,256]{2,1,0:T(8,128)S(1)}, f32[2,256,256]{2,1,0:T(8,128)}, u32[]{:S(2)}) copy-start(f32[2,256,256]{2,1,0:T(8,128)} %probe.1) | copy-start | bytes 1572868
  7.0 11.5 %collective-permute-start.3 = (f32[2,128,256]{2,1,0:T(8,128)S(1)}, f32[2,128,256]{2,1,0:T(8,128)S(1)}, u32[]{:S(2)}, u32[]{:S(2)}) collective-permute-start(f32[2,128,256]{2,1,0:T(8,128)S(1)} %shard_map.64.refs_0_), channel_id=1, source_target_pairs={{0,30},{2,0},{4,2},{6,4},{8,6},{10,8},{12,10},{14,12},{16,14},{18,... | collective-permute-start | bytes 786440 | tf_op jit(solution)/shard_map/ppermute | solution.py:324
  7.1 3.9 %collective-permute-start = (s32[1,2]{1,0:T(1,128)S(1)}, s32[1,2]{1,0:T(1,128)S(1)}, u32[]{:S(2)}, u32[]{:S(2)}) collective-permute-start(s32[1,2]{1,0:T(1,128)S(1)} %copy-done.4), channel_id=1, source_target_pairs={{0,30},{2,0},{4,2},{6,4},{8,6},{10,8},{12,10},{14,12},{16,14},{18,... | collective-permute-start | bytes 32 | tf_op jit(solution)/shard_map/ppermute | solution.py:324
  11.2 7.4 %collective-permute-start.2 = (f32[128,256]{1,0:T(8,128)S(1)}, f32[128,256]{1,0:T(8,128)S(1)}, u32[]{:S(2)}, u32[]{:S(2)}) collective-permute-start(f32[128,256]{1,0:T(8,128)S(1)} %get-tuple-element.22), channel_id=1, source_target_pairs={{0,2},{2,4},{4,6},{6,8},{8,10},{10,12},{12,14},{14,16},{16,18},{18... | collective-permute-start | bytes 393224 | tf_op jit(solution)/shard_map/ppermute | solution.py:324
  11.2 13.6 %collective-permute-start.5 = (f32[2,128,256]{2,1,0:T(8,128)S(1)}, f32[2,128,256]{2,1,0:T(8,128)S(1)}, u32[]{:S(2)}, u32[]{:S(2)}) collective-permute-start(f32[2,128,256]{2,1,0:T(8,128)S(1)} %shard_map.65.own.refs_0_), channel_id=1, source_target_pairs={{0,1},{1,0},{2,3},{3,2},{4,5},{5,4},{6,7},{7,6},{8,9},{9,8},{10,11... | collective-permute-start | bytes 786440 | tf_op jit(solution)/shard_map/ppermute | solution.py:330
  13.2 7.4 %collective-permute-start.4 = (f32[128,256]{1,0:T(8,128)S(1)}, f32[128,256]{1,0:T(8,128)S(1)}, u32[]{:S(2)}, u32[]{:S(2)}) collective-permute-start(f32[128,256]{1,0:T(8,128)S(1)} %get-tuple-element.23), channel_id=1, source_target_pairs={{0,2},{2,4},{4,6},{6,8},{8,10},{10,12},{12,14},{14,16},{16,18},{18... | collective-permute-start | bytes 393224 | tf_op jit(solution)/shard_map/ppermute | solution.py:324
  18.6 6.2 %collective-permute-start.6 = (f32[128,256]{1,0:T(8,128)S(1)}, f32[128,256]{1,0:T(8,128)S(1)}, u32[]{:S(2)}, u32[]{:S(2)}) collective-permute-start(f32[128,256]{1,0:T(8,128)S(1)} %shard_map.68.refs_0_), channel_id=1, source_target_pairs={{0,1},{1,0},{2,3},{3,2},{4,5},{5,4},{6,7},{7,6},{8,9},{9,8},{10,11... | collective-permute-start | bytes 393224 | tf_op jit(solution)/shard_map/ppermute | solution.py:330
  20.7 5.5 %collective-permute-start.7 = (f32[128,256]{1,0:T(8,128)S(1)}, f32[128,256]{1,0:T(8,128)S(1)}, u32[]{:S(2)}, u32[]{:S(2)}) collective-permute-start(f32[128,256]{1,0:T(8,128)S(1)} %shard_map.69.refs_1_), channel_id=1, source_target_pairs={{0,1},{1,0},{2,3},{3,2},{4,5},{5,4},{6,7},{7,6},{8,9},{9,8},{10,11... | collective-permute-start | bytes 393224 | tf_op jit(solution)/shard_map/ppermute | solution.py:330
  24.8 1.4 %copy-start.1 = (bf16[6,256,256]{2,1,0:T(8,128)(2,1)S(1)}, bf16[6,256,256]{2,1,0:T(8,128)(2,1)}, u32[]{:S(2)}) copy-start(bf16[6,256,256]{2,1,0:T(8,128)(2,1)} %constant.15.clone.dft) | copy-start | bytes 2359300
  24.8 1.4 %copy-start.2 = (f32[1,256,256]{2,1,0:T(8,128)S(1)}, f32[1,256,256]{2,1,0:T(8,128)}, u32[]{:S(2)}) copy-start(f32[1,256,256]{2,1,0:T(8,128)} %intensity.3) | copy-start | bytes 786436
  32.6 5.6 %collective-permute-start.10 = (f32[2,128,256]{2,1,0:T(8,128)S(1)}, f32[2,128,256]{2,1,0:T(8,128)S(1)}, u32[]{:S(2)}, u32[]{:S(2)}) collective-permute-start(f32[2,128,256]{2,1,0:T(8,128)S(1)} %get-tuple-element.33), channel_id=1, source_target_pairs={{0,2},{2,0},{4,6},{6,4},{8,10},{10,8},{12,14},{14,12},{16,18},{18,... | collective-permute-start | bytes 786440 | tf_op jit(solution)/shard_map/ppermute | solution.py:410
  32.7 8.1 %collective-permute-start.9 = (f32[2,128,256]{2,1,0:T(8,128)S(1)}, f32[2,128,256]{2,1,0:T(8,128)S(1)}, u32[]{:S(2)}, u32[]{:S(2)}) collective-permute-start(f32[2,128,256]{2,1,0:T(8,128)S(1)} %get-tuple-element.33), channel_id=1, source_target_pairs={{0,30},{2,0},{4,2},{6,4},{8,6},{10,8},{12,10},{14,12},{16,14},{18,... | collective-permute-start | bytes 786440 | tf_op jit(solution)/shard_map/ppermute | solution.py:409
  36.9 10.4 %collective-permute-start.8 = (f32[2,128,256]{2,1,0:T(8,128)S(1)}, f32[2,128,256]{2,1,0:T(8,128)S(1)}, u32[]{:S(2)}, u32[]{:S(2)}) collective-permute-start(f32[2,128,256]{2,1,0:T(8,128)S(1)} %get-tuple-element.29.refs_3_), channel_id=1, source_target_pairs={{2,4},{6,8},{10,12},{14,16},{18,20},{22,24},{26,28},{30,0},{3,5},{... | collective-permute-start | bytes 786440 | tf_op jit(solution)/shard_map/ppermute | solution.py:407
